TPU v7x, 256 devices: a whole 4x4x8 slice. The times are simulated.
256 devices in a mesh: pairs: 128 (over y, x, z), aux: 2 (over core).
Axes of the slice: x: 4, y: 4, z: 8, core: 2. Of those that a mesh axis runs over, the one named last changes fastest.
Arguments:
- blocks: bfloat16 [256, 2048, 256], P('pairs', 'aux'), may hold values from -0.9 to 0.9
- pair_orbs: int32 [2048, 2], P('pairs'), may hold values from 0 to 255, as said below
- pno_count: int32 [2048], P('pairs'), may hold values from 128 to 256
- amplitudes: bfloat16 [2048, 256, 256], P('pairs'), may hold values from -6 to 6
- margins: bfloat16 [2048, 4, 256, 256], P('pairs'), may hold values from -0.375 to 0.375
- couple_target: int32 [2048, 4], replicated, may hold values from 0 to 2047, as said below
- couple_weight: float32 [2048, 4], replicated, may hold values from -1 to 1
- pno_energy: float32 [2048, 256], P('pairs'), may hold values from 0.3 to 4
- occ_energy: float32 [256], replicated, may hold values from -2 to -0.3
Outputs:
- residual: float32 [2048, 256, 256], P('pairs', 'aux')
Inputs may be any that keep to these rules, and one draw needn't show every extreme that they name: `pair_orbs`: the first orbital of pair p belongs to pairs index p // 16 (orbitals o with o // 2 equal to it); the second belongs to that index or an adjacent one. `couple_target`: every target of source pair q is held by pairs index q // 16 or an adjacent one (target t is held by index t // 16).
All inputs are finite; a program needn't handle non-finite values.
Results may differ from a plain program's by a relative error of at most 0.00076.
Values may be sent and summed in bfloat16 or wider, within the bound.
No kernel may reach another device: no remote copies, remote signals or barrier semaphores. Data moves between devices by JAX's collectives and lax.ppermute only.
A program may use at most 128 MiB of HBM per device.

v0:
```python
import jax
import jax.numpy as jnp
from jax import lax
from jax.sharding import PartitionSpec as P


def with_halo(cells, sides, width):
    for axis, dim in sides:
        count = lax.axis_size(axis)
        ends = count - 1
        head = lax.slice_in_dim(cells, 0, width, axis=dim)
        tail = lax.slice_in_dim(cells, cells.shape[dim] - width, cells.shape[dim], axis=dim)
        cells = jnp.concatenate(
            [
                lax.ppermute(tail, axis, [(i, (i + 1) % count) for i in range(ends)]),
                cells,
                lax.ppermute(head, axis, [((i + 1) % count, i) for i in range(ends)]),
            ],
            axis=dim,
        )
    return cells


def split_up(x, dim, devices):
    before, after = (x.shape[:dim], x.shape[dim + 1 :])
    return jnp.moveaxis(x.reshape(*before, devices, -1, *after), dim, 0)


def sum_at_owner(x, axis, dim):
    tiles = split_up(x, dim, lax.axis_size(axis))
    arrived = lax.all_to_all(tiles, axis, split_axis=0, concat_axis=0, tiled=True)
    return arrived.sum(axis=0)


def passed_along(value, axis, steps):
    count = lax.axis_size(axis)
    leading, last = (max(0, -steps), min(count, count - steps))
    return lax.ppermute(value, axis, [(source, source + steps) for source in range(leading, last)])


def coupling_terms(source_margins, source_amplitudes, weights, row_start, row_count):
    margin_rows = lax.dynamic_slice_in_dim(source_margins, row_start, row_count, 2)
    first_product = jnp.einsum(
        "pcak,pkl->pcal", margin_rows, source_amplitudes, preferred_element_type=jnp.float32
    ).astype(jnp.bfloat16)
    second = jnp.einsum(
        "pcal,pcbl->pcab", first_product, source_margins, preferred_element_type=jnp.float32
    )
    return second * weights[:, :, None, None]


def route_terms(pair_terms, local_slots, slot_total):
    flat_terms = pair_terms.reshape((-1,) + pair_terms.shape[2:])
    flat_slots = local_slots.reshape(-1)
    inside = (flat_slots >= 0) & (flat_slots < slot_total)
    flat_slots = jnp.where(inside, flat_slots, slot_total)
    empty = jnp.zeros((slot_total,) + pair_terms.shape[2:], jnp.float32)
    return empty.at[flat_slots].add(flat_terms, mode="drop")


def local(
    blocks,
    pair_orbs,
    pno_count,
    amplitudes,
    margins,
    couple_target,
    couple_weight,
    pno_energy,
    occ_energy,
):
    holder = lax.axis_index("pairs")
    core_index = lax.axis_index("aux")
    pair_count = amplitudes.shape[0]
    orb_count = blocks.shape[0]
    pno_width = amplitudes.shape[2]
    row_count = pno_width // lax.axis_size("aux")
    row_start = core_index * row_count
    padded = with_halo(blocks, (("pairs", 0),), orb_count)
    base_orb = (holder - 1) * orb_count
    left_block = padded[pair_orbs[:, 0] - base_orb]
    right_block = padded[pair_orbs[:, 1] - base_orb]
    partial_value = jnp.einsum(
        "pqa,pqb->pab", left_block, right_block, preferred_element_type=jnp.float32
    )
    exchange_rows = sum_at_owner(partial_value, "aux", 1)
    orbitals = jnp.arange(occ_energy.shape[0], dtype=jnp.int32)
    occ_first = jnp.sum(
        jnp.where(pair_orbs[:, 0:1] == orbitals[None, :], occ_energy[None, :], 0.0), axis=1
    )
    occ_second = jnp.sum(
        jnp.where(pair_orbs[:, 1:2] == orbitals[None, :], occ_energy[None, :], 0.0), axis=1
    )
    energy_rows = lax.dynamic_slice_in_dim(pno_energy, row_start, row_count, 1)
    amp_rows = lax.dynamic_slice_in_dim(amplitudes, row_start, row_count, 1).astype(jnp.float32)
    denominator = (
        energy_rows[:, :, None] + pno_energy[:, None, :] - (occ_first + occ_second)[:, None, None]
    )
    base_terms = exchange_rows + denominator * amp_rows
    own_targets = lax.dynamic_slice_in_dim(couple_target, holder * pair_count, pair_count, 0)
    own_weights = lax.dynamic_slice_in_dim(couple_weight, holder * pair_count, pair_count, 0)
    pair_terms = coupling_terms(margins, amplitudes, own_weights, row_start, row_count)
    local_slots = own_targets - (holder - 1) * pair_count
    grouped = route_terms(pair_terms, local_slots, 3 * pair_count)
    grouped = grouped.reshape((3, pair_count) + grouped.shape[1:])
    from_lower = passed_along(grouped[2], "pairs", 1)
    from_upper = passed_along(grouped[0], "pairs", -1)
    coupling = grouped[1] + from_lower + from_upper
    positions = jnp.arange(pno_width, dtype=jnp.int32)
    col_mask = (positions[None, :] < pno_count[:, None]).astype(jnp.float32)
    row_positions = row_start + jnp.arange(row_count, dtype=jnp.int32)
    row_mask = (row_positions[None, :] < pno_count[:, None]).astype(jnp.float32)
    return (base_terms + coupling) * row_mask[:, :, None] * col_mask[:, None, :]


def solution(mesh):
    placed = (
        P("pairs", "aux", None),
        P("pairs", None),
        P("pairs"),
        P("pairs", None, None),
        P("pairs", None, None, None),
        P(),
        P(),
        P("pairs", None),
        P(),
    )
    return jax.shard_map(
        local, mesh=mesh, in_specs=placed, out_specs=P("pairs", "aux", None), check_vma=False
    )
```

profile of v0, /device:TPU:24, one launch (start us, length us, event | category | flops | bytes accessed | tf_op | source)
XLA Modules:
  0.0 112.5 jit_solution(1611152510495611228)
XLA Ops:
  0.0 0.0 copy-start
  0.0 3.9 %collective-permute-start = (bf16[2,1024,256]{2,1,0:T(8,128)(2,1)}, bf16[2,1024,256]{2,1,0:T(8,128)(2,1)}, u32[]{:S(2)}, u32[]{:S(2)}) collective-permute-start(bf16[2,1024,256]{2,1,0:T(8,128)(2,1)} %param.9), channel_id=1, source_target_pairs={{0,2},{2,4},{4,6},{6,8},{8,10},{10,12},{12,14},{14,16},{16,18},{18... | collective-permute-start | bytes 3145736 | tf_op jit(solution)/shard_map/ppermute | solution.py:15
  4.0 8.2 %collective-permute-start.1 = (bf16[2,1024,256]{2,1,0:T(8,128)(2,1)}, bf16[2,1024,256]{2,1,0:T(8,128)(2,1)}, u32[]{:S(2)}, u32[]{:S(2)}) collective-permute-start(bf16[2,1024,256]{2,1,0:T(8,128)(2,1)} %param.9), channel_id=1, source_target_pairs={{2,0},{4,2},{6,4},{8,6},{10,8},{12,10},{14,12},{16,14},{18,16},{20... | collective-permute-start | bytes 3145736 | tf_op jit(solution)/shard_map/ppermute | solution.py:17
  12.2 0.0 copy-done
  12.2 0.1 constant_dynamic-slice_fusion
  12.3 0.1 copy.23
  12.4 0.8 dynamic-slice_subtract_fusion
  13.1 0.1 copy.22
  13.2 0.1 reshape.115
  13.3 12.4 %broadcast_multiply_fusion = f32[16,4,128,256]{3,2,1,0:T(8,128)} fusion(f32[16,4]{1,0:T(8,128)S(1)} %copy.23, bf16[16,4,256,256]{3,2,1,0:T(8,128)(2,1)} %param.13, s32[]{:T(128)S(6)} %select_n.47, bf16[16,256,256]{2,1,0:T(8,128)(2,1)} %param.12), kind=kOutput, calls=%fused_computation.4 | convolution fusion | flops 2151677952 | bytes 23068932 | tf_op jit(solution)/shard_map/pcal,pcbl->pcab/dot_general | solution.py:46
  25.8 3.4 %broadcast_in_dim.22 = f32[48,128,256]{2,1,0:T(8,128)} broadcast(f32[]{:T(128)} %constant.5.clone.1), dimensions={} | broadcast | bytes 6291460 | tf_op jit(solution)/shard_map/broadcast_in_dim | solution.py:57
  29.2 19.3 %scatter_fusion = f32[48,128,256]{2,1,0:T(8,128)} fusion(f32[48,128,256]{2,1,0:T(8,128)} %broadcast_in_dim.22, s32[64]{0:T(128)S(1)} %fusion.21, f32[64,128,256]{2,1,0:T(8,128)} %bitcast.24), kind=kCustom, calls=%fused_computation.2 | custom fusion | flops 2097152 | bytes 25166080 | tf_op jit(solution)/shard_map/scatter-add | solution.py:58
  48.5 0.0 copy-start.4
  48.5 0.0 copy-start.5
  48.5 0.0 copy-start.2
  48.5 0.0 copy-start.3
  48.5 4.7 %fusion.22 = (f32[16,128,256]{2,1,0:T(8,128)}, f32[16,128,256]{2,1,0:T(8,128)}) fusion(f32[48,128,256]{2,1,0:T(8,128)} %scatter_fusion), kind=kLoop, calls=%fused_computation.41 | loop fusion | bytes 8388608 | tf_op jit(solution)/shard_map/slice | solution.py:106
  53.2 1.9 %collective-permute-start.2 = (f32[16,128,256]{2,1,0:T(8,128)}, f32[16,128,256]{2,1,0:T(8,128)}, u32[]{:S(2)}, u32[]{:S(2)}) collective-permute-start(f32[16,128,256]{2,1,0:T(8,128)} %get-tuple-element.7), channel_id=1, source_target_pairs={{0,2},{2,4},{4,6},{6,8},{8,10},{10,12},{12,14},{14,16},{16,18},{18... | collective-permute-start | bytes 6291464 | tf_op jit(solution)/shard_map/ppermute | solution.py:38
  55.2 8.1 %collective-permute-start.3 = (f32[16,128,256]{2,1,0:T(8,128)}, f32[16,128,256]{2,1,0:T(8,128)}, u32[]{:S(2)}, u32[]{:S(2)}) collective-permute-start(f32[16,128,256]{2,1,0:T(8,128)} %get-tuple-element.8), channel_id=1, source_target_pairs={{2,0},{4,2},{6,4},{8,6},{10,8},{12,10},{14,12},{16,14},{18,16},{20... | collective-permute-start | bytes 6291464 | tf_op jit(solution)/shard_map/ppermute | solution.py:38
  63.3 0.0 copy-done.4
  63.3 0.0 copy-done.5
  63.4 0.2 select_reduce_fusion
  63.5 0.0 copy-done.2
  63.6 0.0 copy-done.3
  63.6 0.1 compare_convert_fusion
  63.7 0.1 fusion.16
  63.8 0.0 collective-permute-done
  63.8 1.3 %constant_dynamic-update-slice_fusion.2 = bf16[6,1024,256]{2,1,0:T(8,128)(2,1)S(1)} fusion(bf16[2,1024,256]{2,1,0:T(8,128)(2,1)} %collective-permute-done), kind=kLoop, calls=%fused_computation.24 | loop fusion | bytes 2097152
  65.1 1.3 %constant_dynamic-update-slice_fusion.1 = bf16[6,1024,256]{2,1,0:T(8,128)(2,1)S(1)} fusion(bf16[6,1024,256]{2,1,0:T(8,128)(2,1)S(1)} %constant_dynamic-update-slice_fusion.2, bf16[2,1024,256]{2,1,0:T(8,128)(2,1)} %param.9), kind=kLoop, calls=%fused_computation.23 | loop fusion | bytes 2097152
  66.4 0.0 collective-permute-done.1
  66.4 1.3 %constant_dynamic-update-slice_fusion = bf16[6,1024,256]{2,1,0:T(8,128)(2,1)S(1)} fusion(bf16[6,1024,256]{2,1,0:T(8,128)(2,1)S(1)} %constant_dynamic-update-slice_fusion.1, bf16[2,1024,256]{2,1,0:T(8,128)(2,1)} %collective-permute-done.1), kind=kLoop, calls=%fused_computation.22 | loop fusion | bytes 2097152 | tf_op jit(solution)/shard_map/concatenate | solution.py:13
  67.7 4.7 %gather_fusion = bf16[16,1024,256]{2,1,0:T(8,128)(2,1)} fusion(bf16[6,1024,256]{2,1,0:T(8,128)(2,1)S(1)} %constant_dynamic-update-slice_fusion, s32[1024]{0:T(1024)S(1)} %get-tuple-element.14), kind=kCustom, calls=%fused_computation | custom fusion | bytes 16777280 | tf_op jit(solution)/shard_map/gather | solution.py:81
  72.3 4.8 %gather_fusion.1 = bf16[16,1024,256]{2,1,0:T(8,128)(2,1)} fusion(bf16[6,1024,256]{2,1,0:T(8,128)(2,1)S(1)} %constant_dynamic-update-slice_fusion, s32[1024]{0:T(1024)S(1)} %get-tuple-element.13), kind=kCustom, calls=%fused_computation.1 | custom fusion | bytes 16777280 | tf_op jit(solution)/shard_map/gather | solution.py:82
  77.1 8.2 %fusion.23 = f32[16,256,256]{2,1,0:T(8,128)S(1)} fusion(bf16[16,1024,256]{2,1,0:T(8,128)(2,1)} %gather_fusion, bf16[16,1024,256]{2,1,0:T(8,128)(2,1)} %gather_fusion.1), kind=kOutput, calls=%fused_computation.42 | convolution fusion | flops 2147483648 | bytes 20971520 | tf_op jit(solution)/shard_map/pqa,pqb->pab/dot_general | solution.py:83
  85.3 0.5 copy.27
  85.8 8.2 %all_to_all.5 = f32[2,16,128,256]{3,2,1,0:T(8,128)} all-to-all(f32[2,16,128,256]{3,2,1,0:T(8,128)S(1)} %bitcast.26), channel_id=1, replica_groups=mesh['pairs'=128,'aux'=2] {'aux'}, dimensions={0} | all-to-all | bytes 8388608 | tf_op jit(solution)/shard_map/all_to_all | solution.py:31
  94.0 0.0 copy-start.1
  94.0 2.7 %reduce_sum.27 = f32[16,128,256]{2,1,0:T(8,128)S(1)} reduce(f32[2,16,128,256]{3,2,1,0:T(8,128)} %all_to_all.5, f32[]{:T(128)} %constant.5.clone.1), dimensions={0}, to_apply=%region_0.0 | reduce | flops 524288 | bytes 6291460 | tf_op jit(solution)/shard_map/reduce_sum | solution.py:32
  96.7 10.0 %collective-permute-done.2 = f32[16,128,256]{2,1,0:T(8,128)} collective-permute-done((f32[16,128,256]{2,1,0:T(8,128)}, f32[16,128,256]{2,1,0:T(8,128)}, u32[]{:S(2)}, u32[]{:S(2)}) %collective-permute-start.2) | collective-permute-done | bytes 2097184 | tf_op jit(solution)/shard_map/ppermute | solution.py:38
  106.8 1.2 %collective-permute-done.3 = f32[16,128,256]{2,1,0:T(8,128)} collective-permute-done((f32[16,128,256]{2,1,0:T(8,128)}, f32[16,128,256]{2,1,0:T(8,128)}, u32[]{:S(2)}, u32[]{:S(2)}) %collective-permute-start.3) | collective-permute-done | bytes 2097184 | tf_op jit(solution)/shard_map/ppermute | solution.py:38
  107.9 4.6 %fusion.13 = f32[16,128,256]{2,1,0:T(8,128)} fusion(f32[16,128,256]{2,1,0:T(8,128)} %collective-permute-done.3, f32[16,128,256]{2,1,0:T(8,128)} %collective-permute-done.2, f32[48,128,256]{2,1,0:T(8,128)} %scatter_fusion, f32[16,128,256]{2,1,0:T(8,128)S(1)} %reduce_sum.27, f32[16,256]{1,0:T(8,128)S(1)} %fusion.16, f32[16,128]{1,0:T(8,128)S(1)} %compare_convert_fusion, ...), kind=kLoop, calls=%fused_computation.13 | loop fusion | flops 5242880 | bytes 11583556 | tf_op jit(solution)/shard_map/mul | solution.py:113
  112.5 0.0 copy-done.1
  (6 shorter events, 0.0 us)
Async XLA Ops:
  0.0 12.2 %copy-start = (f32[2048,4]{0,1:T(4,128)S(1)}, f32[2048,4]{0,1:T(4,128)}, u32[]{:S(2)}) copy-start(f32[2048,4]{0,1:T(4,128)} %param.15) | copy-start | bytes 98308
  0.0 63.8 %collective-permute-start = (bf16[2,1024,256]{2,1,0:T(8,128)(2,1)}, bf16[2,1024,256]{2,1,0:T(8,128)(2,1)}, u32[]{:S(2)}, u32[]{:S(2)}) collective-permute-start(bf16[2,1024,256]{2,1,0:T(8,128)(2,1)} %param.9), channel_id=1, source_target_pairs={{0,2},{2,4},{4,6},{6,8},{8,10},{10,12},{12,14},{14,16},{16,18},{18... | collective-permute-start | bytes 3145736 | tf_op jit(solution)/shard_map/ppermute | solution.py:15
  4.0 62.4 %collective-permute-start.1 = (bf16[2,1024,256]{2,1,0:T(8,128)(2,1)}, bf16[2,1024,256]{2,1,0:T(8,128)(2,1)}, u32[]{:S(2)}, u32[]{:S(2)}) collective-permute-start(bf16[2,1024,256]{2,1,0:T(8,128)(2,1)} %param.9), channel_id=1, source_target_pairs={{2,0},{4,2},{6,4},{8,6},{10,8},{12,10},{14,12},{16,14},{18,16},{20... | collective-permute-start | bytes 3145736 | tf_op jit(solution)/shard_map/ppermute | solution.py:17
  48.5 14.8 %copy-start.4 = (s32[16,2]{0,1:T(2,128)S(1)}, s32[16,2]{0,1:T(2,128)}, u32[]{:S(2)}) copy-start(s32[16,2]{0,1:T(2,128)} %param.10) | copy-start | bytes 388
  48.5 14.8 %copy-start.5 = (f32[256]{0:T(256)S(1)}, f32[256]{0:T(256)}, u32[]{:S(2)}) copy-start(f32[256]{0:T(256)} %param.17) | copy-start | bytes 3076
  48.5 15.0 %copy-start.2 = (f32[16,256]{1,0:T(8,128)S(1)}, f32[16,256]{1,0:T(8,128)}, u32[]{:S(2)}) copy-start(f32[16,256]{1,0:T(8,128)} %param.16) | copy-start | bytes 49156
  48.5 15.1 %copy-start.3 = (s32[16]{0:T(128)S(1)}, s32[16]{0:T(128)}, u32[]{:S(2)}) copy-start(s32[16]{0:T(128)} %param.11) | copy-start | bytes 196
  53.2 53.5 %collective-permute-start.2 = (f32[16,128,256]{2,1,0:T(8,128)}, f32[16,128,256]{2,1,0:T(8,128)}, u32[]{:S(2)}, u32[]{:S(2)}) collective-permute-start(f32[16,128,256]{2,1,0:T(8,128)} %get-tuple-element.7), channel_id=1, source_target_pairs={{0,2},{2,4},{4,6},{6,8},{8,10},{10,12},{12,14},{14,16},{16,18},{18... | collective-permute-start | bytes 6291464 | tf_op jit(solution)/shard_map/ppermute | solution.py:38
  55.2 52.8 %collective-permute-start.3 = (f32[16,128,256]{2,1,0:T(8,128)}, f32[16,128,256]{2,1,0:T(8,128)}, u32[]{:S(2)}, u32[]{:S(2)}) collective-permute-start(f32[16,128,256]{2,1,0:T(8,128)} %get-tuple-element.8), channel_id=1, source_target_pairs={{2,0},{4,2},{6,4},{8,6},{10,8},{12,10},{14,12},{16,14},{18,16},{20... | collective-permute-start | bytes 6291464 | tf_op jit(solution)/shard_map/ppermute | solution.py:38
  94.0 18.6 %copy-start.1 = (f32[2048,4]{0,1:T(4,128)S(1)}, f32[2048,4]{0,1:T(4,128)}, u32[]{:S(2)}) copy-start(f32[2048,4]{0,1:T(4,128)} %param.15) | copy-start | bytes 98308
where the time goes:
time: 113 us
  other arithmetic  27.8 us (25%)
  local copies, waits for them, and re-layouts  22.3 us (20%)
  starting transfers between devices  22.2 us (20%)
  matrix products  20.7 us (18%)
  waiting for transfers between devices  11.2 us (10%)
  blocking collectives  8.16 us (7%)
    scatter-add x1, other arithmetic, route_terms(): return empty.at[flat_slots].add(flat_terms, mode='drop')  19.3 us
    dot_general x1, matrix products, coupling_terms(): jnp.einsum('pcal,pcbl->pcab', first_product, source_margins, preferred_el...  12.4 us
    ppermute x2, waiting for transfers between devices, passed_along(): lax.ppermute(value, axis, [(source, source + steps) for source in range(l...  11.2 us
    ppermute x2, starting transfers between devices, passed_along(): lax.ppermute(value, axis, [(source, source + steps) for source in range(l...  10.1 us
    dot_general x1, matrix products, local(): jnp.einsum('pqa,pqb->pab', left_block, right_block, preferred_element_typ...  8.25 us
    ppermute x1, starting transfers between devices, with_halo(): lax.ppermute(head, axis, [((i + 1) % count, i) for i in range(ends)])  8.24 us
    all_to_all x1, blocking collectives, sum_at_owner(): lax.all_to_all(tiles, axis, split_axis=0, concat_axis=0, tiled=True)  8.16 us
    gather x1, local copies, waits for them, and re-layouts, local(): right_block = padded[pair_orbs[:, 1] - base_orb]  4.77 us
  transfers between devices with their start and end apart: 4, of which 2 were waited for; matrix products, arithmetic and copies ran while one was open for 59% of the time, Pallas kernels for 0%

commit v1 on v0

v1 whole, which is shorter than its diff:
```python
import jax
import jax.numpy as jnp
from jax import lax
from jax.experimental import pallas as pl
from jax.experimental.pallas import tpu as pltpu
from jax.sharding import PartitionSpec as P

AXES = ("pairs", "aux")
BF16, F32 = jnp.bfloat16, jnp.float32
VMEM, SMEM = pltpu.VMEM, pltpu.SMEM
UNROLL = 4
MIB = 1 << 20


def toward(count, cross, flip):
    pairs = []
    for holder in range(count):
        for core in range(2):
            step = 1 if (core == 0) != flip else -1
            if 0 <= holder + step < count:
                dest = (1 - core) if cross else core
                pairs.append((2 * holder + core, 2 * (holder + step) + dest))
    return pairs


def nt_dot(a, b):
    return lax.dot_general(a, b, (((1,), (1,)), ((), ())), preferred_element_type=F32)


def tn_dot(a, b):
    return lax.dot_general(a, b, (((0,), (0,)), ((), ())), preferred_element_type=F32)


def coupling_kernel(core_ref, rel_ref, w_ref, amp_hbm, mar_hbm, msg_ref, own_ref,
                    mbuf, abuf, fbuf, dir_list, own_list, msem, asem):
    core = core_ref[0]
    sources, couplings = mar_hbm.shape[0], mar_hbm.shape[1]
    slots = msg_ref.shape[0]
    half = own_ref.shape[1]
    shift = 2 * slots * core - slots

    def mar_copy(k):
        return pltpu.make_async_copy(
            mar_hbm.at[k // couplings, k % couplings], mbuf.at[k], msem.at[k])

    def amp_copy(q):
        return pltpu.make_async_copy(amp_hbm.at[q], abuf.at[q], asem.at[q])

    def scan(q, carry):
        n_dir, n_own = carry
        amp_copy(q).start()
        for c in range(couplings):
            k = q * couplings + c
            r = rel_ref[c, q]
            d = r + shift
            is_dir = (d >= 0) & (d < slots)
            is_own = (r >= 0) & (r < slots)
            dir_list[n_dir] = k
            own_list[n_own] = k

            @pl.when(is_dir | is_own)
            def _():
                mar_copy(k).start()

            n_dir = n_dir + is_dir.astype(jnp.int32)
            n_own = n_own + is_own.astype(jnp.int32)
        return n_dir, n_own

    n_dir, n_own = lax.fori_loop(0, sources, scan, (jnp.int32(0), jnp.int32(0)))
    for u in range(UNROLL):
        dir_list[n_dir + u] = dir_list[0]
        own_list[n_own + u] = own_list[0]

    @pl.loop(0, slots)
    def _(s):
        msg_ref[s] = jnp.zeros(msg_ref.shape[1:], F32)
        own_ref[s] = jnp.zeros(own_ref.shape[1:], F32)

    def run(items, n, rows, row0, acc, offset, waited):
        def body(g, waited):
            ks = [items[g * UNROLL + u] for u in range(UNROLL)]
            last = ks[0] // couplings
            for u in range(UNROLL):
                @pl.when(g * UNROLL + u < n)
                def _(u=u):
                    mar_copy(ks[u]).wait()

                last = jnp.maximum(last, ks[u] // couplings)

            def wait_amp(q, x):
                amp_copy(q).wait()
                return x

            lax.fori_loop(waited, last + 1, wait_amp, 0)
            for u in range(UNROLL):
                left = mbuf[ks[u], pl.ds(row0, rows), :]
                fbuf[u, :rows] = jnp.dot(
                    left, abuf[ks[u] // couplings], preferred_element_type=F32).astype(BF16)
            for u in range(UNROLL):
                c, q = ks[u] % couplings, ks[u] // couplings
                live = g * UNROLL + u < n
                weight = jnp.where(live, w_ref[c, q], 0.0)
                slot = rel_ref[c, q] + offset
                acc[slot] += weight * nt_dot(fbuf[u, :rows], mbuf[ks[u]])
            return jnp.maximum(waited, last + 1)

        return lax.fori_loop(0, pl.cdiv(n, UNROLL), body, waited)

    waited = run(dir_list, n_dir, msg_ref.shape[1], 0, msg_ref, shift, jnp.int32(0))
    row0 = pl.multiple_of(core * half, half)
    waited = run(own_list, n_own, half, row0, own_ref, 0, waited)

    def drain(q, x):
        amp_copy(q).wait()
        return x

    lax.fori_loop(waited, sources, drain, 0)


def coupling(core, rel, weights, amplitudes, margins):
    pairs, width = amplitudes.shape[0], amplitudes.shape[1]
    couplings = margins.shape[1]
    total = pairs * couplings
    any_spec = pl.BlockSpec(memory_space=pltpu.HBM)
    smem_spec = pl.BlockSpec(memory_space=SMEM)
    vmem_spec = pl.BlockSpec(memory_space=VMEM)
    return pl.pallas_call(
        coupling_kernel,
        out_shape=(
            jax.ShapeDtypeStruct((pairs, width, width), F32),
            jax.ShapeDtypeStruct((pairs, width // 2, width), F32),
        ),
        in_specs=[smem_spec, smem_spec, smem_spec, any_spec, any_spec],
        out_specs=(vmem_spec, vmem_spec),
        scratch_shapes=[
            VMEM((total, width, width), BF16),
            VMEM((pairs, width, width), BF16),
            VMEM((UNROLL, width, width), BF16),
            SMEM((total + UNROLL,), jnp.int32),
            SMEM((total + UNROLL,), jnp.int32),
            pltpu.SemaphoreType.DMA((total,)),
            pltpu.SemaphoreType.DMA((pairs,)),
        ],
        compiler_params=pltpu.CompilerParams(vmem_limit_bytes=12 * MIB),
        cost_estimate=pl.CostEstimate(
            flops=4 * 64 * 128 * 256 * 256, bytes_accessed=16 * MIB, transcendentals=0),
        name="coupling",
    )(core, rel, weights, amplitudes, margins)


def message_kernel(half_ref, pick_ref, a_in, b_in, a_loc, b_loc, acc_ref, out_ref, prod):
    step = pl.program_id(0)
    per = out_ref.shape[0]

    @pl.when(step == 0)
    def _():
        for j in range(2):
            for i in range(2):
                prod[2 * j + i] = tn_dot(a_in[j], a_loc[i]) + tn_dot(b_in[j], b_loc[i])
        prod[4] = jnp.zeros(prod.shape[1:], F32)

    for s in range(per):
        pick = pick_ref[step * per + s]
        out_ref[s] = (acc_ref[s] + prod[pick]).astype(BF16)


def message(half, pick, a_in, b_in, a_loc, b_loc, acc, per=4):
    slots, width = acc.shape[0], acc.shape[2]
    rows = width // 2
    depth = a_in.shape[1]
    lhs = pl.BlockSpec((2, depth, rows), lambda s, half, pick: (0, 0, half[0]))
    rhs = pl.BlockSpec((2, depth, width), lambda s, half, pick: (0, 0, 0))
    return pl.pallas_call(
        message_kernel,
        grid_spec=pltpu.PrefetchScalarGridSpec(
            num_scalar_prefetch=2,
            grid=(slots // per,),
            in_specs=[lhs, lhs, rhs, rhs,
                      pl.BlockSpec((per, rows, width), lambda s, half, pick: (s, half[0], 0))],
            out_specs=pl.BlockSpec((per, rows, width), lambda s, half, pick: (s, 0, 0)),
            scratch_shapes=[VMEM((5, rows, width), F32)],
        ),
        out_shape=jax.ShapeDtypeStruct((slots, rows, width), BF16),
        compiler_params=pltpu.CompilerParams(vmem_limit_bytes=16 * MIB),
        cost_estimate=pl.CostEstimate(
            flops=8 * 2 * 128 * 256 * 512, bytes_accessed=5 * MIB, transcendentals=0),
        name="message",
    )(half, pick, a_in, b_in, a_loc, b_loc, acc)


def exchange_kernel(core_ref, a_in, b_in, a_loc, b_loc, blk, blk_all, out_ref):
    for i in range(2):
        for j in range(2):
            out_ref[0, 2 * i + j] = tn_dot(a_loc[i], a_in[j]) + tn_dot(b_loc[i], b_in[j])
            out_ref[0, 4 + 2 * i + j] = tn_dot(blk[i], blk_all[j])


def exchange(core, a_in, b_in, a_loc, b_loc, blocks):
    depth, width = a_in.shape[1], a_in.shape[2]
    rows = width // 2
    side = lambda g, core: (0, 0, g + core[0] - 2 * g * core[0])
    full = lambda g, core: (0, 0, 0)
    lhs = pl.BlockSpec((2, depth, rows), side)
    rhs = pl.BlockSpec((2, depth, width), full)
    return pl.pallas_call(
        exchange_kernel,
        grid_spec=pltpu.PrefetchScalarGridSpec(
            num_scalar_prefetch=1,
            grid=(2,),
            in_specs=[rhs, rhs, lhs, lhs,
                      pl.BlockSpec((2, blocks.shape[1], rows), side),
                      pl.BlockSpec((2, blocks.shape[1], width), full)],
            out_specs=pl.BlockSpec((1, 8, rows, width), lambda g, core: (g, 0, 0, 0)),
        ),
        out_shape=jax.ShapeDtypeStruct((2, 8, rows, width), F32),
        compiler_params=pltpu.CompilerParams(vmem_limit_bytes=12 * MIB),
        cost_estimate=pl.CostEstimate(
            flops=2 * 8 * 2 * 256 * 256 * 1024, bytes_accessed=6 * MIB, transcendentals=0),
        name="exchange",
    )(core, a_in, b_in, a_loc, b_loc, blocks, blocks)


def base_kernel(core_ref, keep_ix, recv_ix, fkeep, frecv, shift_ref, en_ref, amp_ref, own_ref,
                near_ref, keep_ref, recv_ref, out_ref):
    step = pl.program_id(0)
    per, rows, width = out_ref.shape
    core = core_ref[0]
    for s in range(per):
        p = step * per + s
        cols = en_ref[pl.ds(p, 1), :]
        side = jnp.where(core == 0, cols[:, :rows], cols[:, rows:])
        down = jnp.broadcast_to(side, (rows, rows)).T
        down = jnp.concatenate([down] * (width // rows), axis=1)
        denom = down + cols - shift_ref[p]
        value = denom * amp_ref[s].astype(F32) + own_ref[s] + near_ref[s].astype(F32)
        value += keep_ref[0, keep_ix[p]] * fkeep[p]
        value += recv_ref[recv_ix[p]] * frecv[p]
        out_ref[s] = value


def base(core, keep_ix, recv_ix, fkeep, frecv, shift, energy, amplitudes, own, near, both, recv, per=4):
    slots, rows, width = own.shape
    tile = pl.BlockSpec((per, rows, width), lambda s, core, *_: (s, 0, 0))
    return pl.pallas_call(
        base_kernel,
        grid_spec=pltpu.PrefetchScalarGridSpec(
            num_scalar_prefetch=6,
            grid=(slots // per,),
            in_specs=[
                pl.BlockSpec((slots, width), lambda s, core, *_: (0, 0)),
                pl.BlockSpec((per, rows, width), lambda s, core, *_: (s, core[0], 0)),
                tile, tile,
                pl.BlockSpec((1, 8, rows, width), lambda s, core, *_: (0, 0, 0, 0)),
                pl.BlockSpec((8, rows, width), lambda s, core, *_: (0, 0, 0)),
            ],
            out_specs=tile,
        ),
        out_shape=jax.ShapeDtypeStruct((slots, rows, width), F32),
        compiler_params=pltpu.CompilerParams(vmem_limit_bytes=16 * MIB),
        cost_estimate=pl.CostEstimate(
            flops=16 * 128 * 256 * 8, bytes_accessed=8 * MIB, transcendentals=0),
        name="base",
    )(core, keep_ix, recv_ix, fkeep, frecv, shift, energy, amplitudes, own, near, both, recv)


def final_kernel(core_ref, count_ref, base_ref, far_ref, out_ref):
    step = pl.program_id(0)
    per, rows, width = out_ref.shape
    row = lax.broadcasted_iota(jnp.int32, (rows, width), 0) + core_ref[0] * rows
    col = lax.broadcasted_iota(jnp.int32, (rows, width), 1)
    most = jnp.maximum(row, col)
    for s in range(per):
        value = base_ref[s] + far_ref[s].astype(F32)
        out_ref[s] = jnp.where(most < count_ref[step * per + s], value, 0.0)


def final(core, count, base_terms, far, per=4):
    slots, rows, width = base_terms.shape
    tile = pl.BlockSpec((per, rows, width), lambda s, *_: (s, 0, 0))
    return pl.pallas_call(
        final_kernel,
        grid_spec=pltpu.PrefetchScalarGridSpec(
            num_scalar_prefetch=2,
            grid=(slots // per,),
            in_specs=[tile, tile],
            out_specs=tile,
        ),
        out_shape=jax.ShapeDtypeStruct((slots, rows, width), F32),
        compiler_params=pltpu.CompilerParams(vmem_limit_bytes=8 * MIB),
        cost_estimate=pl.CostEstimate(
            flops=16 * 128 * 256 * 2, bytes_accessed=5 * MIB, transcendentals=0),
        name="final",
    )(core, count, base_terms, far)


def local(blocks, pair_orbs, pno_count, amplitudes, margins, couple_target, couple_weight,
          pno_energy, occ_energy):
    holder = lax.axis_index("pairs").astype(jnp.int32)
    core = lax.axis_index("aux").astype(jnp.int32)
    holders = lax.axis_size("pairs")
    pairs = amplitudes.shape[0]
    orbs = blocks.shape[0]
    depth = blocks.shape[1] // 2
    straight_in = toward(holders, False, True)
    cross_in = toward(holders, True, False)
    straight_out = toward(holders, False, False)
    swap = [(2 * h + c, 2 * h + 1 - c) for h in range(holders) for c in range(2)]

    a_loc = blocks[:, :depth]
    b_own = blocks[:, depth:]
    a_in = lax.ppermute(a_loc, AXES, straight_in)
    b_in = lax.ppermute(b_own, AXES, cross_in)
    b_loc = lax.ppermute(b_own, AXES, swap)
    near_orbs = lax.ppermute(pair_orbs, AXES, straight_in)

    core1 = core.reshape(1)
    rel = lax.dynamic_slice_in_dim(couple_target, holder * pairs, pairs, 0).T - holder * pairs
    weights = lax.dynamic_slice_in_dim(couple_weight, holder * pairs, pairs, 0).T
    msg_acc, own_acc = coupling(
        core1, rel, weights,
        pltpu.with_memory_space_constraint(amplitudes, pltpu.HBM),
        pltpu.with_memory_space_constraint(margins, pltpu.HBM))

    step = 1 - 2 * core
    first = jnp.clip(near_orbs[:, 0] - (holder + step) * orbs, 0, orbs - 1)
    second = near_orbs[:, 1] - holder * orbs
    mine = (second >= 0) & (second < orbs)
    pick = jnp.where(mine, orbs * first + second, 4)

    msg_near = message(core1, pick, a_in, b_in, a_loc, b_loc, msg_acc)
    near = lax.ppermute(msg_near, AXES, straight_out)
    msg_far = message(1 - core1, pick, a_in, b_in, a_loc, b_loc, msg_acc)
    far = lax.ppermute(msg_far, AXES, cross_in)
    both = exchange(core1, a_in, b_in, a_loc, b_loc, blocks)
    recv = lax.ppermute(both[1], AXES, swap)

    i_loc = pair_orbs[:, 0] - holder * orbs
    j_all = pair_orbs[:, 1]
    side = j_all // orbs - holder
    j_loc = j_all % orbs
    index = orbs * i_loc + j_loc
    index = jnp.where(side == 0, index + 4, index)
    fkeep = ((side == 0) | (side == step)).astype(F32)
    frecv = ((side == 0) | (side == -step)).astype(F32)
    orbital = jnp.arange(occ_energy.shape[0], dtype=jnp.int32)
    shift = jnp.sum(
        jnp.where(pair_orbs[:, 0:1] == orbital, occ_energy, 0.0)
        + jnp.where(pair_orbs[:, 1:2] == orbital, occ_energy, 0.0), axis=1)
    base_terms = base(core1, index, index, fkeep, frecv, shift, pno_energy, amplitudes, own_acc,
                      near, both, recv)
    return final(core1, pno_count, base_terms, far)


def solution(mesh):
    placed = (
        P("pairs", "aux", None),
        P("pairs", None),
        P("pairs"),
        P("pairs", None, None),
        P("pairs", None, None, None),
        P(),
        P(),
        P("pairs", None),
        P(),
    )
    return jax.shard_map(
        local, mesh=mesh, in_specs=placed, out_specs=P("pairs", "aux", None), check_vma=False
    )
```

time: 113 us -> 73.3 us (0.65)
  the two profiles are of different devices: /device:TPU:24 before, /device:TPU:25 now
where the time goes in v1:
time: 73.3 us; the launch traced here: 72.8 us
  Pallas kernels  25.7 us (35%)
  starting transfers between devices  24.5 us (33%)
  waiting for transfers between devices  13.6 us (19%)
  local copies, waits for them, and re-layouts  7.76 us (11%)
  other arithmetic  0.99 us (1%)
    ppermute x1, starting transfers between devices, local(): b_in = lax.ppermute(b_own, AXES, cross_in)  9.74 us
    pallas_call x1, Pallas kernels, coupling(): pl.pallas_call(coupling_kernel, out_shape=(jax.ShapeDtypeStruct((pairs, w...  8.66 us
    ppermute x1, waiting for transfers between devices, local(): far = lax.ppermute(msg_far, AXES, cross_in)  7.81 us
    pallas_call x2, Pallas kernels, message(): pl.pallas_call(message_kernel, grid_spec=pltpu.PrefetchScalarGridSpec(num...  7.59 us
    ppermute x1, starting transfers between devices, local(): near = lax.ppermute(msg_near, AXES, straight_out)  5.43 us
    ppermute x1, starting transfers between devices, local(): far = lax.ppermute(msg_far, AXES, cross_in)  4.86 us
    unnamed x22, local copies, waits for them, and re-layouts  4.56 us
    pallas_call x1, Pallas kernels, base(): pl.pallas_call(base_kernel, grid_spec=pltpu.PrefetchScalarGridSpec(num_sc...  3.82 us
  transfers between devices with their start and end apart: 7, of which 3 were waited for; matrix products, arithmetic and copies ran while one was open for 1% of the time, Pallas kernels for 28%

profile of v1, /device:TPU:25, one launch (start us, length us, event | category | flops | bytes accessed | tf_op | source)
XLA Modules:
  0.0 72.8 jit_solution(8863032665931328574)
XLA Ops:
  0.0 0.0 copy-start
  0.0 0.0 copy-start.9
  0.0 2.1 %fusion.4 = (bf16[2,512,256]{2,1,0:T(8,128)(2,1)}, bf16[2,512,256]{2,1,0:T(8,128)(2,1)S(1)}) fusion(bf16[2,1024,256]{2,1,0:T(8,128)(2,1)} %blk_all.1), kind=kLoop, calls=%fused_computation.21 | loop fusion | bytes 2097152 | tf_op jit(solution)/shard_map/slice | solution.py:310
  2.1 0.7 collective-permute-start.3
  2.8 9.7 %collective-permute-start.2 = (bf16[2,512,256]{2,1,0:T(8,128)(2,1)}, bf16[2,512,256]{2,1,0:T(8,128)(2,1)}, u32[]{:S(2)}, u32[]{:S(2)}) collective-permute-start(bf16[2,512,256]{2,1,0:T(8,128)(2,1)} %get-tuple-element.11), channel_id=1, source_target_pairs={{0,3},{2,5},{3,0},{4,7},{5,2},{6,9},{7,4},{8,11},{9,6},{10,13},{11... | collective-permute-start | bytes 1572872 | tf_op jit(solution)/shard_map/ppermute | solution.py:312
  12.5 0.0 copy-done.9
  12.5 1.9 %collective-permute-start = (s32[16,2]{0,1:T(2,128)S(1)}, s32[16,2]{0,1:T(2,128)S(1)}, u32[]{:S(2)}, u32[]{:S(2)}) collective-permute-start(s32[16,2]{0,1:T(2,128)S(1)} %copy-done.9), channel_id=1, source_target_pairs={{1,3},{2,0},{3,5},{4,2},{5,7},{6,4},{7,9},{8,6},{9,11},{10,8},{11,... | collective-permute-start | bytes 392 | tf_op jit(solution)/shard_map/ppermute | solution.py:314
  14.4 1.9 %collective-permute-start.1 = (bf16[2,512,256]{2,1,0:T(8,128)(2,1)S(1)}, bf16[2,512,256]{2,1,0:T(8,128)(2,1)}, u32[]{:S(2)}, u32[]{:S(2)}) collective-permute-start(bf16[2,512,256]{2,1,0:T(8,128)(2,1)S(1)} %get-tuple-element.12.a_loc), channel_id=1, source_target_pairs={{1,3},{2,0},{3,5},{4,2},{5,7},{6,4},{7,9},{8,6},{9,11},{10,8},{11,... | collective-permute-start | bytes 1572872 | tf_op jit(solution)/shard_map/ppermute | solution.py:311
  16.4 0.8 %subtract_bitcast_fusion.rel_ref = s32[4,16]{1,0:T(4,128)S(1)} fusion(s32[2048,4]{0,1:T(4,128)} %param.14, s32[]{:T(128)S(6)} %select_n.35, s32[]{:T(128)S(6)} %mul.25), kind=kLoop, calls=%fused_computation.5 | loop fusion | flops 64 | bytes 520 | tf_op jit(solution)/shard_map/sub | solution.py:317
  17.2 0.0 copy-done
  17.2 0.1 dynamic-slice_bitcast_fusion.w_ref
  17.2 0.0 copy-start.6
  17.2 8.7 %coupling.1 = (f32[16,256,256]{2,1,0:T(8,128)S(1)}, f32[16,128,256]{2,1,0:T(8,128)S(1)}) custom-call(s32[1]{0:T(128)} %bitcast.core_ref.half_ref, s32[4,16]{1,0:T(4,128)S(1)} %subtract_bitcast_fusion.rel_ref, f32[4,16]{1,0:T(4,128)S(1)} %dynamic-slice_bitcast_fusion.w_ref, bf16[16,256,256]{2,1,0:T(8,128)(2,1)} %amp_ref.1, bf16[16,4,256,256]{3,2,1,0:T(8,128)(2,1)} %mar_hbm.1), custom_call_target="tpu_custom_call" | custom-call | flops 2147483648 | bytes 16777216 | tf_op jit(solution)/shard_map/coupling/pallas_call | solution.py:127
  25.9 0.0 copy-start.4
  25.9 0.0 collective-permute-done
  25.9 0.0 collective-permute-done.3.b_loc
  25.9 0.0 collective-permute-done.2.b_in
  26.0 2.7 %collective-permute-done.1.a_in = bf16[2,512,256]{2,1,0:T(8,128)(2,1)} collective-permute-done((bf16[2,512,256]{2,1,0:T(8,128)(2,1)S(1)}, bf16[2,512,256]{2,1,0:T(8,128)(2,1)}, u32[]{:S(2)}, u32[]{:S(2)}) %collective-permute-start.1) | collective-permute-done | bytes 524320 | tf_op jit(solution)/shard_map/ppermute | solution.py:311
  28.7 0.0 copy-done.6
  28.7 3.1 %exchange.1.keep_ref = f32[2,8,128,256]{3,2,1,0:T(8,128)S(1)} custom-call(s32[1]{0:T(128)} %bitcast.core_ref.half_ref, bf16[2,512,256]{2,1,0:T(8,128)(2,1)} %collective-permute-done.1.a_in, bf16[2,512,256]{2,1,0:T(8,128)(2,1)} %collective-permute-done.2.b_in, bf16[2,512,256]{2,1,0:T(8,128)(2,1)S(1)} %get-tuple-element.12.a_loc, ...), custom_call_target="tpu_custom_call" | custom-call | flops 2147483648 | bytes 6291456 | tf_op jit(solution)/shard_map/exchange/pallas_call | solution.py:205
  31.8 0.0 copy-done.4
  31.8 1.0 %slice_bitcast_fusion = f32[8,128,256]{2,1,0:T(8,128)} fusion(f32[2,8,128,256]{3,2,1,0:T(8,128)S(1)} %exchange.1.keep_ref), kind=kLoop, calls=%fused_computation | loop fusion | bytes 2097152 | tf_op jit(solution)/shard_map/squeeze | solution.py:335
  32.9 0.0 copy-start.2
  32.9 1.3 %copy-done.2 = f32[2,8,128,256]{3,2,1,0:T(8,128)} copy-done((f32[2,8,128,256]{3,2,1,0:T(8,128)}, f32[2,8,128,256]{3,2,1,0:T(8,128)S(1)}, u32[]{:S(2)}) %copy-start.2) | copy-done | bytes 2097176
  34.2 0.0 collective-permute-start.5
  34.2 3.8 %message.2 = bf16[16,128,256]{2,1,0:T(8,128)(2,1)} custom-call(s32[1]{0:T(128)} %bitcast.core_ref.half_ref, s32[16]{0:T(128)S(1)} %fusion.1.pick_ref, bf16[2,512,256]{2,1,0:T(8,128)(2,1)} %collective-permute-done.1.a_in, bf16[2,512,256]{2,1,0:T(8,128)(2,1)} %collective-permute-done.2.b_in, bf16[2,512,256]{2,1,0:T(8,128)(2,1)S(1)} %get-tuple-element.12.a_loc, ...), custom_call_target="tpu_custom_call" | custom-call | flops 268435456 | bytes 5242880 | tf_op jit(solution)/shard_map/message/pallas_call | solution.py:173
  38.0 0.0 copy-start.10
  38.0 0.0 copy-start.1
  38.0 0.0 copy-start.7
  38.0 5.4 %collective-permute-start.4 = (bf16[16,128,256]{2,1,0:T(8,128)(2,1)}, bf16[16,128,256]{2,1,0:T(8,128)(2,1)}, u32[]{:S(2)}, u32[]{:S(2)}) collective-permute-start(bf16[16,128,256]{2,1,0:T(8,128)(2,1)} %message.2), channel_id=1, source_target_pairs={{0,2},{2,4},{3,1},{4,6},{5,3},{6,8},{7,5},{8,10},{9,7},{10,12},{11... | collective-permute-start | bytes 3145736 | tf_op jit(solution)/shard_map/ppermute | solution.py:331
  43.4 3.8 %message.3 = bf16[16,128,256]{2,1,0:T(8,128)(2,1)} custom-call(s32[1]{0:T(128)S(6)} %sub.57.half_ref, s32[16]{0:T(128)S(1)} %fusion.1.pick_ref, bf16[2,512,256]{2,1,0:T(8,128)(2,1)} %collective-permute-done.1.a_in, bf16[2,512,256]{2,1,0:T(8,128)(2,1)} %collective-permute-done.2.b_in, bf16[2,512,256]{2,1,0:T(8,128)(2,1)S(1)} %get-tuple-element.12.a_loc, ...), custom_call_target="tpu_custom_call" | custom-call | flops 268435456 | bytes 5242880 | tf_op jit(solution)/shard_map/message/pallas_call | solution.py:173
  47.3 4.9 %collective-permute-start.6 = (bf16[16,128,256]{2,1,0:T(8,128)(2,1)}, bf16[16,128,256]{2,1,0:T(8,128)(2,1)S(1)}, u32[]{:S(2)}, u32[]{:S(2)}) collective-permute-start(bf16[16,128,256]{2,1,0:T(8,128)(2,1)} %message.3), channel_id=1, source_target_pairs={{0,3},{2,5},{3,0},{4,7},{5,2},{6,9},{7,4},{8,11},{9,6},{10,13},{11... | collective-permute-start | bytes 3145736 | tf_op jit(solution)/shard_map/ppermute | solution.py:333
  52.1 0.0 copy-done.10
  52.2 0.2 add_reduce_fusion.shift_ref
  52.4 0.0 collective-permute-done.5.recv_ref
  52.4 3.1 %collective-permute-done.4.near_ref = bf16[16,128,256]{2,1,0:T(8,128)(2,1)} collective-permute-done((bf16[16,128,256]{2,1,0:T(8,128)(2,1)}, bf16[16,128,256]{2,1,0:T(8,128)(2,1)}, u32[]{:S(2)}, u32[]{:S(2)}) %collective-permute-start.4) | collective-permute-done | bytes 1048608 | tf_op jit(solution)/shard_map/ppermute | solution.py:331
  55.5 0.0 copy-done.1
  55.5 0.0 copy-done.7
  55.5 0.0 copy-start.3
  55.5 1.6 %copy-done.3 = f32[2,8,128,256]{3,2,1,0:T(8,128)S(1)} copy-done((f32[2,8,128,256]{3,2,1,0:T(8,128)S(1)}, f32[2,8,128,256]{3,2,1,0:T(8,128)}, u32[]{:S(2)}) %copy-start.3) | copy-done | bytes 2097176
  57.1 0.0 copy-start.5
  57.1 1.6 %copy-done.5 = f32[16,128,256]{2,1,0:T(8,128)S(1)} copy-done((f32[16,128,256]{2,1,0:T(8,128)S(1)}, f32[16,128,256]{2,1,0:T(8,128)}, u32[]{:S(2)}) %copy-start.5) | copy-done | bytes 2097176
  58.7 0.0 copy-start.8
  58.7 3.8 %base.1.base_ref = f32[16,128,256]{2,1,0:T(8,128)S(1)} custom-call(s32[1]{0:T(128)} %bitcast.core_ref.half_ref, s32[16]{0:T(128)S(1)} %add_select_fusion.keep_ix.recv_ix, s32[16]{0:T(128)S(1)} %add_select_fusion.keep_ix.recv_ix, f32[16]{0:T(128)S(1)} %or_convert_fusion.1.fkeep, f32[16]{0:T(128)S(1)} %get-tuple-element.9.frecv, ...), custom_call_target="tpu_custom_call" | custom-call | flops 4194304 | bytes 8388608 | tf_op jit(solution)/shard_map/base/pallas_call | solution.py:244
  62.5 7.8 %collective-permute-done.6.far_ref = bf16[16,128,256]{2,1,0:T(8,128)(2,1)S(1)} collective-permute-done((bf16[16,128,256]{2,1,0:T(8,128)(2,1)}, bf16[16,128,256]{2,1,0:T(8,128)(2,1)S(1)}, u32[]{:S(2)}, u32[]{:S(2)}) %collective-permute-start.6) | collective-permute-done | bytes 1048608 | tf_op jit(solution)/shard_map/ppermute | solution.py:333
  70.3 0.0 copy-done.8
  70.3 2.5 %final.1 = f32[16,128,256]{2,1,0:T(8,128)} custom-call(s32[1]{0:T(128)} %bitcast.core_ref.half_ref, s32[16]{0:T(128)S(1)} %copy-done.8, f32[16,128,256]{2,1,0:T(8,128)S(1)} %base.1.base_ref, bf16[16,128,256]{2,1,0:T(8,128)(2,1)S(1)} %collective-permute-done.6.far_ref), custom_call_target="tpu_custom_call" | custom-call | flops 1048576 | bytes 5242880 | tf_op jit(solution)/shard_map/final/pallas_call | solution.py:280
  (5 shorter events, 0.1 us)
Async XLA Ops:
  0.0 17.2 %copy-start = (f32[2048,4]{0,1:T(4,128)S(1)}, f32[2048,4]{0,1:T(4,128)}, u32[]{:S(2)}) copy-start(f32[2048,4]{0,1:T(4,128)} %param.15) | copy-start | bytes 98308
  0.0 12.5 %copy-start.9 = (s32[16,2]{0,1:T(2,128)S(1)}, s32[16,2]{0,1:T(2,128)}, u32[]{:S(2)}) copy-start(s32[16,2]{0,1:T(2,128)} %param.10) | copy-start | bytes 388
  2.1 23.9 %collective-permute-start.3 = (bf16[2,512,256]{2,1,0:T(8,128)(2,1)}, bf16[2,512,256]{2,1,0:T(8,128)(2,1)S(1)}, u32[]{:S(2)}, u32[]{:S(2)}) collective-permute-start(bf16[2,512,256]{2,1,0:T(8,128)(2,1)} %get-tuple-element.11), channel_id=1, source_target_pairs={{0,1},{1,0},{2,3},{3,2},{4,5},{5,4},{6,7},{7,6},{8,9},{9,8},{10,11... | collective-permute-start | bytes 1572872 | tf_op jit(solution)/shard_map/ppermute | solution.py:313
  2.8 23.2 %collective-permute-start.2 = (bf16[2,512,256]{2,1,0:T(8,128)(2,1)}, bf16[2,512,256]{2,1,0:T(8,128)(2,1)}, u32[]{:S(2)}, u32[]{:S(2)}) collective-permute-start(bf16[2,512,256]{2,1,0:T(8,128)(2,1)} %get-tuple-element.11), channel_id=1, source_target_pairs={{0,3},{2,5},{3,0},{4,7},{5,2},{6,9},{7,4},{8,11},{9,6},{10,13},{11... | collective-permute-start | bytes 1572872 | tf_op jit(solution)/shard_map/ppermute | solution.py:312
  12.5 13.4 %collective-permute-start = (s32[16,2]{0,1:T(2,128)S(1)}, s32[16,2]{0,1:T(2,128)S(1)}, u32[]{:S(2)}, u32[]{:S(2)}) collective-permute-start(s32[16,2]{0,1:T(2,128)S(1)} %copy-done.9), channel_id=1, source_target_pairs={{1,3},{2,0},{3,5},{4,2},{5,7},{6,4},{7,9},{8,6},{9,11},{10,8},{11,... | collective-permute-start | bytes 392 | tf_op jit(solution)/shard_map/ppermute | solution.py:314
  14.4 14.3 %collective-permute-start.1 = (bf16[2,512,256]{2,1,0:T(8,128)(2,1)S(1)}, bf16[2,512,256]{2,1,0:T(8,128)(2,1)}, u32[]{:S(2)}, u32[]{:S(2)}) collective-permute-start(bf16[2,512,256]{2,1,0:T(8,128)(2,1)S(1)} %get-tuple-element.12.a_loc), channel_id=1, source_target_pairs={{1,3},{2,0},{3,5},{4,2},{5,7},{6,4},{7,9},{8,6},{9,11},{10,8},{11,... | collective-permute-start | bytes 1572872 | tf_op jit(solution)/shard_map/ppermute | solution.py:311
  17.2 11.5 %copy-start.6 = (bf16[2,1024,256]{2,1,0:T(8,128)(2,1)S(1)}, bf16[2,1024,256]{2,1,0:T(8,128)(2,1)}, u32[]{:S(2)}) copy-start(bf16[2,1024,256]{2,1,0:T(8,128)(2,1)} %blk_all.1) | copy-start | bytes 3145732
  25.9 5.9 %copy-start.4 = (f32[16,128,256]{2,1,0:T(8,128)}, f32[16,128,256]{2,1,0:T(8,128)S(1)}, u32[]{:S(2)}) copy-start(f32[16,128,256]{2,1,0:T(8,128)S(1)} %get-tuple-element.7.own_ref) | copy-start | bytes 6291460
  32.9 1.3 %copy-start.2 = (f32[2,8,128,256]{3,2,1,0:T(8,128)}, f32[2,8,128,256]{3,2,1,0:T(8,128)S(1)}, u32[]{:S(2)}) copy-start(f32[2,8,128,256]{3,2,1,0:T(8,128)S(1)} %exchange.1.keep_ref) | copy-start | bytes 6291460
  34.2 18.2 %collective-permute-start.5 = (f32[8,128,256]{2,1,0:T(8,128)}, f32[8,128,256]{2,1,0:T(8,128)}, u32[]{:S(2)}, u32[]{:S(2)}) collective-permute-start(f32[8,128,256]{2,1,0:T(8,128)} %slice_bitcast_fusion), channel_id=1, source_target_pairs={{0,1},{1,0},{2,3},{3,2},{4,5},{5,4},{6,7},{7,6},{8,9},{9,8},{10,11... | collective-permute-start | bytes 3145736 | tf_op jit(solution)/shard_map/ppermute | solution.py:335
  38.0 14.1 %copy-start.10 = (f32[256]{0:T(256)S(1)}, f32[256]{0:T(256)}, u32[]{:S(2)}) copy-start(f32[256]{0:T(256)} %param.17) | copy-start | bytes 3076
  38.0 17.5 %copy-start.1 = (bf16[16,256,256]{2,1,0:T(8,128)(2,1)S(1)}, bf16[16,256,256]{2,1,0:T(8,128)(2,1)}, u32[]{:S(2)}) copy-start(bf16[16,256,256]{2,1,0:T(8,128)(2,1)} %amp_ref.1) | copy-start | bytes 6291460
  38.0 17.5 %copy-start.7 = (f32[16,256]{1,0:T(8,128)S(1)}, f32[16,256]{1,0:T(8,128)}, u32[]{:S(2)}) copy-start(f32[16,256]{1,0:T(8,128)} %en_ref.1) | copy-start | bytes 49156
  38.0 17.5 %collective-permute-start.4 = (bf16[16,128,256]{2,1,0:T(8,128)(2,1)}, bf16[16,128,256]{2,1,0:T(8,128)(2,1)}, u32[]{:S(2)}, u32[]{:S(2)}) collective-permute-start(bf16[16,128,256]{2,1,0:T(8,128)(2,1)} %message.2), channel_id=1, source_target_pairs={{0,2},{2,4},{3,1},{4,6},{5,3},{6,8},{7,5},{8,10},{9,7},{10,12},{11... | collective-permute-start | bytes 3145736 | tf_op jit(solution)/shard_map/ppermute | solution.py:331
  47.3 23.1 %collective-permute-start.6 = (bf16[16,128,256]{2,1,0:T(8,128)(2,1)}, bf16[16,128,256]{2,1,0:T(8,128)(2,1)S(1)}, u32[]{:S(2)}, u32[]{:S(2)}) collective-permute-start(bf16[16,128,256]{2,1,0:T(8,128)(2,1)} %message.3), channel_id=1, source_target_pairs={{0,3},{2,5},{3,0},{4,7},{5,2},{6,9},{7,4},{8,11},{9,6},{10,13},{11... | collective-permute-start | bytes 3145736 | tf_op jit(solution)/shard_map/ppermute | solution.py:333
  55.5 1.6 %copy-start.3 = (f32[2,8,128,256]{3,2,1,0:T(8,128)S(1)}, f32[2,8,128,256]{3,2,1,0:T(8,128)}, u32[]{:S(2)}) copy-start(f32[2,8,128,256]{3,2,1,0:T(8,128)} %copy-done.2) | copy-start | bytes 6291460
  57.1 1.6 %copy-start.5 = (f32[16,128,256]{2,1,0:T(8,128)S(1)}, f32[16,128,256]{2,1,0:T(8,128)}, u32[]{:S(2)}) copy-start(f32[16,128,256]{2,1,0:T(8,128)} %copy-done.4) | copy-start | bytes 6291460
  58.7 11.6 %copy-start.8 = (s32[16]{0:T(128)S(1)}, s32[16]{0:T(128)}, u32[]{:S(2)}) copy-start(s32[16]{0:T(128)} %count_ref.1) | copy-start | bytes 196

commit v2 on v0

v2 whole, which is shorter than its diff:
```python
import jax
import jax.numpy as jnp
from jax import lax
from jax.experimental import pallas as pl
from jax.experimental.pallas import tpu as pltpu
from jax.sharding import PartitionSpec as P

AXES = ("pairs", "aux")
BF16, F32 = jnp.bfloat16, jnp.float32
VMEM, SMEM = pltpu.VMEM, pltpu.SMEM
UNROLL = 4
MIB = 1 << 20


def toward(count, cross, flip):
    pairs = []
    for holder in range(count):
        for core in range(2):
            step = 1 if (core == 0) != flip else -1
            if 0 <= holder + step < count:
                dest = (1 - core) if cross else core
                pairs.append((2 * holder + core, 2 * (holder + step) + dest))
    return pairs


def nt_dot(a, b):
    return lax.dot_general(a, b, (((1,), (1,)), ((), ())), preferred_element_type=F32)


def tn_dot(a, b):
    return lax.dot_general(a, b, (((0,), (0,)), ((), ())), preferred_element_type=F32)


def coupling_kernel(first_ref, rel_ref, w_ref, amp_hbm, mar_hbm, acc_ref,
                    mbuf, abuf, fbuf, items, msem, asem):
    sources, couplings = mar_hbm.shape[0], mar_hbm.shape[1]
    slots, rows = acc_ref.shape[0], acc_ref.shape[1]
    shift = first_ref[0]
    row0 = pl.multiple_of(first_ref[1], rows) if rows < mar_hbm.shape[2] else 0

    def mar_copy(k):
        return pltpu.make_async_copy(
            mar_hbm.at[k // couplings, k % couplings], mbuf.at[k], msem.at[k])

    def amp_copy(q):
        return pltpu.make_async_copy(amp_hbm.at[q], abuf.at[q], asem.at[q])

    def scan(q, n):
        amp_copy(q).start()
        for c in range(couplings):
            k = q * couplings + c
            slot = rel_ref[c, q] - shift
            mine = (slot >= 0) & (slot < slots)
            items[n] = k

            @pl.when(mine)
            def _():
                mar_copy(k).start()

            n = n + mine.astype(jnp.int32)
        return n

    n = lax.fori_loop(0, sources, scan, jnp.int32(0))
    for u in range(UNROLL):
        items[n + u] = items[0]

    @pl.loop(0, slots)
    def _(s):
        acc_ref[s] = jnp.zeros(acc_ref.shape[1:], F32)

    def wait_amp(q, x):
        amp_copy(q).wait()
        return x

    def body(g, waited):
        ks = [items[g * UNROLL + u] for u in range(UNROLL)]
        last = ks[0] // couplings
        for u in range(UNROLL):
            @pl.when(g * UNROLL + u < n)
            def _(u=u):
                mar_copy(ks[u]).wait()

            last = jnp.maximum(last, ks[u] // couplings)

        lax.fori_loop(waited, last + 1, wait_amp, 0)
        for u in range(UNROLL):
            left = mbuf[ks[u], pl.ds(row0, rows), :]
            fbuf[u] = jnp.dot(
                left, abuf[ks[u] // couplings], preferred_element_type=F32).astype(BF16)
        for u in range(UNROLL):
            c, q = ks[u] % couplings, ks[u] // couplings
            weight = jnp.where(g * UNROLL + u < n, w_ref[c, q], 0.0)
            acc_ref[rel_ref[c, q] - shift] += weight * nt_dot(fbuf[u], mbuf[ks[u]])
        return jnp.maximum(waited, last + 1)

    waited = lax.fori_loop(0, pl.cdiv(n, UNROLL), body, jnp.int32(0))
    lax.fori_loop(waited, sources, wait_amp, 0)


def coupling(first, rel, weights, amplitudes, margins, rows):
    pairs, width = amplitudes.shape[0], amplitudes.shape[1]
    total = pairs * margins.shape[1]
    any_spec = pl.BlockSpec(memory_space=pltpu.HBM)
    smem_spec = pl.BlockSpec(memory_space=SMEM)
    return pl.pallas_call(
        coupling_kernel,
        out_shape=jax.ShapeDtypeStruct((pairs, rows, width), F32),
        in_specs=[smem_spec, smem_spec, smem_spec, any_spec, any_spec],
        out_specs=pl.BlockSpec(memory_space=VMEM),
        scratch_shapes=[
            VMEM((total, width, width), BF16),
            VMEM((pairs, width, width), BF16),
            VMEM((UNROLL, rows, width), BF16),
            SMEM((total + UNROLL,), jnp.int32),
            pltpu.SemaphoreType.DMA((total,)),
            pltpu.SemaphoreType.DMA((pairs,)),
        ],
        compiler_params=pltpu.CompilerParams(vmem_limit_bytes=12 * MIB),
        cost_estimate=pl.CostEstimate(
            flops=2 * 22 * rows * 2 * 256 * 256, bytes_accessed=6 * MIB, transcendentals=0),
    )(first, rel, weights,
      pltpu.with_memory_space_constraint(amplitudes, pltpu.HBM),
      pltpu.with_memory_space_constraint(margins, pltpu.HBM))


def whole(kernel, out_shape, n_smem, n_vmem, limit, cost, **extra):
    vmem = pl.BlockSpec(memory_space=VMEM)
    return pl.pallas_call(
        kernel,
        out_shape=out_shape,
        in_specs=[pl.BlockSpec(memory_space=SMEM)] * n_smem + [vmem] * n_vmem,
        out_specs=jax.tree.map(lambda _: vmem, out_shape),
        compiler_params=pltpu.CompilerParams(vmem_limit_bytes=limit * MIB),
        cost_estimate=pl.CostEstimate(flops=cost[0], bytes_accessed=cost[1] * MIB, transcendentals=0),
        **extra,
    )


def message_kernel(half_ref, pick_ref, near_blk, blk, acc_ref, *rest):
    out_refs, prod = rest[:-1], rest[-1]
    rows = prod.shape[1]
    row0 = pl.multiple_of(half_ref[0] * rows, rows)
    for j in range(2):
        for i in range(2):
            prod[2 * j + i] = tn_dot(near_blk[j, :, pl.ds(row0, rows)], blk[i])
    prod[4] = jnp.zeros(prod.shape[1:], F32)
    start = 0
    for out in out_refs:
        @pl.loop(0, out.shape[0])
        def _(s, out=out, start=start):
            out[s] = (acc_ref[start + s, pl.ds(row0, rows), :]
                      + prod[pick_ref[start + s]]).astype(BF16)

        start += out.shape[0]


def message(half, pick, near_blk, blk, acc, chunks):
    width = acc.shape[2]
    rows = width // 2
    return whole(
        message_kernel,
        [jax.ShapeDtypeStruct((n, rows, width), BF16) for n in chunks],
        2, 3, 4, (4 * 2 * 128 * 256 * 1024, 4),
        scratch_shapes=[VMEM((5, rows, width), F32)],
    )(half, pick, near_blk, blk, acc)


def exchange_kernel(core_ref, near_blk, blk, keep_ref, send_ref):
    rows = keep_ref.shape[1]
    for out, side in ((keep_ref, core_ref[0]), (send_ref, 1 - core_ref[0])):
        row0 = pl.multiple_of(side * rows, rows)
        for i in range(2):
            left = blk[i, :, pl.ds(row0, rows)]
            for j in range(2):
                out[2 * i + j] = tn_dot(left, near_blk[j])
                out[4 + 2 * i + j] = tn_dot(left, blk[j])


def exchange(core, near_blk, blk):
    width = blk.shape[2]
    half = jax.ShapeDtypeStruct((8, width // 2, width), F32)
    return whole(
        exchange_kernel, [half, half], 1, 2, 4, (16 * 2 * 128 * 256 * 1024, 4),
    )(core, near_blk, blk)


def base_kernel(core_ref, ix_ref, fkeep, frecv, shift_ref, en_ref, amp_ref, own_ref,
                near_ref, keep_ref, recv_ref, out_ref):
    slots, rows, width = out_ref.shape
    core = core_ref[0]
    row0 = pl.multiple_of(core * rows, rows)

    @pl.loop(0, slots)
    def _(p):
        cols = en_ref[pl.ds(p, 1), :]
        side = jnp.where(core == 0, cols[:, :rows], cols[:, rows:])
        down = jnp.broadcast_to(side, (rows, rows)).T
        down = jnp.concatenate([down] * (width // rows), axis=1)
        denom = down + cols - shift_ref[p]
        value = denom * amp_ref[p, pl.ds(row0, rows), :].astype(F32)
        value += own_ref[p] + near_ref[p].astype(F32)
        value += keep_ref[ix_ref[p]] * fkeep[p]
        value += recv_ref[ix_ref[p]] * frecv[p]
        out_ref[p] = value


def base(core, index, fkeep, frecv, shift, energy, amplitudes, own, near, keep, recv):
    return whole(
        base_kernel, jax.ShapeDtypeStruct(own.shape, F32), 5, 6, 4, (16 * 128 * 256 * 8, 8),
    )(core, index, fkeep, frecv, shift, energy, amplitudes, own, near, keep, recv)


def final_kernel(start, core_ref, count_ref, base_ref, far_ref, *rest):
    out_hbm, buf, sem = rest[-3:]
    slots, rows, width = far_ref.shape
    row = lax.broadcasted_iota(jnp.int32, (rows, width), 0) + core_ref[0] * rows
    col = lax.broadcasted_iota(jnp.int32, (rows, width), 1)
    most = jnp.maximum(row, col)

    def put(s):
        return pltpu.make_async_copy(buf.at[s], out_hbm.at[start + s], sem.at[s])

    @pl.loop(0, slots)
    def _(s):
        value = base_ref[start + s] + far_ref[s].astype(F32)
        buf[s] = jnp.where(most < count_ref[start + s], value, 0.0)
        put(s).start()

    @pl.loop(0, slots)
    def _(s):
        put(s).wait()


def final(start, core, count, base_terms, far, earlier=None):
    slots, rows, width = far.shape
    smem = pl.BlockSpec(memory_space=SMEM)
    vmem = pl.BlockSpec(memory_space=VMEM)
    hbm = pl.BlockSpec(memory_space=pltpu.HBM)
    more = [] if earlier is None else [earlier]

    def kernel(*refs):
        final_kernel(start, *refs)

    return pl.pallas_call(
        kernel,
        out_shape=jax.ShapeDtypeStruct(base_terms.shape, F32),
        in_specs=[smem, smem, vmem, vmem] + [hbm] * len(more),
        out_specs=hbm,
        scratch_shapes=[VMEM((slots, rows, width), F32), pltpu.SemaphoreType.DMA((slots,))],
        input_output_aliases={4: 0} if more else {},
        compiler_params=pltpu.CompilerParams(vmem_limit_bytes=4 * MIB),
        cost_estimate=pl.CostEstimate(
            flops=slots * 128 * 256 * 2, bytes_accessed=slots * MIB // 4, transcendentals=0),
    )(core, count, base_terms, far, *more)


def local(blocks, pair_orbs, pno_count, amplitudes, margins, couple_target, couple_weight,
          pno_energy, occ_energy):
    holder = lax.axis_index("pairs").astype(jnp.int32)
    core = lax.axis_index("aux").astype(jnp.int32)
    holders = lax.axis_size("pairs")
    pairs, width = amplitudes.shape[0], amplitudes.shape[1]
    orbs = blocks.shape[0]
    straight_in = toward(holders, False, True)
    straight_out = toward(holders, False, False)
    cross_out = toward(holders, True, False)
    swap = [(2 * h + c, 2 * h + 1 - c) for h in range(holders) for c in range(2)]

    near_blk = lax.ppermute(blocks, AXES, straight_in)
    near_orbs = lax.ppermute(pair_orbs, AXES, straight_in)

    core1 = core.reshape(1)
    rel = lax.dynamic_slice_in_dim(couple_target, holder * pairs, pairs, 0).T - holder * pairs
    weights = lax.dynamic_slice_in_dim(couple_weight, holder * pairs, pairs, 0).T
    step = 1 - 2 * core
    toward_first = jnp.stack([step * pairs, jnp.int32(0)])
    msg_acc = coupling(toward_first, rel, weights, amplitudes, margins, width)

    first = jnp.clip(near_orbs[:, 0] - (holder + step) * orbs, 0, orbs - 1)
    second = near_orbs[:, 1] - holder * orbs
    pick = jnp.where((second >= 0) & (second < orbs), orbs * first + second, 4)
    chunks = [pairs * 3 // 4, pairs - pairs * 3 // 4]
    msg_near, = message(core1, pick, near_blk, blocks, msg_acc, [pairs])
    near = lax.ppermute(msg_near, AXES, straight_out)
    msg_far = message(1 - core1, pick, near_blk, blocks, msg_acc, chunks)
    far = lax.ppermute(msg_far[0], AXES, cross_out)
    last = lax.ppermute(msg_far[1], AXES, cross_out)

    keep, send = exchange(core1, near_blk, blocks)
    recv = lax.ppermute(send, AXES, swap)
    own_first = jnp.stack([jnp.int32(0), core * (width // 2)])
    own = coupling(own_first, rel, weights, amplitudes, margins, width // 2)

    j_all = pair_orbs[:, 1]
    side = j_all // orbs - holder
    index = orbs * (pair_orbs[:, 0] - holder * orbs) + j_all % orbs
    index = jnp.where(side == 0, index + 4, index)
    fkeep = ((side == 0) | (side == step)).astype(F32)
    frecv = ((side == 0) | (side == -step)).astype(F32)
    orbital = jnp.arange(occ_energy.shape[0], dtype=jnp.int32)
    shift = jnp.sum(
        jnp.where(pair_orbs[:, 0:1] == orbital, occ_energy, 0.0)
        + jnp.where(pair_orbs[:, 1:2] == orbital, occ_energy, 0.0), axis=1)
    base_terms = base(core1, index, fkeep, frecv, shift, pno_energy, amplitudes, own, near,
                      keep, recv)
    out = final(0, core1, pno_count, base_terms, far)
    return final(chunks[0], core1, pno_count, base_terms, last, out)


def solution(mesh):
    placed = (
        P("pairs", "aux", None),
        P("pairs", None),
        P("pairs"),
        P("pairs", None, None),
        P("pairs", None, None, None),
        P(),
        P(),
        P("pairs", None),
        P(),
    )

    return jax.shard_map(
        local, mesh=mesh, in_specs=placed, out_specs=P("pairs", "aux", None), check_vma=False
    )
```

time: 113 us -> 66.1 us (0.58)
  the two profiles are of different devices: /device:TPU:24 before, /device:TPU:25 now
where the time goes in v2:
time: 66.1 us; the launch traced here: 65.7 us
  starting transfers between devices  26.7 us (40%)
  Pallas kernels  23.5 us (36%)
  local copies, waits for them, and re-layouts  7.44 us (11%)
  waiting for transfers between devices  6.72 us (10%)
  other arithmetic  1.14 us (2%)
    pallas_call x2, Pallas kernels, coupling(): pl.pallas_call(coupling_kernel, out_shape=jax.ShapeDtypeStruct((pairs, ro...  11.1 us
    ppermute x1, starting transfers between devices, local(): near = lax.ppermute(msg_near, AXES, straight_out)  8.28 us
    ppermute x1, starting transfers between devices, local(): last = lax.ppermute(msg_far[1], AXES, cross_out)  8.12 us
    unnamed x24, local copies, waits for them, and re-layouts  7.37 us
    ppermute x1, waiting for transfers between devices, local(): near_orbs = lax.ppermute(pair_orbs, AXES, straight_in)  6.7 us
    ppermute x1, starting transfers between devices, local(): near_blk = lax.ppermute(blocks, AXES, straight_in)  3.67 us
    ppermute x1, starting transfers between devices, local(): near_orbs = lax.ppermute(pair_orbs, AXES, straight_in)  3.55 us
    pallas_call x2, Pallas kernels, message(): whole(message_kernel, [jax.ShapeDtypeStruct((n, rows, width), BF16) for n...  3.49 us
  transfers between devices with their start and end apart: 6, of which 1 were waited for; matrix products, arithmetic and copies ran while one was open for 2% of the time, Pallas kernels for 30%

profile of v2, /device:TPU:25, one launch (start us, length us, event | category | flops | bytes accessed | tf_op | source)
XLA Modules:
  0.0 65.7 jit_solution(5366088747722165269)
XLA Ops:
  0.0 0.0 copy-start
  0.0 3.7 %collective-permute-start.1 = (bf16[2,1024,256]{2,1,0:T(8,128)(2,1)}, bf16[2,1024,256]{2,1,0:T(8,128)(2,1)S(1)}, u32[]{:S(2)}, u32[]{:S(2)}) collective-permute-start(bf16[2,1024,256]{2,1,0:T(8,128)(2,1)} %blk.5), channel_id=1, source_target_pairs={{1,3},{2,0},{3,5},{4,2},{5,7},{6,4},{7,9},{8,6},{9,11},{10,8},{11,... | collective-permute-start | bytes 3145736 | tf_op jit(solution)/shard_map/ppermute | solution.py:269
  3.7 3.5 %collective-permute-start = (s32[16,2]{0,1:T(2,128)}, s32[16,2]{0,1:T(2,128)S(1)}, u32[]{:S(2)}, u32[]{:S(2)}) collective-permute-start(s32[16,2]{0,1:T(2,128)} %param.10), channel_id=1, source_target_pairs={{1,3},{2,0},{3,5},{4,2},{5,7},{6,4},{7,9},{8,6},{9,11},{10,8},{11,... | collective-permute-start | bytes 392 | tf_op jit(solution)/shard_map/ppermute | solution.py:270
  7.2 0.1 pad_add_fusion.1.first_ref
  7.3 0.8 %subtract_bitcast_fusion.rel_ref = s32[4,16]{1,0:T(4,128)S(1)} fusion(s32[2048,4]{0,1:T(4,128)} %param.14, s32[]{:T(128)S(6)} %select_n.35, s32[]{:T(128)S(6)} %mul.32), kind=kLoop, calls=%fused_computation.4 | loop fusion | flops 64 | bytes 520 | tf_op jit(solution)/shard_map/sub | solution.py:273
  8.1 0.0 copy-done
  8.1 0.1 dynamic-slice_bitcast_fusion.w_ref
  8.1 0.0 copy-start.5
  8.2 5.6 %shard_map.92.acc_ref = f32[16,256,256]{2,1,0:T(8,128)S(1)} custom-call(s32[2]{0:T(128)S(1)} %pad_add_fusion.1.first_ref, s32[4,16]{1,0:T(4,128)S(1)} %subtract_bitcast_fusion.rel_ref, f32[4,16]{1,0:T(4,128)S(1)} %dynamic-slice_bitcast_fusion.w_ref, bf16[16,256,256]{2,1,0:T(8,128)(2,1)} %amp_ref.1, bf16[16,4,256,256]{3,2,1,0:T(8,128)(2,1)} %mar_hbm.3), custom_call_target="tpu_custom_call" | custom-call | flops 1476395008 | bytes 6291456 | tf_op jit(solution)/shard_map/pallas_call | solution.py:105
  13.8 0.0 copy-start.1
  13.8 1.9 %copy-done.1 = f32[16,256,256]{2,1,0:T(8,128)} copy-done((f32[16,256,256]{2,1,0:T(8,128)}, f32[16,256,256]{2,1,0:T(8,128)S(1)}, u32[]{:S(2)}) %copy-start.1) | copy-done | bytes 4194328
  15.7 6.7 %collective-permute-done = s32[16,2]{0,1:T(2,128)S(1)} collective-permute-done((s32[16,2]{0,1:T(2,128)}, s32[16,2]{0,1:T(2,128)S(1)}, u32[]{:S(2)}, u32[]{:S(2)}) %collective-permute-start) | collective-permute-done | bytes 160 | tf_op jit(solution)/shard_map/ppermute | solution.py:270
  22.4 0.0 collective-permute-done.1.near_blk
  22.5 0.0 copy-done.5
  22.5 2.3 %shard_map.94 = (f32[8,128,256]{2,1,0:T(8,128)S(1)}, f32[8,128,256]{2,1,0:T(8,128)}) custom-call(s32[1]{0:T(128)} %bitcast.half_ref.core_ref.refs_0_, bf16[2,1024,256]{2,1,0:T(8,128)(2,1)S(1)} %collective-permute-done.1.near_blk, bf16[2,1024,256]{2,1,0:T(8,128)(2,1)S(1)} %copy-done.5), custom_call_target="tpu_custom_call" | custom-call | flops 1073741824 | bytes 4194304 | tf_op jit(solution)/shard_map/pallas_call | solution.py:182
  24.7 0.0 copy-start.6
  24.7 1.0 %copy-done.6 = f32[8,128,256]{2,1,0:T(8,128)} copy-done((f32[8,128,256]{2,1,0:T(8,128)}, f32[8,128,256]{2,1,0:T(8,128)S(1)}, u32[]{:S(2)}) %copy-start.6) | copy-done | bytes 1048600
  25.7 1.1 %collective-permute-start.3 = (f32[8,128,256]{2,1,0:T(8,128)}, f32[8,128,256]{2,1,0:T(8,128)}, u32[]{:S(2)}, u32[]{:S(2)}) collective-permute-start(f32[8,128,256]{2,1,0:T(8,128)} %get-tuple-element.10), channel_id=1, source_target_pairs={{0,1},{1,0},{2,3},{3,2},{4,5},{5,4},{6,7},{7,6},{8,9},{9,8},{10,11... | collective-permute-start | bytes 3145736 | tf_op jit(solution)/shard_map/ppermute | solution.py:290
  26.9 0.0 copy-start.2
  26.9 2.2 %copy-done.2 = f32[16,256,256]{2,1,0:T(8,128)S(1)} copy-done((f32[16,256,256]{2,1,0:T(8,128)S(1)}, f32[16,256,256]{2,1,0:T(8,128)}, u32[]{:S(2)}) %copy-start.2) | copy-done | bytes 4194328
  29.1 0.0 copy-start.10
  29.1 0.0 copy-start.11
  29.1 1.3 %shard_map.93 = bf16[16,128,256]{2,1,0:T(8,128)(2,1)S(1)} custom-call(s32[1]{0:T(128)} %bitcast.half_ref.core_ref.refs_0_, s32[16]{0:T(128)S(1)} %fusion.1.pick_ref, bf16[2,1024,256]{2,1,0:T(8,128)(2,1)S(1)} %collective-permute-done.1.near_blk, bf16[2,1024,256]{2,1,0:T(8,128)(2,1)S(1)} %copy-done.5, f32[16,256,256]{2,1,0:T(8,128)S(1)} %copy-done.2), custom_call_target="tpu_custom_call" | custom-call | flops 268435456 | bytes 4194304 | tf_op jit(solution)/shard_map/pallas_call | solution.py:160
  30.4 8.3 %collective-permute-start.2 = (bf16[16,128,256]{2,1,0:T(8,128)(2,1)S(1)}, bf16[16,128,256]{2,1,0:T(8,128)(2,1)}, u32[]{:S(2)}, u32[]{:S(2)}) collective-permute-start(bf16[16,128,256]{2,1,0:T(8,128)(2,1)S(1)} %shard_map.93), channel_id=1, source_target_pairs={{0,2},{2,4},{3,1},{4,6},{5,3},{6,8},{7,5},{8,10},{9,7},{10,12},{11... | collective-permute-start | bytes 3145736 | tf_op jit(solution)/shard_map/ppermute | solution.py:284
  38.7 0.0 copy-done.10
  38.7 0.0 copy-done.11
  38.7 0.2 add_reduce_fusion.shift_ref
  38.9 0.0 copy-start.3
  38.9 2.2 %copy-done.3 = f32[16,256,256]{2,1,0:T(8,128)S(1)} copy-done((f32[16,256,256]{2,1,0:T(8,128)S(1)}, f32[16,256,256]{2,1,0:T(8,128)}, u32[]{:S(2)}) %copy-start.3) | copy-done | bytes 4194328
  41.1 2.2 %shard_map.96 = (bf16[12,128,256]{2,1,0:T(8,128)(2,1)}, bf16[4,128,256]{2,1,0:T(8,128)(2,1)S(1)}) custom-call(s32[1]{0:T(128)S(6)} %sub.57.half_ref, s32[16]{0:T(128)S(1)} %fusion.1.pick_ref, bf16[2,1024,256]{2,1,0:T(8,128)(2,1)S(1)} %collective-permute-done.1.near_blk, bf16[2,1024,256]{2,1,0:T(8,128)(2,1)S(1)} %copy-done.5, f32[16,256,256]{2,1,0:T(8,128)S(1)} %copy-done.3), custom_call_target="tpu_custom_call" | custom-call | flops 268435456 | bytes 4194304 | tf_op jit(solution)/shard_map/pallas_call | solution.py:160
  43.3 1.9 %collective-permute-start.5 = (bf16[12,128,256]{2,1,0:T(8,128)(2,1)}, bf16[12,128,256]{2,1,0:T(8,128)(2,1)S(1)}, u32[]{:S(2)}, u32[]{:S(2)}) collective-permute-start(bf16[12,128,256]{2,1,0:T(8,128)(2,1)} %get-tuple-element.12), channel_id=1, source_target_pairs={{0,3},{2,5},{3,0},{4,7},{5,2},{6,9},{7,4},{8,11},{9,6},{10,13},{11... | collective-permute-start | bytes 2359304 | tf_op jit(solution)/shard_map/ppermute | solution.py:286
  45.2 0.1 pad_add_fusion.first_ref
  45.3 0.0 copy-start.4
  45.3 0.0 copy-start.7
  45.3 0.0 copy-start.8
  45.3 8.1 %collective-permute-start.4 = (bf16[4,128,256]{2,1,0:T(8,128)(2,1)S(1)}, bf16[4,128,256]{2,1,0:T(8,128)(2,1)S(1)}, u32[]{:S(2)}, u32[]{:S(2)}) collective-permute-start(bf16[4,128,256]{2,1,0:T(8,128)(2,1)S(1)} %get-tuple-element.11), channel_id=1, source_target_pairs={{0,3},{2,5},{3,0},{4,7},{5,2},{6,9},{7,4},{8,11},{9,6},{10,13},{11... | collective-permute-start | bytes 786440 | tf_op jit(solution)/shard_map/ppermute | solution.py:287
  53.4 5.5 %shard_map.91.own_ref = f32[16,128,256]{2,1,0:T(8,128)S(1)} custom-call(s32[2]{0:T(128)S(1)} %pad_add_fusion.first_ref, s32[4,16]{1,0:T(4,128)S(1)} %subtract_bitcast_fusion.rel_ref, f32[4,16]{1,0:T(4,128)S(1)} %dynamic-slice_bitcast_fusion.w_ref, bf16[16,256,256]{2,1,0:T(8,128)(2,1)} %amp_ref.1, bf16[16,4,256,256]{3,2,1,0:T(8,128)(2,1)} %mar_hbm.3), custom_call_target="tpu_custom_call" | custom-call | flops 738197504 | bytes 6291456 | tf_op jit(solution)/shard_map/pallas_call | solution.py:105
  59.0 0.0 collective-permute-done.3.recv_ref
  59.0 0.0 collective-permute-done.2.near_ref
  59.0 0.0 copy-done.4
  59.0 0.0 copy-done.7
  59.0 0.0 copy-done.8
  59.0 0.0 copy-start.9
  59.1 3.4 %shard_map.95.refs_2_ = f32[16,128,256]{2,1,0:T(8,128)S(1)} custom-call(s32[1]{0:T(128)} %bitcast.half_ref.core_ref.refs_0_, s32[16]{0:T(128)S(1)} %add_select_fusion.ix_ref, f32[16]{0:T(128)S(1)} %or_convert_fusion.1.fkeep, f32[16]{0:T(128)S(1)} %get-tuple-element.13.frecv, f32[16]{0:T(128)S(1)} %add_reduce_fusion.shift_ref, f32[16,256]{1,0:T(8,128)S(1)} %copy-done.8, ...), custom_call_target="tpu_custom_call" | custom-call | flops 4194304 | bytes 8388608 | tf_op jit(solution)/shard_map/pallas_call | solution.py:208
  62.5 0.0 collective-permute-done.5.refs_3_
  62.5 0.0 copy-done.9
  62.5 1.8 %shard_map.97.refs_4_ = f32[16,128,256]{2,1,0:T(8,128)} custom-call(s32[1]{0:T(128)} %bitcast.half_ref.core_ref.refs_0_, s32[16]{0:T(128)S(1)} %copy-done.9, f32[16,128,256]{2,1,0:T(8,128)S(1)} %shard_map.95.refs_2_, bf16[12,128,256]{2,1,0:T(8,128)(2,1)S(1)} %collective-permute-done.5.refs_3_), custom_call_target="tpu_custom_call" | custom-call | flops 786432 | bytes 3145728 | tf_op jit(solution)/shard_map/pallas_call | solution.py:244
  64.3 0.0 collective-permute-done.4.refs_3_
  64.3 1.4 %shard_map.98 = f32[16,128,256]{2,1,0:T(8,128)} custom-call(s32[1]{0:T(128)} %bitcast.half_ref.core_ref.refs_0_, s32[16]{0:T(128)S(1)} %copy-done.9, f32[16,128,256]{2,1,0:T(8,128)S(1)} %shard_map.95.refs_2_, bf16[4,128,256]{2,1,0:T(8,128)(2,1)S(1)} %collective-permute-done.4.refs_3_, f32[16,128,256]{2,1,0:T(8,128)} %shard_map.97.refs_4_), custom_call_target="tpu_custom_call", output_to_operand_aliasing={{}: (4, {})} | custom-call | flops 262144 | bytes 1048576 | tf_op jit(solution)/shard_map/pallas_call | solution.py:244
  (5 shorter events, 0.0 us)
Async XLA Ops:
  0.0 8.1 %copy-start = (f32[2048,4]{0,1:T(4,128)S(1)}, f32[2048,4]{0,1:T(4,128)}, u32[]{:S(2)}) copy-start(f32[2048,4]{0,1:T(4,128)} %param.15) | copy-start | bytes 98308
  0.0 22.4 %collective-permute-start.1 = (bf16[2,1024,256]{2,1,0:T(8,128)(2,1)}, bf16[2,1024,256]{2,1,0:T(8,128)(2,1)S(1)}, u32[]{:S(2)}, u32[]{:S(2)}) collective-permute-start(bf16[2,1024,256]{2,1,0:T(8,128)(2,1)} %blk.5), channel_id=1, source_target_pairs={{1,3},{2,0},{3,5},{4,2},{5,7},{6,4},{7,9},{8,6},{9,11},{10,8},{11,... | collective-permute-start | bytes 3145736 | tf_op jit(solution)/shard_map/ppermute | solution.py:269
  3.7 18.8 %collective-permute-start = (s32[16,2]{0,1:T(2,128)}, s32[16,2]{0,1:T(2,128)S(1)}, u32[]{:S(2)}, u32[]{:S(2)}) collective-permute-start(s32[16,2]{0,1:T(2,128)} %param.10), channel_id=1, source_target_pairs={{1,3},{2,0},{3,5},{4,2},{5,7},{6,4},{7,9},{8,6},{9,11},{10,8},{11,... | collective-permute-start | bytes 392 | tf_op jit(solution)/shard_map/ppermute | solution.py:270
  8.1 14.3 %copy-start.5 = (bf16[2,1024,256]{2,1,0:T(8,128)(2,1)S(1)}, bf16[2,1024,256]{2,1,0:T(8,128)(2,1)}, u32[]{:S(2)}) copy-start(bf16[2,1024,256]{2,1,0:T(8,128)(2,1)} %blk.5) | copy-start | bytes 3145732
  13.8 2.0 %copy-start.1 = (f32[16,256,256]{2,1,0:T(8,128)}, f32[16,256,256]{2,1,0:T(8,128)S(1)}, u32[]{:S(2)}) copy-start(f32[16,256,256]{2,1,0:T(8,128)S(1)} %shard_map.92.acc_ref) | copy-start | bytes 12582916
  24.7 1.0 %copy-start.6 = (f32[8,128,256]{2,1,0:T(8,128)}, f32[8,128,256]{2,1,0:T(8,128)S(1)}, u32[]{:S(2)}) copy-start(f32[8,128,256]{2,1,0:T(8,128)S(1)} %get-tuple-element.9.keep_ref) | copy-start | bytes 3145732
  25.7 33.3 %collective-permute-start.3 = (f32[8,128,256]{2,1,0:T(8,128)}, f32[8,128,256]{2,1,0:T(8,128)}, u32[]{:S(2)}, u32[]{:S(2)}) collective-permute-start(f32[8,128,256]{2,1,0:T(8,128)} %get-tuple-element.10), channel_id=1, source_target_pairs={{0,1},{1,0},{2,3},{3,2},{4,5},{5,4},{6,7},{7,6},{8,9},{9,8},{10,11... | collective-permute-start | bytes 3145736 | tf_op jit(solution)/shard_map/ppermute | solution.py:290
  26.9 2.2 %copy-start.2 = (f32[16,256,256]{2,1,0:T(8,128)S(1)}, f32[16,256,256]{2,1,0:T(8,128)}, u32[]{:S(2)}) copy-start(f32[16,256,256]{2,1,0:T(8,128)} %copy-done.1) | copy-start | bytes 12582916
  29.1 9.6 %copy-start.10 = (s32[16,2]{0,1:T(2,128)S(1)}, s32[16,2]{0,1:T(2,128)}, u32[]{:S(2)}) copy-start(s32[16,2]{0,1:T(2,128)} %param.10) | copy-start | bytes 388
  29.1 9.6 %copy-start.11 = (f32[256]{0:T(256)S(1)}, f32[256]{0:T(256)}, u32[]{:S(2)}) copy-start(f32[256]{0:T(256)} %param.17) | copy-start | bytes 3076
  30.4 28.6 %collective-permute-start.2 = (bf16[16,128,256]{2,1,0:T(8,128)(2,1)S(1)}, bf16[16,128,256]{2,1,0:T(8,128)(2,1)}, u32[]{:S(2)}, u32[]{:S(2)}) collective-permute-start(bf16[16,128,256]{2,1,0:T(8,128)(2,1)S(1)} %shard_map.93), channel_id=1, source_target_pairs={{0,2},{2,4},{3,1},{4,6},{5,3},{6,8},{7,5},{8,10},{9,7},{10,12},{11... | collective-permute-start | bytes 3145736 | tf_op jit(solution)/shard_map/ppermute | solution.py:284
  38.9 2.2 %copy-start.3 = (f32[16,256,256]{2,1,0:T(8,128)S(1)}, f32[16,256,256]{2,1,0:T(8,128)}, u32[]{:S(2)}) copy-start(f32[16,256,256]{2,1,0:T(8,128)} %copy-done.1) | copy-start | bytes 12582916
  43.3 19.2 %collective-permute-start.5 = (bf16[12,128,256]{2,1,0:T(8,128)(2,1)}, bf16[12,128,256]{2,1,0:T(8,128)(2,1)S(1)}, u32[]{:S(2)}, u32[]{:S(2)}) collective-permute-start(bf16[12,128,256]{2,1,0:T(8,128)(2,1)} %get-tuple-element.12), channel_id=1, source_target_pairs={{0,3},{2,5},{3,0},{4,7},{5,2},{6,9},{7,4},{8,11},{9,6},{10,13},{11... | collective-permute-start | bytes 2359304 | tf_op jit(solution)/shard_map/ppermute | solution.py:286
  45.3 13.7 %copy-start.4 = (bf16[16,256,256]{2,1,0:T(8,128)(2,1)S(1)}, bf16[16,256,256]{2,1,0:T(8,128)(2,1)}, u32[]{:S(2)}) copy-start(bf16[16,256,256]{2,1,0:T(8,128)(2,1)} %amp_ref.1) | copy-start | bytes 6291460
  45.3 13.7 %copy-start.7 = (f32[8,128,256]{2,1,0:T(8,128)S(1)}, f32[8,128,256]{2,1,0:T(8,128)}, u32[]{:S(2)}) copy-start(f32[8,128,256]{2,1,0:T(8,128)} %copy-done.6) | copy-start | bytes 3145732
  45.3 13.7 %copy-start.8 = (f32[16,256]{1,0:T(8,128)S(1)}, f32[16,256]{1,0:T(8,128)}, u32[]{:S(2)}) copy-start(f32[16,256]{1,0:T(8,128)} %en_ref.1) | copy-start | bytes 49156
  45.3 19.0 %collective-permute-start.4 = (bf16[4,128,256]{2,1,0:T(8,128)(2,1)S(1)}, bf16[4,128,256]{2,1,0:T(8,128)(2,1)S(1)}, u32[]{:S(2)}, u32[]{:S(2)}) collective-permute-start(bf16[4,128,256]{2,1,0:T(8,128)(2,1)S(1)} %get-tuple-element.11), channel_id=1, source_target_pairs={{0,3},{2,5},{3,0},{4,7},{5,2},{6,9},{7,4},{8,11},{9,6},{10,13},{11... | collective-permute-start | bytes 786440 | tf_op jit(solution)/shard_map/ppermute | solution.py:287
  59.0 3.5 %copy-start.9 = (s32[16]{0:T(128)S(1)}, s32[16]{0:T(128)}, u32[]{:S(2)}) copy-start(s32[16]{0:T(128)} %refs_1_.3) | copy-start | bytes 196

commit v3 on v2

v3 whole, which is shorter than its diff:
```python
import functools

import jax
import jax.numpy as jnp
from jax import lax
from jax.experimental import pallas as pl
from jax.experimental.pallas import tpu as pltpu
from jax.sharding import PartitionSpec as P

AXES = ("pairs", "aux")
BF16, F32 = jnp.bfloat16, jnp.float32
VMEM, SMEM = pltpu.VMEM, pltpu.SMEM
UNROLL = 4
MIB = 1 << 20


def toward(count, cross, flip):
    pairs = []
    for holder in range(count):
        for core in range(2):
            step = 1 if (core == 0) != flip else -1
            if 0 <= holder + step < count:
                dest = (1 - core) if cross else core
                pairs.append((2 * holder + core, 2 * (holder + step) + dest))
    return pairs


def nt_dot(a, b):
    return lax.dot_general(a, b, (((1,), (1,)), ((), ())), preferred_element_type=F32)


def tn_dot(a, b):
    return lax.dot_general(a, b, (((0,), (0,)), ((), ())), preferred_element_type=F32)


def coupling_kernel(early, meta_ref, rel_ref, w_ref, amp_hbm, mar_hbm, acc_ref, *rest):
    (far_ref, early_ref), rest = (rest[:2], rest[2:]) if early else ((None, None), rest)
    mbuf, fbuf, items, msem = rest[:4]
    abuf, asem = rest[4:] if early else (amp_hbm, None)
    sources, couplings = mar_hbm.shape[0], mar_hbm.shape[1]
    slots, rows = acc_ref.shape[0], acc_ref.shape[1]
    core = meta_ref[1]
    shift = (1 - 2 * core) * slots if early else 0
    row0 = pl.multiple_of(core * rows, rows)
    far0 = pl.multiple_of(rows - core * rows, rows)

    def mar_copy(k):
        return pltpu.make_async_copy(
            mar_hbm.at[k // couplings, k % couplings], mbuf.at[k], msem.at[k])

    def amp_copy(q):
        return pltpu.make_async_copy(amp_hbm.at[q], abuf.at[q], asem.at[q])

    def scan(q, n):
        if early:
            amp_copy(q).start()
        for c in range(couplings):
            k = q * couplings + c
            slot = rel_ref[c, q] - shift
            mine = (slot >= 0) & (slot < slots)
            items[n] = k

            @pl.when(mine)
            def _():
                mar_copy(k).start()

            n = n + mine.astype(jnp.int32)
        return n

    n = lax.fori_loop(0, sources, scan, jnp.int32(0))
    for u in range(UNROLL):
        items[n + u] = items[0]

    @pl.loop(0, slots)
    def _(s):
        acc_ref[s] = jnp.zeros(acc_ref.shape[1:], F32)
        if early:
            far_ref[s] = jnp.zeros(acc_ref.shape[1:], F32)

    def wait_amp(q, x):
        amp_copy(q).wait()
        return x

    def body(g, waited):
        ks = [items[g * UNROLL + u] for u in range(UNROLL)]
        last = ks[0] // couplings
        for u in range(UNROLL):
            @pl.when(g * UNROLL + u < n)
            def _(u=u):
                mar_copy(ks[u]).wait()

            last = jnp.maximum(last, ks[u] // couplings)

        if early:
            lax.fori_loop(waited, last + 1, wait_amp, 0)
        for u in range(UNROLL):
            left = mbuf[ks[u], pl.ds(row0, rows), :]
            if early:
                left = jnp.concatenate([left, mbuf[ks[u], pl.ds(far0, rows), :]], axis=0)
            fbuf[u] = jnp.dot(
                left, abuf[ks[u] // couplings], preferred_element_type=F32).astype(BF16)
        for u in range(UNROLL):
            c, q = ks[u] % couplings, ks[u] // couplings
            weight = jnp.where(g * UNROLL + u < n, w_ref[c, q], 0.0)
            term = weight * nt_dot(fbuf[u], mbuf[ks[u]])
            acc_ref[rel_ref[c, q] - shift] += term[:rows]
            if early:
                far_ref[rel_ref[c, q] - shift] += term[rows:]
        return jnp.maximum(waited, last + 1)

    waited = lax.fori_loop(0, pl.cdiv(n, UNROLL), body, jnp.int32(0))
    if early:
        lax.fori_loop(waited, sources, wait_amp, 0)

        @pl.loop(0, slots)
        def _(s):
            early_ref[s] = acc_ref[s, :early].astype(BF16)


def coupling(meta, rel, weights, amplitudes, margins, rows, early):
    pairs, width = amplitudes.shape[0], amplitudes.shape[1]
    total = pairs * margins.shape[1]
    hbm = pl.BlockSpec(memory_space=pltpu.HBM)
    vmem = pl.BlockSpec(memory_space=VMEM)
    smem = pl.BlockSpec(memory_space=SMEM)
    out_shape = [jax.ShapeDtypeStruct((pairs, rows, width), F32)]
    scratch = [
        VMEM((total, width, width), BF16),
        VMEM((UNROLL, 2 * rows if early else rows, width), BF16),
        SMEM((total + UNROLL,), jnp.int32),
        pltpu.SemaphoreType.DMA((total,)),
    ]
    if early:
        amplitudes = pltpu.with_memory_space_constraint(amplitudes, pltpu.HBM)
        out_shape += [out_shape[0], jax.ShapeDtypeStruct((pairs, early, width), BF16)]
        scratch += [VMEM((pairs, width, width), BF16), pltpu.SemaphoreType.DMA((pairs,))]
    return pl.pallas_call(
        functools.partial(coupling_kernel, early),
        out_shape=out_shape,
        in_specs=[smem, smem, smem, hbm if early else vmem, hbm],
        out_specs=[vmem] * len(out_shape),
        scratch_shapes=scratch,
        compiler_params=pltpu.CompilerParams(vmem_limit_bytes=12 * MIB),
        cost_estimate=pl.CostEstimate(
            flops=2 * 22 * 2 * rows * 256 * 256, bytes_accessed=6 * MIB, transcendentals=0),
    )(meta, rel, weights, amplitudes, pltpu.with_memory_space_constraint(margins, pltpu.HBM))


def whole(kernel, out_shape, n_smem, n_vmem, limit, cost, **extra):
    vmem = pl.BlockSpec(memory_space=VMEM)
    return pl.pallas_call(
        kernel,
        out_shape=out_shape,
        in_specs=[pl.BlockSpec(memory_space=SMEM)] * n_smem + [vmem] * n_vmem,
        out_specs=jax.tree.map(lambda _: vmem, out_shape),
        compiler_params=pltpu.CompilerParams(vmem_limit_bytes=limit * MIB),
        cost_estimate=pl.CostEstimate(flops=cost[0], bytes_accessed=cost[1] * MIB, transcendentals=0),
        **extra,
    )


def products(far, near_blk, blk, meta_ref, prod):
    rows = prod.shape[1]
    core = meta_ref[1]
    row0 = pl.multiple_of((1 - core if far else core) * rows, rows)
    for j in range(2):
        for i in range(2):
            prod[2 * j + i] = tn_dot(near_blk[j, :, pl.ds(row0, rows)], blk[i])
    prod[4] = jnp.zeros(prod.shape[1:], F32)


def pick(meta_ref, orbs_ref, s):
    second = orbs_ref[1, s] - 2 * meta_ref[0]
    mine = (second >= 0) & (second < 2)
    return jnp.where(mine, 2 * (orbs_ref[0, s] % 2) + second, 4)


def near_kernel(meta_ref, orbs_ref, near_blk, blk, acc_ref, out, prod):
    products(False, near_blk, blk, meta_ref, prod)
    slots, early = acc_ref.shape[0], prod.shape[1] - out.shape[1]

    @pl.loop(0, slots)
    def _(s):
        out[s] = (acc_ref[s, early:] + prod[pick(meta_ref, orbs_ref, s), early:]).astype(BF16)

    for k in range(4):
        out[slots + k] = prod[k, :early].astype(BF16)


def far_kernel(meta_ref, orbs_ref, near_blk, blk, acc_ref, *rest):
    out_refs, prod = rest[:-1], rest[-1]
    products(True, near_blk, blk, meta_ref, prod)
    start = 0
    for out in out_refs:
        @pl.loop(0, out.shape[0])
        def _(s, out=out, start=start):
            out[s] = (acc_ref[start + s]
                      + prod[pick(meta_ref, orbs_ref, start + s)]).astype(BF16)

        start += out.shape[0]


def message(kernel, meta, orbs, near_blk, blk, acc, outs):
    width = acc.shape[2]
    return whole(
        kernel,
        [jax.ShapeDtypeStruct((*n, width), BF16) for n in outs],
        2, 3, 4, (4 * 2 * 128 * 256 * 1024, 4),
        scratch_shapes=[VMEM((5, width // 2, width), F32)],
    )(meta, orbs, near_blk, blk, acc)


def exchange_kernel(meta_ref, near_blk, blk, keep_ref, send_ref):
    rows = keep_ref.shape[1]
    for out, side in ((keep_ref, meta_ref[1]), (send_ref, 1 - meta_ref[1])):
        row0 = pl.multiple_of(side * rows, rows)
        for i in range(2):
            left = blk[i, :, pl.ds(row0, rows)]
            for j in range(2):
                out[2 * i + j] = tn_dot(left, near_blk[j])
                out[4 + 2 * i + j] = tn_dot(left, blk[j])


def exchange(meta, near_blk, blk):
    width = blk.shape[2]
    half = jax.ShapeDtypeStruct((8, width // 2, width), F32)
    return whole(
        exchange_kernel, [half, half], 1, 2, 4, (16 * 2 * 128 * 256 * 1024, 4),
    )(meta, near_blk, blk)


def base_kernel(meta_ref, orbs_ref, occ_ref, en_ref, amp_ref, own_ref,
                early_ref, near_ref, keep_ref, recv_ref, out_ref):
    slots, rows, width = out_ref.shape
    early = early_ref.shape[1]
    holder, core = meta_ref[0], meta_ref[1]
    row0 = pl.multiple_of(core * rows, rows)

    @pl.loop(0, slots)
    def _(p):
        first, second = orbs_ref[0, p], orbs_ref[1, p]
        side = second // 2 - holder
        step = 1 - 2 * core
        index = 2 * (first % 2) + second % 2
        both = index + jnp.where(side == 0, 4, 0)
        cols = en_ref[pl.ds(p, 1), :]
        mine = jnp.where(core == 0, cols[:, :rows], cols[:, rows:])
        down = jnp.broadcast_to(mine, (rows, rows)).T
        down = jnp.concatenate([down] * (width // rows), axis=1)
        denom = down + cols - (occ_ref[first] + occ_ref[second])
        value = denom * amp_ref[p, pl.ds(row0, rows), :].astype(F32)
        value += own_ref[p]
        value += keep_ref[both] * jnp.where(side == -step, 0.0, 1.0)
        value += recv_ref[both] * jnp.where(side == step, 0.0, 1.0)
        lacking = near_ref[slots + index].astype(F32) * jnp.where(side == -step, 1.0, 0.0)
        out_ref[p, :early] = value[:early] + early_ref[p].astype(F32) + lacking
        out_ref[p, early:] = value[early:] + near_ref[p].astype(F32)


def base(meta, orbs, occ, energy, amplitudes, own, early, near, keep, recv):
    return whole(
        base_kernel, jax.ShapeDtypeStruct(own.shape, F32), 3, 7, 4, (16 * 128 * 256 * 8, 8),
    )(meta, orbs, occ, energy, amplitudes, own, early, near, keep, recv)


def final_kernel(start, meta_ref, count_ref, base_ref, far_ref, *rest):
    out_hbm, buf, sem = rest[-3:]
    slots, rows, width = far_ref.shape
    row = lax.broadcasted_iota(jnp.int32, (rows, width), 0) + meta_ref[1] * rows
    col = lax.broadcasted_iota(jnp.int32, (rows, width), 1)
    most = jnp.maximum(row, col)

    def put(s):
        return pltpu.make_async_copy(buf.at[s], out_hbm.at[start + s], sem.at[s])

    @pl.loop(0, slots)
    def _(s):
        value = base_ref[start + s] + far_ref[s].astype(F32)
        buf[s] = jnp.where(most < count_ref[start + s], value, 0.0)
        put(s).start()

    @pl.loop(0, slots)
    def _(s):
        put(s).wait()


def final(start, meta, count, base_terms, far, earlier=None):
    slots, rows, width = far.shape
    smem = pl.BlockSpec(memory_space=SMEM)
    vmem = pl.BlockSpec(memory_space=VMEM)
    hbm = pl.BlockSpec(memory_space=pltpu.HBM)
    more = [] if earlier is None else [earlier]

    def kernel(*refs):
        final_kernel(start, *refs)

    return pl.pallas_call(
        kernel,
        out_shape=jax.ShapeDtypeStruct(base_terms.shape, F32),
        in_specs=[smem, smem, vmem, vmem] + [hbm] * len(more),
        out_specs=hbm,
        scratch_shapes=[VMEM((slots, rows, width), F32), pltpu.SemaphoreType.DMA((slots,))],
        input_output_aliases={4: 0} if more else {},
        compiler_params=pltpu.CompilerParams(vmem_limit_bytes=4 * MIB),
        cost_estimate=pl.CostEstimate(
            flops=slots * 128 * 256 * 2, bytes_accessed=slots * MIB // 4, transcendentals=0),
    )(meta, count, base_terms, far, *more)


def local(blocks, pair_orbs, pno_count, amplitudes, margins, couple_target, couple_weight,
          pno_energy, occ_energy):
    holder = lax.axis_index("pairs").astype(jnp.int32)
    core = lax.axis_index("aux").astype(jnp.int32)
    holders = lax.axis_size("pairs")
    pairs, width = amplitudes.shape[0], amplitudes.shape[1]
    straight_in = toward(holders, False, True)
    straight_out = toward(holders, False, False)
    cross_out = toward(holders, True, False)
    swap = [(2 * h + c, 2 * h + 1 - c) for h in range(holders) for c in range(2)]

    orbs = pair_orbs.T
    near_blk = lax.ppermute(blocks, AXES, straight_in)
    near_orbs = lax.ppermute(orbs, AXES, straight_in)

    meta = jnp.stack([holder, core])
    rel = lax.dynamic_slice_in_dim(couple_target, holder * pairs, pairs, 0).T - holder * pairs
    weights = lax.dynamic_slice_in_dim(couple_weight, holder * pairs, pairs, 0).T
    rows, early_rows = width // 2, width // 4
    acc_near, acc_far, msg_early = coupling(
        meta, rel, weights, amplitudes, margins, rows, early_rows)
    early = lax.ppermute(msg_early, AXES, straight_out)

    chunks = [pairs * 3 // 4, pairs - pairs * 3 // 4]
    msg_near, = message(
        near_kernel, meta, near_orbs, near_blk, blocks, acc_near,
        [(pairs + 4, rows - early_rows)])
    near = lax.ppermute(msg_near, AXES, straight_out)
    msg_far = message(
        far_kernel, meta, near_orbs, near_blk, blocks, acc_far,
        [(n, rows) for n in chunks])
    far = lax.ppermute(msg_far[0], AXES, cross_out)
    last = lax.ppermute(msg_far[1], AXES, cross_out)

    keep, send = exchange(meta, near_blk, blocks)
    recv = lax.ppermute(send, AXES, swap)
    own, = coupling(meta, rel, weights, amplitudes, margins, rows, 0)
    base_terms = base(meta, orbs, occ_energy, pno_energy, amplitudes, own, early, near,
                      keep, recv)
    out = final(0, meta, pno_count, base_terms, far)
    return final(chunks[0], meta, pno_count, base_terms, last, out)


def solution(mesh):
    placed = (
        P("pairs", "aux", None),
        P("pairs", None),
        P("pairs"),
        P("pairs", None, None),
        P("pairs", None, None, None),
        P(),
        P(),
        P("pairs", None),
        P(),
    )

    return jax.shard_map(
        local, mesh=mesh, in_specs=placed, out_specs=P("pairs", "aux", None), check_vma=False
    )
```

time: 66.1 us -> 72.4 us (1.095)
  the two profiles are of different devices: /device:TPU:25 before, /device:TPU:24 now
where the time goes in v3:
time: 72.4 us; the launch traced here: 72 us
  starting transfers between devices  30.5 us (42%)
  Pallas kernels  20.7 us (29%)
  waiting for transfers between devices  18.3 us (25%)
  local copies, waits for them, and re-layouts  1.34 us (2%)
  other arithmetic  0.84 us (1%)
    pallas_call x2, Pallas kernels, coupling(): pl.pallas_call(functools.partial(coupling_kernel, early), out_shape=out_s...  10.3 us
    ppermute x1, starting transfers between devices, local(): near_blk = lax.ppermute(blocks, AXES, straight_in)  10.3 us
    ppermute x1, waiting for transfers between devices, local(): near_blk = lax.ppermute(blocks, AXES, straight_in)  9.6 us
    ppermute x1, starting transfers between devices, local(): last = lax.ppermute(msg_far[1], AXES, cross_out)  9.47 us
    ppermute x1, waiting for transfers between devices, local(): early = lax.ppermute(msg_early, AXES, straight_out)  8.7 us
    ppermute x1, starting transfers between devices, local(): early = lax.ppermute(msg_early, AXES, straight_out)  3.96 us
    pallas_call x2, Pallas kernels, final(): pl.pallas_call(kernel, out_shape=jax.ShapeDtypeStruct(base_terms.shape, F...  3.21 us
    ppermute x1, starting transfers between devices, local(): near_orbs = lax.ppermute(orbs, AXES, straight_in)  2.92 us
  transfers between devices with their start and end apart: 7, of which 2 were waited for; matrix products, arithmetic and copies ran while one was open for 1% of the time, Pallas kernels for 27%

profile of v3, /device:TPU:24, one launch (start us, length us, event | category | flops | bytes accessed | tf_op | source)
XLA Modules:
  0.0 72.0 jit_solution(3123206418096545864)
XLA Ops:
  0.0 0.0 copy-start
  0.0 10.3 %collective-permute-start.2 = (bf16[2,1024,256]{2,1,0:T(8,128)(2,1)}, bf16[2,1024,256]{2,1,0:T(8,128)(2,1)S(1)}, u32[]{:S(2)}, u32[]{:S(2)}) collective-permute-start(bf16[2,1024,256]{2,1,0:T(8,128)(2,1)} %blk.5), channel_id=1, source_target_pairs={{1,3},{2,0},{3,5},{4,2},{5,7},{6,4},{7,9},{8,6},{9,11},{10,8},{11,... | collective-permute-start | bytes 3145736 | tf_op jit(solution)/shard_map/ppermute | solution.py:322
  10.3 2.9 %collective-permute-start.1 = (s32[2,16]{1,0:T(2,128)}, s32[2,16]{1,0:T(2,128)S(1)}, u32[]{:S(2)}, u32[]{:S(2)}) collective-permute-start(s32[2,16]{1,0:T(2,128)} %bitcast.7), channel_id=1, source_target_pairs={{1,3},{2,0},{3,5},{4,2},{5,7},{6,4},{7,9},{8,6},{9,11},{10,8},{11,... | collective-permute-start | bytes 392 | tf_op jit(solution)/shard_map/ppermute | solution.py:323
  13.2 0.1 pad_add_fusion.meta_ref.refs_0_
  13.3 9.6 %collective-permute-done.2.near_blk = bf16[2,1024,256]{2,1,0:T(8,128)(2,1)S(1)} collective-permute-done((bf16[2,1024,256]{2,1,0:T(8,128)(2,1)}, bf16[2,1024,256]{2,1,0:T(8,128)(2,1)S(1)}, u32[]{:S(2)}, u32[]{:S(2)}) %collective-permute-start.2) | collective-permute-done | bytes 1048608 | tf_op jit(solution)/shard_map/ppermute | solution.py:322
  22.9 0.0 copy-start.2
  22.9 1.2 %copy-done.2 = bf16[2,1024,256]{2,1,0:T(8,128)(2,1)S(1)} copy-done((bf16[2,1024,256]{2,1,0:T(8,128)(2,1)S(1)}, bf16[2,1024,256]{2,1,0:T(8,128)(2,1)}, u32[]{:S(2)}) %copy-start.2) | copy-done | bytes 1048600
  24.1 1.9 %shard_map.94 = (f32[8,128,256]{2,1,0:T(8,128)S(1)}, f32[8,128,256]{2,1,0:T(8,128)S(1)}) custom-call(s32[2]{0:T(128)S(1)} %pad_add_fusion.meta_ref.refs_0_, bf16[2,1024,256]{2,1,0:T(8,128)(2,1)S(1)} %collective-permute-done.2.near_blk, bf16[2,1024,256]{2,1,0:T(8,128)(2,1)S(1)} %copy-done.2), custom_call_target="tpu_custom_call" | custom-call | flops 1073741824 | bytes 4194304 | tf_op jit(solution)/shard_map/pallas_call | solution.py:227
  26.0 0.1 collective-permute-start.4
  26.1 0.8 %subtract_bitcast_fusion.rel_ref = s32[4,16]{1,0:T(4,128)S(1)} fusion(s32[2048,4]{0,1:T(4,128)} %param.14, s32[]{:T(128)S(6)} %select_n.4, s32[]{:T(128)S(6)} %mul.2), kind=kLoop, calls=%fused_computation.1 | loop fusion | flops 64 | bytes 520 | tf_op jit(solution)/shard_map/sub | solution.py:326
  26.9 0.0 copy-done
  26.9 0.1 dynamic-slice_bitcast_fusion.w_ref
  26.9 0.0 copy-start.3
  26.9 5.2 %shard_map.92 = (f32[16,128,256]{2,1,0:T(8,128)S(1)}, f32[16,128,256]{2,1,0:T(8,128)S(1)}, bf16[16,64,256]{2,1,0:T(8,128)(2,1)S(1)}) custom-call(s32[2]{0:T(128)S(1)} %pad_add_fusion.meta_ref.refs_0_, s32[4,16]{1,0:T(4,128)S(1)} %subtract_bitcast_fusion.rel_ref, f32[4,16]{1,0:T(4,128)S(1)} %dynamic-slice_bitcast_fusion.w_ref, bf16[16,256,256]{2,1,0:T(8,128)(2,1)} %amp_ref.1, ...), custom_call_target="tpu_custom_call" | custom-call | flops 738197504 | bytes 6291456 | tf_op jit(solution)/shard_map/pallas_call | solution.py:137
  32.2 0.0 collective-permute-done.1.orbs_ref
  32.2 0.0 copy-done.3
  32.2 1.4 %shard_map.96 = (bf16[12,128,256]{2,1,0:T(8,128)(2,1)S(1)}, bf16[4,128,256]{2,1,0:T(8,128)(2,1)S(1)}) custom-call(s32[2]{0:T(128)S(1)} %pad_add_fusion.meta_ref.refs_0_, s32[2,16]{1,0:T(2,128)S(1)} %collective-permute-done.1.orbs_ref, bf16[2,1024,256]{2,1,0:T(8,128)(2,1)S(1)} %collective-permute-done.2.near_blk, bf16[2,1024,256]{2,1,0:T(8,128)(2,1)S(1)} %copy-done.3, ...), custom_call_target="tpu_custom_call" | custom-call | flops 268435456 | bytes 4194304 | tf_op jit(solution)/shard_map/pallas_call | solution.py:205
  33.6 1.9 %collective-permute-start.6 = (bf16[12,128,256]{2,1,0:T(8,128)(2,1)S(1)}, bf16[12,128,256]{2,1,0:T(8,128)(2,1)S(1)}, u32[]{:S(2)}, u32[]{:S(2)}) collective-permute-start(bf16[12,128,256]{2,1,0:T(8,128)(2,1)S(1)} %get-tuple-element.18), channel_id=1, source_target_pairs={{0,3},{2,5},{3,0},{4,7},{5,2},{6,9},{7,4},{8,11},{9,6},{10,13},{11... | collective-permute-start | bytes 2359304 | tf_op jit(solution)/shard_map/ppermute | solution.py:341
  35.5 0.0 copy-start.1
  35.5 1.3 %shard_map.93 = bf16[20,64,256]{2,1,0:T(8,128)(2,1)S(1)} custom-call(s32[2]{0:T(128)S(1)} %pad_add_fusion.meta_ref.refs_0_, s32[2,16]{1,0:T(2,128)S(1)} %collective-permute-done.1.orbs_ref, bf16[2,1024,256]{2,1,0:T(8,128)(2,1)S(1)} %collective-permute-done.2.near_blk, bf16[2,1024,256]{2,1,0:T(8,128)(2,1)S(1)} %copy-done.3, ...), custom_call_target="tpu_custom_call" | custom-call | flops 268435456 | bytes 4194304 | tf_op jit(solution)/shard_map/pallas_call | solution.py:205
  36.9 1.9 %collective-permute-start.3 = (bf16[20,64,256]{2,1,0:T(8,128)(2,1)S(1)}, bf16[20,64,256]{2,1,0:T(8,128)(2,1)S(1)}, u32[]{:S(2)}, u32[]{:S(2)}) collective-permute-start(bf16[20,64,256]{2,1,0:T(8,128)(2,1)S(1)} %shard_map.93), channel_id=1, source_target_pairs={{0,2},{2,4},{3,1},{4,6},{5,3},{6,8},{7,5},{8,10},{9,7},{10,12},{11... | collective-permute-start | bytes 1966088 | tf_op jit(solution)/shard_map/ppermute | solution.py:337
  38.8 4.0 %collective-permute-start = (bf16[16,64,256]{2,1,0:T(8,128)(2,1)S(1)}, bf16[16,64,256]{2,1,0:T(8,128)(2,1)S(1)}, u32[]{:S(2)}, u32[]{:S(2)}) collective-permute-start(bf16[16,64,256]{2,1,0:T(8,128)(2,1)S(1)} %get-tuple-element.12), channel_id=1, source_target_pairs={{0,2},{2,4},{3,1},{4,6},{5,3},{6,8},{7,5},{8,10},{9,7},{10,12},{11... | collective-permute-start | bytes 1572872 | tf_op jit(solution)/shard_map/ppermute | solution.py:331
  42.8 0.0 copy-start.4
  42.8 0.0 copy-start.6
  42.8 0.0 copy-start.7
  42.8 9.5 %collective-permute-start.5 = (bf16[4,128,256]{2,1,0:T(8,128)(2,1)S(1)}, bf16[4,128,256]{2,1,0:T(8,128)(2,1)S(1)}, u32[]{:S(2)}, u32[]{:S(2)}) collective-permute-start(bf16[4,128,256]{2,1,0:T(8,128)(2,1)S(1)} %get-tuple-element.17), channel_id=1, source_target_pairs={{0,3},{2,5},{3,0},{4,7},{5,2},{6,9},{7,4},{8,11},{9,6},{10,13},{11... | collective-permute-start | bytes 786440 | tf_op jit(solution)/shard_map/ppermute | solution.py:342
  52.3 0.0 copy-done.1
  52.3 5.1 %shard_map.91.own_ref = f32[16,128,256]{2,1,0:T(8,128)S(1)} custom-call(s32[2]{0:T(128)S(1)} %pad_add_fusion.meta_ref.refs_0_, s32[4,16]{1,0:T(4,128)S(1)} %subtract_bitcast_fusion.rel_ref, f32[4,16]{1,0:T(4,128)S(1)} %dynamic-slice_bitcast_fusion.w_ref, bf16[16,256,256]{2,1,0:T(8,128)(2,1)S(1)} %copy-done.1, bf16[16,4,256,256]{3,2,1,0:T(8,128)(2,1)} %mar_hbm.3), custom_call_target="tpu_custom_call" | custom-call | flops 738197504 | bytes 6291456 | tf_op jit(solution)/shard_map/pallas_call | solution.py:137
  57.4 8.7 %collective-permute-done.early_ref = bf16[16,64,256]{2,1,0:T(8,128)(2,1)S(1)} collective-permute-done((bf16[16,64,256]{2,1,0:T(8,128)(2,1)S(1)}, bf16[16,64,256]{2,1,0:T(8,128)(2,1)S(1)}, u32[]{:S(2)}, u32[]{:S(2)}) %collective-permute-start) | collective-permute-done | bytes 524320 | tf_op jit(solution)/shard_map/ppermute | solution.py:331
  66.1 0.0 collective-permute-done.3.near_ref
  66.1 0.0 collective-permute-done.4.recv_ref
  66.1 0.0 copy-done.4
  66.1 0.0 copy-done.6
  66.2 0.0 copy-done.7
  66.2 0.0 copy-start.5
  66.2 2.5 %shard_map.95.refs_2_ = f32[16,128,256]{2,1,0:T(8,128)S(1)} custom-call(s32[2]{0:T(128)S(1)} %pad_add_fusion.meta_ref.refs_0_, s32[2,16]{1,0:T(2,128)S(1)} %bitcast.8, f32[256]{0:T(256)S(1)} %copy-done.7, f32[16,256]{1,0:T(8,128)S(1)} %copy-done.4, bf16[16,256,256]{2,1,0:T(8,128)(2,1)S(1)} %copy-done.1, f32[16,128,256]{2,1,0:T(8,128)S(1)} %shard_map.91.own_ref, ...), custom_call_target="tpu_custom_call" | custom-call | flops 4194304 | bytes 8388608 | tf_op jit(solution)/shard_map/pallas_call | solution.py:261
  68.7 0.0 collective-permute-done.6.refs_3_
  68.7 0.0 copy-done.5
  68.7 1.8 %shard_map.97.refs_4_ = f32[16,128,256]{2,1,0:T(8,128)} custom-call(s32[2]{0:T(128)S(1)} %pad_add_fusion.meta_ref.refs_0_, s32[16]{0:T(128)S(1)} %copy-done.5, f32[16,128,256]{2,1,0:T(8,128)S(1)} %shard_map.95.refs_2_, bf16[12,128,256]{2,1,0:T(8,128)(2,1)S(1)} %collective-permute-done.6.refs_3_), custom_call_target="tpu_custom_call" | custom-call | flops 786432 | bytes 3145728 | tf_op jit(solution)/shard_map/pallas_call | solution.py:297
  70.6 0.0 collective-permute-done.5.refs_3_
  70.6 1.4 %shard_map.98 = f32[16,128,256]{2,1,0:T(8,128)} custom-call(s32[2]{0:T(128)S(1)} %pad_add_fusion.meta_ref.refs_0_, s32[16]{0:T(128)S(1)} %copy-done.5, f32[16,128,256]{2,1,0:T(8,128)S(1)} %shard_map.95.refs_2_, bf16[4,128,256]{2,1,0:T(8,128)(2,1)S(1)} %collective-permute-done.5.refs_3_, ...), custom_call_target="tpu_custom_call", output_to_operand_aliasing={{}: (4, {})} | custom-call | flops 262144 | bytes 1048576 | tf_op jit(solution)/shard_map/pallas_call | solution.py:297
Async XLA Ops:
  0.0 26.9 %copy-start = (f32[2048,4]{0,1:T(4,128)S(1)}, f32[2048,4]{0,1:T(4,128)}, u32[]{:S(2)}) copy-start(f32[2048,4]{0,1:T(4,128)} %param.15) | copy-start | bytes 98308
  0.0 22.9 %collective-permute-start.2 = (bf16[2,1024,256]{2,1,0:T(8,128)(2,1)}, bf16[2,1024,256]{2,1,0:T(8,128)(2,1)S(1)}, u32[]{:S(2)}, u32[]{:S(2)}) collective-permute-start(bf16[2,1024,256]{2,1,0:T(8,128)(2,1)} %blk.5), channel_id=1, source_target_pairs={{1,3},{2,0},{3,5},{4,2},{5,7},{6,4},{7,9},{8,6},{9,11},{10,8},{11,... | collective-permute-start | bytes 3145736 | tf_op jit(solution)/shard_map/ppermute | solution.py:322
  10.3 21.9 %collective-permute-start.1 = (s32[2,16]{1,0:T(2,128)}, s32[2,16]{1,0:T(2,128)S(1)}, u32[]{:S(2)}, u32[]{:S(2)}) collective-permute-start(s32[2,16]{1,0:T(2,128)} %bitcast.7), channel_id=1, source_target_pairs={{1,3},{2,0},{3,5},{4,2},{5,7},{6,4},{7,9},{8,6},{9,11},{10,8},{11,... | collective-permute-start | bytes 392 | tf_op jit(solution)/shard_map/ppermute | solution.py:323
  22.9 1.2 %copy-start.2 = (bf16[2,1024,256]{2,1,0:T(8,128)(2,1)S(1)}, bf16[2,1024,256]{2,1,0:T(8,128)(2,1)}, u32[]{:S(2)}) copy-start(bf16[2,1024,256]{2,1,0:T(8,128)(2,1)} %blk.5) | copy-start | bytes 3145732
  26.0 40.1 %collective-permute-start.4 = (f32[8,128,256]{2,1,0:T(8,128)S(1)}, f32[8,128,256]{2,1,0:T(8,128)S(1)}, u32[]{:S(2)}, u32[]{:S(2)}) collective-permute-start(f32[8,128,256]{2,1,0:T(8,128)S(1)} %get-tuple-element.15), channel_id=1, source_target_pairs={{0,1},{1,0},{2,3},{3,2},{4,5},{5,4},{6,7},{7,6},{8,9},{9,8},{10,11... | collective-permute-start | bytes 3145736 | tf_op jit(solution)/shard_map/ppermute | solution.py:345
  26.9 5.3 %copy-start.3 = (bf16[2,1024,256]{2,1,0:T(8,128)(2,1)S(1)}, bf16[2,1024,256]{2,1,0:T(8,128)(2,1)}, u32[]{:S(2)}) copy-start(bf16[2,1024,256]{2,1,0:T(8,128)(2,1)} %blk.5) | copy-start | bytes 3145732
  33.6 35.1 %collective-permute-start.6 = (bf16[12,128,256]{2,1,0:T(8,128)(2,1)S(1)}, bf16[12,128,256]{2,1,0:T(8,128)(2,1)S(1)}, u32[]{:S(2)}, u32[]{:S(2)}) collective-permute-start(bf16[12,128,256]{2,1,0:T(8,128)(2,1)S(1)} %get-tuple-element.18), channel_id=1, source_target_pairs={{0,3},{2,5},{3,0},{4,7},{5,2},{6,9},{7,4},{8,11},{9,6},{10,13},{11... | collective-permute-start | bytes 2359304 | tf_op jit(solution)/shard_map/ppermute | solution.py:341
  35.5 16.8 %copy-start.1 = (bf16[16,256,256]{2,1,0:T(8,128)(2,1)S(1)}, bf16[16,256,256]{2,1,0:T(8,128)(2,1)}, u32[]{:S(2)}) copy-start(bf16[16,256,256]{2,1,0:T(8,128)(2,1)} %amp_ref.1) | copy-start | bytes 6291460
  36.9 29.2 %collective-permute-start.3 = (bf16[20,64,256]{2,1,0:T(8,128)(2,1)S(1)}, bf16[20,64,256]{2,1,0:T(8,128)(2,1)S(1)}, u32[]{:S(2)}, u32[]{:S(2)}) collective-permute-start(bf16[20,64,256]{2,1,0:T(8,128)(2,1)S(1)} %shard_map.93), channel_id=1, source_target_pairs={{0,2},{2,4},{3,1},{4,6},{5,3},{6,8},{7,5},{8,10},{9,7},{10,12},{11... | collective-permute-start | bytes 1966088 | tf_op jit(solution)/shard_map/ppermute | solution.py:337
  38.8 27.3 %collective-permute-start = (bf16[16,64,256]{2,1,0:T(8,128)(2,1)S(1)}, bf16[16,64,256]{2,1,0:T(8,128)(2,1)S(1)}, u32[]{:S(2)}, u32[]{:S(2)}) collective-permute-start(bf16[16,64,256]{2,1,0:T(8,128)(2,1)S(1)} %get-tuple-element.12), channel_id=1, source_target_pairs={{0,2},{2,4},{3,1},{4,6},{5,3},{6,8},{7,5},{8,10},{9,7},{10,12},{11... | collective-permute-start | bytes 1572872 | tf_op jit(solution)/shard_map/ppermute | solution.py:331
  42.8 23.4 %copy-start.4 = (f32[16,256]{1,0:T(8,128)S(1)}, f32[16,256]{1,0:T(8,128)}, u32[]{:S(2)}) copy-start(f32[16,256]{1,0:T(8,128)} %en_ref.1) | copy-start | bytes 49156
  42.8 23.3 %copy-start.6 = (s32[16,2]{0,1:T(2,128)S(1)}, s32[16,2]{0,1:T(2,128)}, u32[]{:S(2)}) copy-start(s32[16,2]{0,1:T(2,128)} %param.10) | copy-start | bytes 388
  42.8 23.3 %copy-start.7 = (f32[256]{0:T(256)S(1)}, f32[256]{0:T(256)}, u32[]{:S(2)}) copy-start(f32[256]{0:T(256)} %occ_ref.1) | copy-start | bytes 3076
  42.8 27.7 %collective-permute-start.5 = (bf16[4,128,256]{2,1,0:T(8,128)(2,1)S(1)}, bf16[4,128,256]{2,1,0:T(8,128)(2,1)S(1)}, u32[]{:S(2)}, u32[]{:S(2)}) collective-permute-start(bf16[4,128,256]{2,1,0:T(8,128)(2,1)S(1)} %get-tuple-element.17), channel_id=1, source_target_pairs={{0,3},{2,5},{3,0},{4,7},{5,2},{6,9},{7,4},{8,11},{9,6},{10,13},{11... | collective-permute-start | bytes 786440 | tf_op jit(solution)/shard_map/ppermute | solution.py:342
  66.2 2.6 %copy-start.5 = (s32[16]{0:T(128)S(1)}, s32[16]{0:T(128)}, u32[]{:S(2)}) copy-start(s32[16]{0:T(128)} %refs_1_.3) | copy-start | bytes 196

commit v4 on v3

--- a/solution.py
+++ b/solution.py
@@ -33,117 +33,143 @@
     return lax.dot_general(a, b, (((0,), (0,)), ((), ())), preferred_element_type=F32)
 
 
-def coupling_kernel(early, meta_ref, rel_ref, w_ref, amp_hbm, mar_hbm, acc_ref, *rest):
-    (far_ref, early_ref), rest = (rest[:2], rest[2:]) if early else ((None, None), rest)
-    mbuf, fbuf, items, msem = rest[:4]
-    abuf, asem = rest[4:] if early else (amp_hbm, None)
-    sources, couplings = mar_hbm.shape[0], mar_hbm.shape[1]
-    slots, rows = acc_ref.shape[0], acc_ref.shape[1]
-    core = meta_ref[1]
-    shift = (1 - 2 * core) * slots if early else 0
-    row0 = pl.multiple_of(core * rows, rows)
-    far0 = pl.multiple_of(rows - core * rows, rows)
-
-    def mar_copy(k):
-        return pltpu.make_async_copy(
-            mar_hbm.at[k // couplings, k % couplings], mbuf.at[k], msem.at[k])
-
-    def amp_copy(q):
-        return pltpu.make_async_copy(amp_hbm.at[q], abuf.at[q], asem.at[q])
-
-    def scan(q, n):
-        if early:
-            amp_copy(q).start()
-        for c in range(couplings):
-            k = q * couplings + c
-            slot = rel_ref[c, q] - shift
-            mine = (slot >= 0) & (slot < slots)
-            items[n] = k
-
-            @pl.when(mine)
-            def _():
-                mar_copy(k).start()
-
-            n = n + mine.astype(jnp.int32)
-        return n
-
-    n = lax.fori_loop(0, sources, scan, jnp.int32(0))
+def sum_terms(items, n, rel_ref, w_ref, shift, mbuf, abuf, fbuf, row0s, acc_refs, ready):
+    couplings, rows = rel_ref.shape[0], acc_refs[0].shape[1]
     for u in range(UNROLL):
         items[n + u] = items[0]
 
-    @pl.loop(0, slots)
+    @pl.loop(0, acc_refs[0].shape[0])
     def _(s):
-        acc_ref[s] = jnp.zeros(acc_ref.shape[1:], F32)
-        if early:
-            far_ref[s] = jnp.zeros(acc_ref.shape[1:], F32)
-
-    def wait_amp(q, x):
-        amp_copy(q).wait()
-        return x
-
-    def body(g, waited):
+        for acc in acc_refs:
+            acc[s] = jnp.zeros(acc.shape[1:], F32)
+
+    def body(g, carry):
         ks = [items[g * UNROLL + u] for u in range(UNROLL)]
-        last = ks[0] // couplings
+        live = [g * UNROLL + u < n for u in range(UNROLL)]
+        carry = ready(ks, live, carry)
         for u in range(UNROLL):
-            @pl.when(g * UNROLL + u < n)
-            def _(u=u):
-                mar_copy(ks[u]).wait()
-
-            last = jnp.maximum(last, ks[u] // couplings)
-
-        if early:
-            lax.fori_loop(waited, last + 1, wait_amp, 0)
-        for u in range(UNROLL):
-            left = mbuf[ks[u], pl.ds(row0, rows), :]
-            if early:
-                left = jnp.concatenate([left, mbuf[ks[u], pl.ds(far0, rows), :]], axis=0)
+            parts = [mbuf[ks[u], pl.ds(row0, rows), :] for row0 in row0s]
+            left = parts[0] if len(parts) == 1 else jnp.concatenate(parts, axis=0)
             fbuf[u] = jnp.dot(
                 left, abuf[ks[u] // couplings], preferred_element_type=F32).astype(BF16)
         for u in range(UNROLL):
             c, q = ks[u] % couplings, ks[u] // couplings
-            weight = jnp.where(g * UNROLL + u < n, w_ref[c, q], 0.0)
+            weight = jnp.where(live[u], w_ref[c, q], 0.0)
             term = weight * nt_dot(fbuf[u], mbuf[ks[u]])
-            acc_ref[rel_ref[c, q] - shift] += term[:rows]
-            if early:
-                far_ref[rel_ref[c, q] - shift] += term[rows:]
+            for k, acc in enumerate(acc_refs):
+                acc[rel_ref[c, q] - shift] += term[k * rows:(k + 1) * rows]
+        return carry
+
+    return lax.fori_loop(0, pl.cdiv(n, UNROLL), body, jnp.int32(0))
+
+
+def list_terms(items, rel_ref, shift, slots, found):
+    couplings, sources = rel_ref.shape
+
+    def scan(q, n):
+        for c in range(couplings):
+            slot = rel_ref[c, q] - shift
+            mine = (slot >= 0) & (slot < slots)
+            items[n] = q * couplings + c
+            if found is not None:
+                pl.when(mine)(functools.partial(found, q, c))
+            n = n + mine.astype(jnp.int32)
+        return n
+
+    return lax.fori_loop(0, sources, scan, jnp.int32(0))
+
+
+def outward_kernel(meta_ref, rel_ref, w_ref, amp_hbm, mar_hbm, near_ref, far_ref, early_ref,
+                   mbuf, abuf, fbuf, items, own_items, msem, asem):
+    couplings, sources = rel_ref.shape
+    slots, rows, early = near_ref.shape[0], near_ref.shape[1], early_ref.shape[1]
+    core = meta_ref[1]
+    shift = (1 - 2 * core) * slots
+
+    def mar_copy(k):
+        return pltpu.make_async_copy(
+            mar_hbm.at[k // couplings, k % couplings], mbuf.at[k], msem.at[k])
+
+    def amp_copy(q):
+        return pltpu.make_async_copy(amp_hbm.at[q], abuf.at[q], asem.at[q])
+
+    @pl.loop(0, sources // 4)
+    def _(q):
+        amp_copy(q).start()
+
+    n = list_terms(items, rel_ref, shift, slots, lambda q, c: mar_copy(q * couplings + c).start())
+
+    @pl.loop(sources // 4, sources)
+    def _(q):
+        amp_copy(q).start()
+
+    n_own = list_terms(
+        own_items, rel_ref, 0, slots, lambda q, c: mar_copy(q * couplings + c).start())
+
+    def wait_amp(q, x):
+        amp_copy(q).wait()
+        return x
+
+    def ready(ks, live, waited):
+        last = ks[0] // couplings
+        for k, on in zip(ks, live):
+            pl.when(on)(lambda k=k: mar_copy(k).wait())
+            last = jnp.maximum(last, k // couplings)
+        lax.fori_loop(waited, last + 1, wait_amp, 0)
         return jnp.maximum(waited, last + 1)
 
-    waited = lax.fori_loop(0, pl.cdiv(n, UNROLL), body, jnp.int32(0))
-    if early:
-        lax.fori_loop(waited, sources, wait_amp, 0)
-
-        @pl.loop(0, slots)
-        def _(s):
-            early_ref[s] = acc_ref[s, :early].astype(BF16)
-
-
-def coupling(meta, rel, weights, amplitudes, margins, rows, early):
+    row0s = [pl.multiple_of(core * rows, rows), pl.multiple_of(rows - core * rows, rows)]
+    waited = sum_terms(
+        items, n, rel_ref, w_ref, shift, mbuf, abuf, fbuf, row0s, [near_ref, far_ref], ready)
+
+    @pl.loop(0, slots)
+    def _(s):
+        early_ref[s] = near_ref[s, :early].astype(BF16)
+
+    lax.fori_loop(waited, sources, wait_amp, 0)
+
+    @pl.loop(0, n_own)
+    def _(i):
+        mar_copy(own_items[i]).wait()
+
+
+def own_kernel(meta_ref, rel_ref, w_ref, abuf, mbuf, acc_ref, fbuf, items):
+    slots, rows = acc_ref.shape[0], acc_ref.shape[1]
+    n = list_terms(items, rel_ref, 0, slots, None)
+    sum_terms(items, n, rel_ref, w_ref, 0, mbuf, abuf, fbuf,
+              [pl.multiple_of(meta_ref[1] * rows, rows)], [acc_ref], lambda ks, live, c: c)
+
+
+def outward(meta, rel, weights, amplitudes, margins, rows, early):
     pairs, width = amplitudes.shape[0], amplitudes.shape[1]
     total = pairs * margins.shape[1]
     hbm = pl.BlockSpec(memory_space=pltpu.HBM)
     vmem = pl.BlockSpec(memory_space=VMEM)
     smem = pl.BlockSpec(memory_space=SMEM)
-    out_shape = [jax.ShapeDtypeStruct((pairs, rows, width), F32)]
-    scratch = [
-        VMEM((total, width, width), BF16),
-        VMEM((UNROLL, 2 * rows if early else rows, width), BF16),
-        SMEM((total + UNROLL,), jnp.int32),
-        pltpu.SemaphoreType.DMA((total,)),
-    ]
-    if early:
-        amplitudes = pltpu.with_memory_space_constraint(amplitudes, pltpu.HBM)
-        out_shape += [out_shape[0], jax.ShapeDtypeStruct((pairs, early, width), BF16)]
-        scratch += [VMEM((pairs, width, width), BF16), pltpu.SemaphoreType.DMA((pairs,))]
+    half = jax.ShapeDtypeStruct((pairs, rows, width), F32)
     return pl.pallas_call(
-        functools.partial(coupling_kernel, early),
-        out_shape=out_shape,
-        in_specs=[smem, smem, smem, hbm if early else vmem, hbm],
-        out_specs=[vmem] * len(out_shape),
-        scratch_shapes=scratch,
-        compiler_params=pltpu.CompilerParams(vmem_limit_bytes=12 * MIB),
+        outward_kernel,
+        out_shape=[
+            half, half,
+            jax.ShapeDtypeStruct((pairs, early, width), BF16),
+            jax.ShapeDtypeStruct((total, width, width), BF16),
+            jax.ShapeDtypeStruct((pairs, width, width), BF16),
+        ],
+        in_specs=[smem, smem, smem, hbm, hbm],
+        out_specs=[vmem] * 5,
+        scratch_shapes=[
+            VMEM((UNROLL, width, width), BF16),
+            SMEM((total + UNROLL,), jnp.int32),
+            SMEM((total + UNROLL,), jnp.int32),
+            pltpu.SemaphoreType.DMA((total,)),
+            pltpu.SemaphoreType.DMA((pairs,)),
+        ],
+        compiler_params=pltpu.CompilerParams(vmem_limit_bytes=4 * MIB),
         cost_estimate=pl.CostEstimate(
-            flops=2 * 22 * 2 * rows * 256 * 256, bytes_accessed=6 * MIB, transcendentals=0),
-    )(meta, rel, weights, amplitudes, pltpu.with_memory_space_constraint(margins, pltpu.HBM))
+            flops=2 * 22 * 2 * 256 * 256 * 256, bytes_accessed=8 * MIB, transcendentals=0),
+        name="outward",
+    )(meta, rel, weights, pltpu.with_memory_space_constraint(amplitudes, pltpu.HBM),
+      pltpu.with_memory_space_constraint(margins, pltpu.HBM))
 
 
 def whole(kernel, out_shape, n_smem, n_vmem, limit, cost, **extra):
@@ -177,14 +203,16 @@
 
 def near_kernel(meta_ref, orbs_ref, near_blk, blk, acc_ref, out, prod):
     products(False, near_blk, blk, meta_ref, prod)
-    slots, early = acc_ref.shape[0], prod.shape[1] - out.shape[1]
+    slots, early = acc_ref.shape[0], out.shape[1]
+    parts = prod.shape[1] // early - 1
 
     @pl.loop(0, slots)
     def _(s):
-        out[s] = (acc_ref[s, early:] + prod[pick(meta_ref, orbs_ref, s), early:]).astype(BF16)
+        value = acc_ref[s, early:] + prod[pick(meta_ref, orbs_ref, s), early:]
+        out[pl.ds(parts * s, parts)] = value.astype(BF16).reshape(parts, early, -1)
 
     for k in range(4):
-        out[slots + k] = prod[k, :early].astype(BF16)
+        out[parts * slots + k] = prod[k, :early].astype(BF16)
 
 
 def far_kernel(meta_ref, orbs_ref, near_blk, blk, acc_ref, *rest):
@@ -233,6 +261,7 @@
                 early_ref, near_ref, keep_ref, recv_ref, out_ref):
     slots, rows, width = out_ref.shape
     early = early_ref.shape[1]
+    parts = rows // early - 1
     holder, core = meta_ref[0], meta_ref[1]
     row0 = pl.multiple_of(core * rows, rows)
 
@@ -252,9 +281,10 @@
         value += own_ref[p]
         value += keep_ref[both] * jnp.where(side == -step, 0.0, 1.0)
         value += recv_ref[both] * jnp.where(side == step, 0.0, 1.0)
-        lacking = near_ref[slots + index].astype(F32) * jnp.where(side == -step, 1.0, 0.0)
+        lacking = near_ref[parts * slots + index].astype(F32) * jnp.where(side == -step, 1.0, 0.0)
         out_ref[p, :early] = value[:early] + early_ref[p].astype(F32) + lacking
-        out_ref[p, early:] = value[early:] + near_ref[p].astype(F32)
+        late = near_ref[pl.ds(parts * p, parts)].reshape(rows - early, width)
+        out_ref[p, early:] = value[early:] + late.astype(F32)
 
 
 def base(meta, orbs, occ, energy, amplitudes, own, early, near, keep, recv):
@@ -325,15 +355,15 @@
     meta = jnp.stack([holder, core])
     rel = lax.dynamic_slice_in_dim(couple_target, holder * pairs, pairs, 0).T - holder * pairs
     weights = lax.dynamic_slice_in_dim(couple_weight, holder * pairs, pairs, 0).T
-    rows, early_rows = width // 2, width // 4
-    acc_near, acc_far, msg_early = coupling(
+    rows, early_rows = width // 2, width // 8
+    acc_near, acc_far, msg_early, held_mar, held_amp = outward(
         meta, rel, weights, amplitudes, margins, rows, early_rows)
     early = lax.ppermute(msg_early, AXES, straight_out)
 
     chunks = [pairs * 3 // 4, pairs - pairs * 3 // 4]
     msg_near, = message(
         near_kernel, meta, near_orbs, near_blk, blocks, acc_near,
-        [(pairs + 4, rows - early_rows)])
+        [(pairs * (rows // early_rows - 1) + 4, early_rows)])
     near = lax.ppermute(msg_near, AXES, straight_out)
     msg_far = message(
         far_kernel, meta, near_orbs, near_blk, blocks, acc_far,
@@ -343,8 +373,13 @@
 
     keep, send = exchange(meta, near_blk, blocks)
     recv = lax.ppermute(send, AXES, swap)
-    own, = coupling(meta, rel, weights, amplitudes, margins, rows, 0)
-    base_terms = base(meta, orbs, occ_energy, pno_energy, amplitudes, own, early, near,
+    own = whole(
+        own_kernel, jax.ShapeDtypeStruct((pairs, rows, width), F32), 3, 2, 4,
+        (2 * 22 * 2 * rows * 256 * 256, 4),
+        scratch_shapes=[VMEM((UNROLL, rows, width), BF16),
+                        SMEM((held_mar.shape[0] + UNROLL,), jnp.int32)],
+    )(meta, rel, weights, held_amp, held_mar)
+    base_terms = base(meta, orbs, occ_energy, pno_energy, held_amp, own, early, near,
                       keep, recv)
     out = final(0, meta, pno_count, base_terms, far)
     return final(chunks[0], meta, pno_count, base_terms, last, out)

time: 72.4 us -> 71.9 us (level)
    ppermute x1, starting transfers between devices: 1.92 us -> 4.22 us  [local(): far = lax.ppermute(msg_far[0], AXES, cross_out)]
    ppermute x1, starting transfers between devices: 3.96 us -> 1.92 us  [local(): early = lax.ppermute(msg_early, AXES, straight_out)]
    ppermute x1, waiting for transfers between devices: 8.7 us -> 9.58 us  [local(): early = lax.ppermute(msg_early, AXES, straight_out)]
    ppermute x1, waiting for transfers between devices: 9.6 us -> 8.85 us  [local(): near_blk = lax.ppermute(blocks, AXES, straight_in)]
  transfers between devices with their start and end apart: 7 -> 7, of which waited for: 2 -> 2; matrix products, arithmetic and copies ran while one was open for 1% -> 1% of each run, Pallas kernels for 27% -> 26%
where the time goes in v4:
time: 71.9 us; the launch traced here: 71.5 us
  starting transfers between devices  30.4 us (42%)
  Pallas kernels  20.3 us (28%)
  waiting for transfers between devices  18.4 us (26%)
  local copies, waits for them, and re-layouts  1.34 us (2%)
  other arithmetic  0.83 us (1%)
    ppermute x1, starting transfers between devices, local(): near_blk = lax.ppermute(blocks, AXES, straight_in)  10.3 us
    ppermute x1, waiting for transfers between devices, local(): early = lax.ppermute(msg_early, AXES, straight_out)  9.58 us
    ppermute x1, starting transfers between devices, local(): last = lax.ppermute(msg_far[1], AXES, cross_out)  9.02 us
    ppermute x1, waiting for transfers between devices, local(): near_blk = lax.ppermute(blocks, AXES, straight_in)  8.85 us
    pallas_call x1, Pallas kernels, outward(): pl.pallas_call(outward_kernel, out_shape=[half, half, jax.ShapeDtypeStruc...  6.32 us
    ppermute x1, starting transfers between devices, local(): far = lax.ppermute(msg_far[0], AXES, cross_out)  4.22 us
    pallas_call x1, Pallas kernels, local(): whole(own_kernel, jax.ShapeDtypeStruct((pairs, rows, width), F32), 3, 2,...  3.64 us
    pallas_call x2, Pallas kernels, final(): pl.pallas_call(kernel, out_shape=jax.ShapeDtypeStruct(base_terms.shape, F...  3.21 us
  transfers between devices with their start and end apart: 7, of which 2 were waited for; matrix products, arithmetic and copies ran while one was open for 1% of the time, Pallas kernels for 26%

profile of v4, /device:TPU:24, one launch (start us, length us, event | category | flops | bytes accessed | tf_op | source)
XLA Modules:
  0.0 71.5 jit_solution(7065495690826640206)
XLA Ops:
  0.0 0.0 copy-start
  0.0 10.3 %collective-permute-start.2 = (bf16[2,1024,256]{2,1,0:T(8,128)(2,1)}, bf16[2,1024,256]{2,1,0:T(8,128)(2,1)S(1)}, u32[]{:S(2)}, u32[]{:S(2)}) collective-permute-start(bf16[2,1024,256]{2,1,0:T(8,128)(2,1)} %blk.5), channel_id=1, source_target_pairs={{1,3},{2,0},{3,5},{4,2},{5,7},{6,4},{7,9},{8,6},{9,11},{10,8},{11,... | collective-permute-start | bytes 3145736 | tf_op jit(solution)/shard_map/ppermute | solution.py:352
  10.3 2.9 %collective-permute-start.1 = (s32[2,16]{1,0:T(2,128)}, s32[2,16]{1,0:T(2,128)S(1)}, u32[]{:S(2)}, u32[]{:S(2)}) collective-permute-start(s32[2,16]{1,0:T(2,128)} %bitcast.7), channel_id=1, source_target_pairs={{1,3},{2,0},{3,5},{4,2},{5,7},{6,4},{7,9},{8,6},{9,11},{10,8},{11,... | collective-permute-start | bytes 392 | tf_op jit(solution)/shard_map/ppermute | solution.py:353
  13.2 0.1 pad_add_fusion.meta_ref.refs_0_
  13.3 0.8 %subtract_bitcast_fusion.rel_ref = s32[4,16]{1,0:T(4,128)S(1)} fusion(s32[2048,4]{0,1:T(4,128)} %param.14, s32[]{:T(128)S(6)} %select_n.4, s32[]{:T(128)S(6)} %mul.2), kind=kLoop, calls=%fused_computation.1 | loop fusion | flops 64 | bytes 520 | tf_op jit(solution)/shard_map/sub | solution.py:356
  14.0 8.8 %collective-permute-done.2.near_blk = bf16[2,1024,256]{2,1,0:T(8,128)(2,1)S(1)} collective-permute-done((bf16[2,1024,256]{2,1,0:T(8,128)(2,1)}, bf16[2,1024,256]{2,1,0:T(8,128)(2,1)S(1)}, u32[]{:S(2)}, u32[]{:S(2)}) %collective-permute-start.2) | collective-permute-done | bytes 1048608 | tf_op jit(solution)/shard_map/ppermute | solution.py:352
  22.9 0.0 copy-start.1
  22.9 1.2 %copy-done.1 = bf16[2,1024,256]{2,1,0:T(8,128)(2,1)S(1)} copy-done((bf16[2,1024,256]{2,1,0:T(8,128)(2,1)S(1)}, bf16[2,1024,256]{2,1,0:T(8,128)(2,1)}, u32[]{:S(2)}) %copy-start.1) | copy-done | bytes 1048600
  24.1 1.9 %shard_map.93 = (f32[8,128,256]{2,1,0:T(8,128)S(1)}, f32[8,128,256]{2,1,0:T(8,128)S(1)}) custom-call(s32[2]{0:T(128)S(1)} %pad_add_fusion.meta_ref.refs_0_, bf16[2,1024,256]{2,1,0:T(8,128)(2,1)S(1)} %collective-permute-done.2.near_blk, bf16[2,1024,256]{2,1,0:T(8,128)(2,1)S(1)} %copy-done.1), custom_call_target="tpu_custom_call" | custom-call | flops 1073741824 | bytes 4194304 | tf_op jit(solution)/shard_map/pallas_call | solution.py:255
  26.0 0.1 collective-permute-start.4
  26.1 0.0 copy-done
  26.1 0.1 dynamic-slice_bitcast_fusion.w_ref
  26.2 0.0 copy-start.2
  26.2 6.3 %outward.1 = (f32[16,128,256]{2,1,0:T(8,128)S(1)}, f32[16,128,256]{2,1,0:T(8,128)S(1)}, bf16[16,32,256]{2,1,0:T(8,128)(2,1)S(1)}, bf16[64,256,256]{2,1,0:T(8,128)(2,1)S(1)}, bf16[16,256,256]{2,1,0:T(8,128)(2,1)S(1)}) custom-call(s32[2]{0:T(128)S(1)} %pad_add_fusion.meta_ref.refs_0_, s32[4,16]{1,0:T(4,128)S(1)} %subtract_bitcast_fusion.rel_ref, ...), custom_call_target="tpu_custom_call" | custom-call | flops 1476395008 | bytes 8388608 | tf_op jit(solution)/shard_map/outward/pallas_call | solution.py:150
  32.5 0.0 collective-permute-done.1.orbs_ref
  32.5 0.0 copy-done.2
  32.5 1.4 %shard_map.92 = bf16[52,32,256]{2,1,0:T(8,128)(2,1)S(1)} custom-call(s32[2]{0:T(128)S(1)} %pad_add_fusion.meta_ref.refs_0_, s32[2,16]{1,0:T(2,128)S(1)} %collective-permute-done.1.orbs_ref, bf16[2,1024,256]{2,1,0:T(8,128)(2,1)S(1)} %collective-permute-done.2.near_blk, bf16[2,1024,256]{2,1,0:T(8,128)(2,1)S(1)} %copy-done.2, ...), custom_call_target="tpu_custom_call" | custom-call | flops 268435456 | bytes 4194304 | tf_op jit(solution)/shard_map/pallas_call | solution.py:233
  33.9 1.9 %collective-permute-start.3 = (bf16[52,32,256]{2,1,0:T(8,128)(2,1)S(1)}, bf16[52,32,256]{2,1,0:T(8,128)(2,1)S(1)}, u32[]{:S(2)}, u32[]{:S(2)}) collective-permute-start(bf16[52,32,256]{2,1,0:T(8,128)(2,1)S(1)} %shard_map.92), channel_id=1, source_target_pairs={{0,2},{2,4},{3,1},{4,6},{5,3},{6,8},{7,5},{8,10},{9,7},{10,12},{11... | collective-permute-start | bytes 2555912 | tf_op jit(solution)/shard_map/ppermute | solution.py:367
  35.8 1.4 %shard_map.95 = (bf16[12,128,256]{2,1,0:T(8,128)(2,1)S(1)}, bf16[4,128,256]{2,1,0:T(8,128)(2,1)S(1)}) custom-call(s32[2]{0:T(128)S(1)} %pad_add_fusion.meta_ref.refs_0_, s32[2,16]{1,0:T(2,128)S(1)} %collective-permute-done.1.orbs_ref, bf16[2,1024,256]{2,1,0:T(8,128)(2,1)S(1)} %collective-permute-done.2.near_blk, bf16[2,1024,256]{2,1,0:T(8,128)(2,1)S(1)} %copy-done.2, ...), custom_call_target="tpu_custom_call" | custom-call | flops 268435456 | bytes 4194304 | tf_op jit(solution)/shard_map/pallas_call | solution.py:233
  37.2 4.2 %collective-permute-start.6 = (bf16[12,128,256]{2,1,0:T(8,128)(2,1)S(1)}, bf16[12,128,256]{2,1,0:T(8,128)(2,1)S(1)}, u32[]{:S(2)}, u32[]{:S(2)}) collective-permute-start(bf16[12,128,256]{2,1,0:T(8,128)(2,1)S(1)} %get-tuple-element.22), channel_id=1, source_target_pairs={{0,3},{2,5},{3,0},{4,7},{5,2},{6,9},{7,4},{8,11},{9,6},{10,13},{11... | collective-permute-start | bytes 2359304 | tf_op jit(solution)/shard_map/ppermute | solution.py:371
  41.5 1.9 %collective-permute-start = (bf16[16,32,256]{2,1,0:T(8,128)(2,1)S(1)}, bf16[16,32,256]{2,1,0:T(8,128)(2,1)S(1)}, u32[]{:S(2)}, u32[]{:S(2)}) collective-permute-start(bf16[16,32,256]{2,1,0:T(8,128)(2,1)S(1)} %get-tuple-element.16), channel_id=1, source_target_pairs={{0,2},{2,4},{3,1},{4,6},{5,3},{6,8},{7,5},{8,10},{9,7},{10,12},{11... | collective-permute-start | bytes 786440 | tf_op jit(solution)/shard_map/ppermute | solution.py:361
  43.4 9.0 %collective-permute-start.5 = (bf16[4,128,256]{2,1,0:T(8,128)(2,1)S(1)}, bf16[4,128,256]{2,1,0:T(8,128)(2,1)S(1)}, u32[]{:S(2)}, u32[]{:S(2)}) collective-permute-start(bf16[4,128,256]{2,1,0:T(8,128)(2,1)S(1)} %get-tuple-element.21), channel_id=1, source_target_pairs={{0,3},{2,5},{3,0},{4,7},{5,2},{6,9},{7,4},{8,11},{9,6},{10,13},{11... | collective-permute-start | bytes 786440 | tf_op jit(solution)/shard_map/ppermute | solution.py:372
  52.4 0.0 copy-start.3
  52.4 0.0 copy-start.5
  52.5 0.0 copy-start.6
  52.5 3.6 %shard_map.91.own_ref = f32[16,128,256]{2,1,0:T(8,128)S(1)} custom-call(s32[2]{0:T(128)S(1)} %pad_add_fusion.meta_ref.refs_0_, s32[4,16]{1,0:T(4,128)S(1)} %subtract_bitcast_fusion.rel_ref, f32[4,16]{1,0:T(4,128)S(1)} %dynamic-slice_bitcast_fusion.w_ref, bf16[16,256,256]{2,1,0:T(8,128)(2,1)S(1)} %get-tuple-element.14.abuf.amp_ref, ...), custom_call_target="tpu_custom_call" | custom-call | flops 738197504 | bytes 4194304 | tf_op jit(solution)/shard_map/pallas_call | solution.py:376
  56.1 9.6 %collective-permute-done.early_ref = bf16[16,32,256]{2,1,0:T(8,128)(2,1)S(1)} collective-permute-done((bf16[16,32,256]{2,1,0:T(8,128)(2,1)S(1)}, bf16[16,32,256]{2,1,0:T(8,128)(2,1)S(1)}, u32[]{:S(2)}, u32[]{:S(2)}) %collective-permute-start) | collective-permute-done | bytes 262176 | tf_op jit(solution)/shard_map/ppermute | solution.py:361
  65.7 0.0 collective-permute-done.3.near_ref
  65.7 0.0 collective-permute-done.4.recv_ref
  65.7 0.0 copy-done.3
  65.7 0.0 copy-done.5
  65.7 0.0 copy-done.6
  65.7 0.0 copy-start.4
  65.7 2.5 %shard_map.94.refs_2_ = f32[16,128,256]{2,1,0:T(8,128)S(1)} custom-call(s32[2]{0:T(128)S(1)} %pad_add_fusion.meta_ref.refs_0_, s32[2,16]{1,0:T(2,128)S(1)} %bitcast.8, f32[256]{0:T(256)S(1)} %copy-done.6, f32[16,256]{1,0:T(8,128)S(1)} %copy-done.3, bf16[16,256,256]{2,1,0:T(8,128)(2,1)S(1)} %get-tuple-element.14.abuf.amp_ref, ...), custom_call_target="tpu_custom_call" | custom-call | flops 4194304 | bytes 8388608 | tf_op jit(solution)/shard_map/pallas_call | solution.py:291
  68.3 0.0 collective-permute-done.6.refs_3_
  68.3 0.0 copy-done.4
  68.3 1.8 %shard_map.96.refs_4_ = f32[16,128,256]{2,1,0:T(8,128)} custom-call(s32[2]{0:T(128)S(1)} %pad_add_fusion.meta_ref.refs_0_, s32[16]{0:T(128)S(1)} %copy-done.4, f32[16,128,256]{2,1,0:T(8,128)S(1)} %shard_map.94.refs_2_, bf16[12,128,256]{2,1,0:T(8,128)(2,1)S(1)} %collective-permute-done.6.refs_3_), custom_call_target="tpu_custom_call" | custom-call | flops 786432 | bytes 3145728 | tf_op jit(solution)/shard_map/pallas_call | solution.py:327
  70.1 0.0 collective-permute-done.5.refs_3_
  70.1 1.4 %shard_map.97 = f32[16,128,256]{2,1,0:T(8,128)} custom-call(s32[2]{0:T(128)S(1)} %pad_add_fusion.meta_ref.refs_0_, s32[16]{0:T(128)S(1)} %copy-done.4, f32[16,128,256]{2,1,0:T(8,128)S(1)} %shard_map.94.refs_2_, bf16[4,128,256]{2,1,0:T(8,128)(2,1)S(1)} %collective-permute-done.5.refs_3_, ...), custom_call_target="tpu_custom_call", output_to_operand_aliasing={{}: (4, {})} | custom-call | flops 262144 | bytes 1048576 | tf_op jit(solution)/shard_map/pallas_call | solution.py:327
Async XLA Ops:
  0.0 26.1 %copy-start = (f32[2048,4]{0,1:T(4,128)S(1)}, f32[2048,4]{0,1:T(4,128)}, u32[]{:S(2)}) copy-start(f32[2048,4]{0,1:T(4,128)} %param.15) | copy-start | bytes 98308
  0.0 22.9 %collective-permute-start.2 = (bf16[2,1024,256]{2,1,0:T(8,128)(2,1)}, bf16[2,1024,256]{2,1,0:T(8,128)(2,1)S(1)}, u32[]{:S(2)}, u32[]{:S(2)}) collective-permute-start(bf16[2,1024,256]{2,1,0:T(8,128)(2,1)} %blk.5), channel_id=1, source_target_pairs={{1,3},{2,0},{3,5},{4,2},{5,7},{6,4},{7,9},{8,6},{9,11},{10,8},{11,... | collective-permute-start | bytes 3145736 | tf_op jit(solution)/shard_map/ppermute | solution.py:352
  10.3 22.3 %collective-permute-start.1 = (s32[2,16]{1,0:T(2,128)}, s32[2,16]{1,0:T(2,128)S(1)}, u32[]{:S(2)}, u32[]{:S(2)}) collective-permute-start(s32[2,16]{1,0:T(2,128)} %bitcast.7), channel_id=1, source_target_pairs={{1,3},{2,0},{3,5},{4,2},{5,7},{6,4},{7,9},{8,6},{9,11},{10,8},{11,... | collective-permute-start | bytes 392 | tf_op jit(solution)/shard_map/ppermute | solution.py:353
  22.9 1.2 %copy-start.1 = (bf16[2,1024,256]{2,1,0:T(8,128)(2,1)S(1)}, bf16[2,1024,256]{2,1,0:T(8,128)(2,1)}, u32[]{:S(2)}) copy-start(bf16[2,1024,256]{2,1,0:T(8,128)(2,1)} %blk.5) | copy-start | bytes 3145732
  26.0 39.7 %collective-permute-start.4 = (f32[8,128,256]{2,1,0:T(8,128)S(1)}, f32[8,128,256]{2,1,0:T(8,128)S(1)}, u32[]{:S(2)}, u32[]{:S(2)}) collective-permute-start(f32[8,128,256]{2,1,0:T(8,128)S(1)} %get-tuple-element.19), channel_id=1, source_target_pairs={{0,1},{1,0},{2,3},{3,2},{4,5},{5,4},{6,7},{7,6},{8,9},{9,8},{10,11... | collective-permute-start | bytes 3145736 | tf_op jit(solution)/shard_map/ppermute | solution.py:375
  26.2 6.3 %copy-start.2 = (bf16[2,1024,256]{2,1,0:T(8,128)(2,1)S(1)}, bf16[2,1024,256]{2,1,0:T(8,128)(2,1)}, u32[]{:S(2)}) copy-start(bf16[2,1024,256]{2,1,0:T(8,128)(2,1)} %blk.5) | copy-start | bytes 3145732
  33.9 31.8 %collective-permute-start.3 = (bf16[52,32,256]{2,1,0:T(8,128)(2,1)S(1)}, bf16[52,32,256]{2,1,0:T(8,128)(2,1)S(1)}, u32[]{:S(2)}, u32[]{:S(2)}) collective-permute-start(bf16[52,32,256]{2,1,0:T(8,128)(2,1)S(1)} %shard_map.92), channel_id=1, source_target_pairs={{0,2},{2,4},{3,1},{4,6},{5,3},{6,8},{7,5},{8,10},{9,7},{10,12},{11... | collective-permute-start | bytes 2555912 | tf_op jit(solution)/shard_map/ppermute | solution.py:367
  37.2 31.0 %collective-permute-start.6 = (bf16[12,128,256]{2,1,0:T(8,128)(2,1)S(1)}, bf16[12,128,256]{2,1,0:T(8,128)(2,1)S(1)}, u32[]{:S(2)}, u32[]{:S(2)}) collective-permute-start(bf16[12,128,256]{2,1,0:T(8,128)(2,1)S(1)} %get-tuple-element.22), channel_id=1, source_target_pairs={{0,3},{2,5},{3,0},{4,7},{5,2},{6,9},{7,4},{8,11},{9,6},{10,13},{11... | collective-permute-start | bytes 2359304 | tf_op jit(solution)/shard_map/ppermute | solution.py:371
  41.5 24.2 %collective-permute-start = (bf16[16,32,256]{2,1,0:T(8,128)(2,1)S(1)}, bf16[16,32,256]{2,1,0:T(8,128)(2,1)S(1)}, u32[]{:S(2)}, u32[]{:S(2)}) collective-permute-start(bf16[16,32,256]{2,1,0:T(8,128)(2,1)S(1)} %get-tuple-element.16), channel_id=1, source_target_pairs={{0,2},{2,4},{3,1},{4,6},{5,3},{6,8},{7,5},{8,10},{9,7},{10,12},{11... | collective-permute-start | bytes 786440 | tf_op jit(solution)/shard_map/ppermute | solution.py:361
  43.4 26.7 %collective-permute-start.5 = (bf16[4,128,256]{2,1,0:T(8,128)(2,1)S(1)}, bf16[4,128,256]{2,1,0:T(8,128)(2,1)S(1)}, u32[]{:S(2)}, u32[]{:S(2)}) collective-permute-start(bf16[4,128,256]{2,1,0:T(8,128)(2,1)S(1)} %get-tuple-element.21), channel_id=1, source_target_pairs={{0,3},{2,5},{3,0},{4,7},{5,2},{6,9},{7,4},{8,11},{9,6},{10,13},{11... | collective-permute-start | bytes 786440 | tf_op jit(solution)/shard_map/ppermute | solution.py:372
  52.4 13.3 %copy-start.3 = (f32[16,256]{1,0:T(8,128)S(1)}, f32[16,256]{1,0:T(8,128)}, u32[]{:S(2)}) copy-start(f32[16,256]{1,0:T(8,128)} %en_ref.1) | copy-start | bytes 49156
  52.4 13.3 %copy-start.5 = (s32[16,2]{0,1:T(2,128)S(1)}, s32[16,2]{0,1:T(2,128)}, u32[]{:S(2)}) copy-start(s32[16,2]{0,1:T(2,128)} %param.10) | copy-start | bytes 388
  52.5 13.3 %copy-start.6 = (f32[256]{0:T(256)S(1)}, f32[256]{0:T(256)}, u32[]{:S(2)}) copy-start(f32[256]{0:T(256)} %occ_ref.1) | copy-start | bytes 3076
  65.7 2.6 %copy-start.4 = (s32[16]{0:T(128)S(1)}, s32[16]{0:T(128)}, u32[]{:S(2)}) copy-start(s32[16]{0:T(128)} %refs_1_.3) | copy-start | bytes 196

commit v5 on v3

--- a/solution.py
+++ b/solution.py
@@ -33,10 +33,11 @@
     return lax.dot_general(a, b, (((0,), (0,)), ((), ())), preferred_element_type=F32)
 
 
-def coupling_kernel(early, meta_ref, rel_ref, w_ref, amp_hbm, mar_hbm, acc_ref, *rest):
-    (far_ref, early_ref), rest = (rest[:2], rest[2:]) if early else ((None, None), rest)
-    mbuf, fbuf, items, msem = rest[:4]
-    abuf, asem = rest[4:] if early else (amp_hbm, None)
+def coupling_kernel(early, meta_ref, rel_ref, w_ref, amp_hbm, mar_hbm, *rest):
+    if early:
+        far_ref, early_ref, mbuf, fbuf, items, msem, abuf, asem, acc_ref = rest
+    else:
+        (acc_ref, mbuf, fbuf, items, msem), abuf = rest, amp_hbm
     sources, couplings = mar_hbm.shape[0], mar_hbm.shape[1]
     slots, rows = acc_ref.shape[0], acc_ref.shape[1]
     core = meta_ref[1]
@@ -132,15 +133,16 @@
     ]
     if early:
         amplitudes = pltpu.with_memory_space_constraint(amplitudes, pltpu.HBM)
-        out_shape += [out_shape[0], jax.ShapeDtypeStruct((pairs, early, width), BF16)]
-        scratch += [VMEM((pairs, width, width), BF16), pltpu.SemaphoreType.DMA((pairs,))]
+        out_shape.append(jax.ShapeDtypeStruct((pairs, early, width), BF16))
+        scratch += [VMEM((pairs, width, width), BF16), pltpu.SemaphoreType.DMA((pairs,)),
+                    VMEM((pairs, rows, width), F32)]
     return pl.pallas_call(
         functools.partial(coupling_kernel, early),
         out_shape=out_shape,
         in_specs=[smem, smem, smem, hbm if early else vmem, hbm],
         out_specs=[vmem] * len(out_shape),
         scratch_shapes=scratch,
-        compiler_params=pltpu.CompilerParams(vmem_limit_bytes=12 * MIB),
+        compiler_params=pltpu.CompilerParams(vmem_limit_bytes=14 * MIB),
         cost_estimate=pl.CostEstimate(
             flops=2 * 22 * 2 * rows * 256 * 256, bytes_accessed=6 * MIB, transcendentals=0),
     )(meta, rel, weights, amplitudes, pltpu.with_memory_space_constraint(margins, pltpu.HBM))
@@ -175,16 +177,10 @@
     return jnp.where(mine, 2 * (orbs_ref[0, s] % 2) + second, 4)
 
 
-def near_kernel(meta_ref, orbs_ref, near_blk, blk, acc_ref, out, prod):
+def near_kernel(meta_ref, near_blk, blk, out, prod):
     products(False, near_blk, blk, meta_ref, prod)
-    slots, early = acc_ref.shape[0], prod.shape[1] - out.shape[1]
-
-    @pl.loop(0, slots)
-    def _(s):
-        out[s] = (acc_ref[s, early:] + prod[pick(meta_ref, orbs_ref, s), early:]).astype(BF16)
-
     for k in range(4):
-        out[slots + k] = prod[k, :early].astype(BF16)
+        out[k] = prod[k].astype(BF16)
 
 
 def far_kernel(meta_ref, orbs_ref, near_blk, blk, acc_ref, *rest):
@@ -200,14 +196,13 @@
         start += out.shape[0]
 
 
-def message(kernel, meta, orbs, near_blk, blk, acc, outs):
-    width = acc.shape[2]
+def message(kernel, smem, vmem, outs, width):
     return whole(
         kernel,
         [jax.ShapeDtypeStruct((*n, width), BF16) for n in outs],
-        2, 3, 4, (4 * 2 * 128 * 256 * 1024, 4),
+        len(smem), len(vmem), 4, (4 * 2 * 128 * 256 * 1024, 4),
         scratch_shapes=[VMEM((5, width // 2, width), F32)],
-    )(meta, orbs, near_blk, blk, acc)
+    )(*smem, *vmem)
 
 
 def exchange_kernel(meta_ref, near_blk, blk, keep_ref, send_ref):
@@ -232,7 +227,6 @@
 def base_kernel(meta_ref, orbs_ref, occ_ref, en_ref, amp_ref, own_ref,
                 early_ref, near_ref, keep_ref, recv_ref, out_ref):
     slots, rows, width = out_ref.shape
-    early = early_ref.shape[1]
     holder, core = meta_ref[0], meta_ref[1]
     row0 = pl.multiple_of(core * rows, rows)
 
@@ -252,9 +246,8 @@
         value += own_ref[p]
         value += keep_ref[both] * jnp.where(side == -step, 0.0, 1.0)
         value += recv_ref[both] * jnp.where(side == step, 0.0, 1.0)
-        lacking = near_ref[slots + index].astype(F32) * jnp.where(side == -step, 1.0, 0.0)
-        out_ref[p, :early] = value[:early] + early_ref[p].astype(F32) + lacking
-        out_ref[p, early:] = value[early:] + near_ref[p].astype(F32)
+        value += near_ref[index].astype(F32) * jnp.where(side == -step, 1.0, 0.0)
+        out_ref[p] = value + early_ref[p].astype(F32)
 
 
 def base(meta, orbs, occ, energy, amplitudes, own, early, near, keep, recv):
@@ -325,19 +318,18 @@
     meta = jnp.stack([holder, core])
     rel = lax.dynamic_slice_in_dim(couple_target, holder * pairs, pairs, 0).T - holder * pairs
     weights = lax.dynamic_slice_in_dim(couple_weight, holder * pairs, pairs, 0).T
-    rows, early_rows = width // 2, width // 4
-    acc_near, acc_far, msg_early = coupling(
-        meta, rel, weights, amplitudes, margins, rows, early_rows)
+    rows = width // 2
+    acc_far, msg_early = coupling(
+        meta, rel, weights, amplitudes, margins, rows, rows)
     early = lax.ppermute(msg_early, AXES, straight_out)
 
     chunks = [pairs * 3 // 4, pairs - pairs * 3 // 4]
     msg_near, = message(
-        near_kernel, meta, near_orbs, near_blk, blocks, acc_near,
-        [(pairs + 4, rows - early_rows)])
+        near_kernel, [meta], [near_blk, blocks], [(4, rows)], width)
     near = lax.ppermute(msg_near, AXES, straight_out)
     msg_far = message(
-        far_kernel, meta, near_orbs, near_blk, blocks, acc_far,
-        [(n, rows) for n in chunks])
+        far_kernel, [meta, near_orbs], [near_blk, blocks, acc_far],
+        [(n, rows) for n in chunks], width)
     far = lax.ppermute(msg_far[0], AXES, cross_out)
     last = lax.ppermute(msg_far[1], AXES, cross_out)
 

time: 72.4 us -> 68.2 us (0.942)
  waiting for transfers between devices: 18.3 us -> 11.5 us
  starting transfers between devices: 30.5 us -> 34.6 us
  local copies, waits for them, and re-layouts: 1.34 us -> 0.11 us
    ppermute x1, waiting for transfers between devices: 8.7 us -> 0.01 us  [local(): early = lax.ppermute(msg_early, AXES, straight_out)]
    ppermute x1, starting transfers between devices: 2.92 us -> 8.49 us  [local(): near_orbs = lax.ppermute(orbs, AXES, straight_in)]
    ppermute x1, starting transfers between devices: 3.96 us -> 1.92 us  [local(): early = lax.ppermute(msg_early, AXES, straight_out)]
    ppermute x1, waiting for transfers between devices: 0.01 us -> 1.28 us  [local(): near_orbs = lax.ppermute(orbs, AXES, straight_in)]
    ppermute x1, waiting for transfers between devices: 0.01 us -> 1.24 us  [local(): near = lax.ppermute(msg_near, AXES, straight_out)]
    unnamed x16 -> x14, local copies, waits for them, and re-layouts: 1.26 us -> 0.04 us
  transfers between devices with their start and end apart: 7 -> 7, of which waited for: 2 -> 3; matrix products, arithmetic and copies ran while one was open for 1% -> 1% of each run, Pallas kernels for 27% -> 28%
where the time goes in v5:
time: 68.2 us; the launch traced here: 67.8 us
  starting transfers between devices  34.6 us (51%)
  Pallas kernels  20.5 us (30%)
  waiting for transfers between devices  11.5 us (17%)
  other arithmetic  0.83 us (1%)
    pallas_call x2, Pallas kernels, coupling(): pl.pallas_call(functools.partial(coupling_kernel, early), out_shape=out_s...  10.4 us
    ppermute x1, starting transfers between devices, local(): near_blk = lax.ppermute(blocks, AXES, straight_in)  10.3 us
    ppermute x1, starting transfers between devices, local(): last = lax.ppermute(msg_far[1], AXES, cross_out)  9.85 us
    ppermute x1, waiting for transfers between devices, local(): near_blk = lax.ppermute(blocks, AXES, straight_in)  8.98 us
    ppermute x1, starting transfers between devices, local(): near_orbs = lax.ppermute(orbs, AXES, straight_in)  8.49 us
    pallas_call x2, Pallas kernels, final(): pl.pallas_call(kernel, out_shape=jax.ShapeDtypeStruct(base_terms.shape, F...  3.21 us
    pallas_call x1, Pallas kernels, base(): whole(base_kernel, jax.ShapeDtypeStruct(own.shape, F32), 3, 7, 4, (16 * 1...  2.58 us
    pallas_call x2, Pallas kernels, message(): whole(kernel, [jax.ShapeDtypeStruct((*n, width), BF16) for n in outs], le...  2.43 us
  transfers between devices with their start and end apart: 7, of which 3 were waited for; matrix products, arithmetic and copies ran while one was open for 1% of the time, Pallas kernels for 28%

profile of v5, /device:TPU:24, one launch (start us, length us, event | category | flops | bytes accessed | tf_op | source)
XLA Modules:
  0.0 67.8 jit_solution(16449167428519483514)
XLA Ops:
  0.0 0.0 copy-start
  0.0 10.3 %collective-permute-start.1 = (bf16[2,1024,256]{2,1,0:T(8,128)(2,1)}, bf16[2,1024,256]{2,1,0:T(8,128)(2,1)S(1)}, u32[]{:S(2)}, u32[]{:S(2)}) collective-permute-start(bf16[2,1024,256]{2,1,0:T(8,128)(2,1)} %blk.5), channel_id=1, source_target_pairs={{1,3},{2,0},{3,5},{4,2},{5,7},{6,4},{7,9},{8,6},{9,11},{10,8},{11,... | collective-permute-start | bytes 3145736 | tf_op jit(solution)/shard_map/ppermute | solution.py:315
  10.3 0.1 pad_add_fusion.meta_ref.refs_0_
  10.4 0.8 %subtract_bitcast_fusion.rel_ref = s32[4,16]{1,0:T(4,128)S(1)} fusion(s32[2048,4]{0,1:T(4,128)} %param.14, s32[]{:T(128)S(6)} %select_n.4, s32[]{:T(128)S(6)} %mul.2), kind=kLoop, calls=%fused_computation.1 | loop fusion | flops 64 | bytes 520 | tf_op jit(solution)/shard_map/sub | solution.py:319
  11.1 0.0 copy-done
  11.1 0.1 dynamic-slice_bitcast_fusion.w_ref
  11.2 0.0 copy-start.2
  11.2 5.3 %shard_map.92 = (f32[16,128,256]{2,1,0:T(8,128)S(1)}, bf16[16,128,256]{2,1,0:T(8,128)(2,1)S(1)}) custom-call(s32[2]{0:T(128)S(1)} %pad_add_fusion.meta_ref.refs_0_, s32[4,16]{1,0:T(4,128)S(1)} %subtract_bitcast_fusion.rel_ref, f32[4,16]{1,0:T(4,128)S(1)} %dynamic-slice_bitcast_fusion.w_ref, bf16[16,256,256]{2,1,0:T(8,128)(2,1)} %amp_ref.1, ...), custom_call_target="tpu_custom_call" | custom-call | flops 738197504 | bytes 6291456 | tf_op jit(solution)/shard_map/pallas_call | solution.py:139
  16.5 0.0 copy-start.5
  16.5 1.9 %collective-permute-start = (bf16[16,128,256]{2,1,0:T(8,128)(2,1)S(1)}, bf16[16,128,256]{2,1,0:T(8,128)(2,1)S(1)}, u32[]{:S(2)}, u32[]{:S(2)}) collective-permute-start(bf16[16,128,256]{2,1,0:T(8,128)(2,1)S(1)} %get-tuple-element.11), channel_id=1, source_target_pairs={{0,2},{2,4},{3,1},{4,6},{5,3},{6,8},{7,5},{8,10},{9,7},{10,12},{11... | collective-permute-start | bytes 3145736 | tf_op jit(solution)/shard_map/ppermute | solution.py:324
  18.4 9.0 %collective-permute-done.1.near_blk = bf16[2,1024,256]{2,1,0:T(8,128)(2,1)S(1)} collective-permute-done((bf16[2,1024,256]{2,1,0:T(8,128)(2,1)}, bf16[2,1024,256]{2,1,0:T(8,128)(2,1)S(1)}, u32[]{:S(2)}, u32[]{:S(2)}) %collective-permute-start.1) | collective-permute-done | bytes 1048608 | tf_op jit(solution)/shard_map/ppermute | solution.py:315
  27.4 0.0 copy-done.2
  27.4 1.9 %shard_map.94 = (f32[8,128,256]{2,1,0:T(8,128)S(1)}, f32[8,128,256]{2,1,0:T(8,128)S(1)}) custom-call(s32[2]{0:T(128)S(1)} %pad_add_fusion.meta_ref.refs_0_, bf16[2,1024,256]{2,1,0:T(8,128)(2,1)S(1)} %collective-permute-done.1.near_blk, bf16[2,1024,256]{2,1,0:T(8,128)(2,1)S(1)} %copy-done.2), custom_call_target="tpu_custom_call" | custom-call | flops 1073741824 | bytes 4194304 | tf_op jit(solution)/shard_map/pallas_call | solution.py:222
  29.3 0.1 collective-permute-start.3
  29.4 0.0 copy-done.5
  29.4 8.5 %collective-permute-start.4 = (s32[2,16]{1,0:T(2,128)S(1)}, s32[2,16]{1,0:T(2,128)S(1)}, u32[]{:S(2)}, u32[]{:S(2)}) collective-permute-start(s32[2,16]{1,0:T(2,128)S(1)} %bitcast.7), channel_id=1, source_target_pairs={{1,3},{2,0},{3,5},{4,2},{5,7},{6,4},{7,9},{8,6},{9,11},{10,8},{11,... | collective-permute-start | bytes 392 | tf_op jit(solution)/shard_map/ppermute | solution.py:316
  37.9 1.3 %collective-permute-done.4.orbs_ref = s32[2,16]{1,0:T(2,128)S(1)} collective-permute-done((s32[2,16]{1,0:T(2,128)S(1)}, s32[2,16]{1,0:T(2,128)S(1)}, u32[]{:S(2)}, u32[]{:S(2)}) %collective-permute-start.4) | collective-permute-done | bytes 160 | tf_op jit(solution)/shard_map/ppermute | solution.py:316
  39.2 1.4 %shard_map.96 = (bf16[12,128,256]{2,1,0:T(8,128)(2,1)S(1)}, bf16[4,128,256]{2,1,0:T(8,128)(2,1)S(1)}) custom-call(s32[2]{0:T(128)S(1)} %pad_add_fusion.meta_ref.refs_0_, s32[2,16]{1,0:T(2,128)S(1)} %collective-permute-done.4.orbs_ref, bf16[2,1024,256]{2,1,0:T(8,128)(2,1)S(1)} %collective-permute-done.1.near_blk, bf16[2,1024,256]{2,1,0:T(8,128)(2,1)S(1)} %copy-done.2, ...), custom_call_target="tpu_custom_call" | custom-call | flops 268435456 | bytes 4194304 | tf_op jit(solution)/shard_map/pallas_call | solution.py:200
  40.6 0.0 copy-start.1
  40.6 2.1 %collective-permute-start.6 = (bf16[12,128,256]{2,1,0:T(8,128)(2,1)S(1)}, bf16[12,128,256]{2,1,0:T(8,128)(2,1)S(1)}, u32[]{:S(2)}, u32[]{:S(2)}) collective-permute-start(bf16[12,128,256]{2,1,0:T(8,128)(2,1)S(1)} %get-tuple-element.16), channel_id=1, source_target_pairs={{0,3},{2,5},{3,0},{4,7},{5,2},{6,9},{7,4},{8,11},{9,6},{10,13},{11... | collective-permute-start | bytes 2359304 | tf_op jit(solution)/shard_map/ppermute | solution.py:333
  42.7 1.0 %shard_map.93 = bf16[4,128,256]{2,1,0:T(8,128)(2,1)S(1)} custom-call(s32[2]{0:T(128)S(1)} %pad_add_fusion.meta_ref.refs_0_, bf16[2,1024,256]{2,1,0:T(8,128)(2,1)S(1)} %collective-permute-done.1.near_blk, bf16[2,1024,256]{2,1,0:T(8,128)(2,1)S(1)} %copy-done.2), custom_call_target="tpu_custom_call" | custom-call | flops 268435456 | bytes 4194304 | tf_op jit(solution)/shard_map/pallas_call | solution.py:200
  43.7 1.9 %collective-permute-start.2 = (bf16[4,128,256]{2,1,0:T(8,128)(2,1)S(1)}, bf16[4,128,256]{2,1,0:T(8,128)(2,1)S(1)}, u32[]{:S(2)}, u32[]{:S(2)}) collective-permute-start(bf16[4,128,256]{2,1,0:T(8,128)(2,1)S(1)} %shard_map.93), channel_id=1, source_target_pairs={{0,2},{2,4},{3,1},{4,6},{5,3},{6,8},{7,5},{8,10},{9,7},{10,12},{11... | collective-permute-start | bytes 786440 | tf_op jit(solution)/shard_map/ppermute | solution.py:329
  45.6 0.0 copy-start.3
  45.6 0.0 copy-start.6
  45.7 9.9 %collective-permute-start.5 = (bf16[4,128,256]{2,1,0:T(8,128)(2,1)S(1)}, bf16[4,128,256]{2,1,0:T(8,128)(2,1)S(1)}, u32[]{:S(2)}, u32[]{:S(2)}) collective-permute-start(bf16[4,128,256]{2,1,0:T(8,128)(2,1)S(1)} %get-tuple-element.15), channel_id=1, source_target_pairs={{0,3},{2,5},{3,0},{4,7},{5,2},{6,9},{7,4},{8,11},{9,6},{10,13},{11... | collective-permute-start | bytes 786440 | tf_op jit(solution)/shard_map/ppermute | solution.py:334
  55.5 0.0 copy-done.1
  55.5 5.1 %shard_map.91.own_ref = f32[16,128,256]{2,1,0:T(8,128)S(1)} custom-call(s32[2]{0:T(128)S(1)} %pad_add_fusion.meta_ref.refs_0_, s32[4,16]{1,0:T(4,128)S(1)} %subtract_bitcast_fusion.rel_ref, f32[4,16]{1,0:T(4,128)S(1)} %dynamic-slice_bitcast_fusion.w_ref, bf16[16,256,256]{2,1,0:T(8,128)(2,1)S(1)} %copy-done.1, bf16[16,4,256,256]{3,2,1,0:T(8,128)(2,1)} %mar_hbm.3), custom_call_target="tpu_custom_call" | custom-call | flops 738197504 | bytes 6291456 | tf_op jit(solution)/shard_map/pallas_call | solution.py:139
  60.7 0.0 collective-permute-done.early_ref
  60.7 1.2 %collective-permute-done.2.near_ref = bf16[4,128,256]{2,1,0:T(8,128)(2,1)S(1)} collective-permute-done((bf16[4,128,256]{2,1,0:T(8,128)(2,1)S(1)}, bf16[4,128,256]{2,1,0:T(8,128)(2,1)S(1)}, u32[]{:S(2)}, u32[]{:S(2)}) %collective-permute-start.2) | collective-permute-done | bytes 262176 | tf_op jit(solution)/shard_map/ppermute | solution.py:329
  61.9 0.0 collective-permute-done.3.recv_ref
  61.9 0.0 copy-done.3
  61.9 0.0 copy-done.6
  61.9 0.0 copy-start.4
  61.9 2.6 %shard_map.95.refs_2_ = f32[16,128,256]{2,1,0:T(8,128)S(1)} custom-call(s32[2]{0:T(128)S(1)} %pad_add_fusion.meta_ref.refs_0_, s32[2,16]{1,0:T(2,128)S(1)} %bitcast.8, f32[256]{0:T(256)S(1)} %copy-done.6, f32[16,256]{1,0:T(8,128)S(1)} %copy-done.3, bf16[16,256,256]{2,1,0:T(8,128)(2,1)S(1)} %copy-done.1, f32[16,128,256]{2,1,0:T(8,128)S(1)} %shard_map.91.own_ref, ...), custom_call_target="tpu_custom_call" | custom-call | flops 4194304 | bytes 8388608 | tf_op jit(solution)/shard_map/pallas_call | solution.py:254
  64.5 0.0 collective-permute-done.6.refs_3_
  64.5 0.0 copy-done.4
  64.5 1.8 %shard_map.97.refs_4_ = f32[16,128,256]{2,1,0:T(8,128)} custom-call(s32[2]{0:T(128)S(1)} %pad_add_fusion.meta_ref.refs_0_, s32[16]{0:T(128)S(1)} %copy-done.4, f32[16,128,256]{2,1,0:T(8,128)S(1)} %shard_map.95.refs_2_, bf16[12,128,256]{2,1,0:T(8,128)(2,1)S(1)} %collective-permute-done.6.refs_3_), custom_call_target="tpu_custom_call" | custom-call | flops 786432 | bytes 3145728 | tf_op jit(solution)/shard_map/pallas_call | solution.py:290
  66.3 0.0 collective-permute-done.5.refs_3_
  66.4 1.4 %shard_map.98 = f32[16,128,256]{2,1,0:T(8,128)} custom-call(s32[2]{0:T(128)S(1)} %pad_add_fusion.meta_ref.refs_0_, s32[16]{0:T(128)S(1)} %copy-done.4, f32[16,128,256]{2,1,0:T(8,128)S(1)} %shard_map.95.refs_2_, bf16[4,128,256]{2,1,0:T(8,128)(2,1)S(1)} %collective-permute-done.5.refs_3_, ...), custom_call_target="tpu_custom_call", output_to_operand_aliasing={{}: (4, {})} | custom-call | flops 262144 | bytes 1048576 | tf_op jit(solution)/shard_map/pallas_call | solution.py:290
Async XLA Ops:
  0.0 11.1 %copy-start = (f32[2048,4]{0,1:T(4,128)S(1)}, f32[2048,4]{0,1:T(4,128)}, u32[]{:S(2)}) copy-start(f32[2048,4]{0,1:T(4,128)} %param.15) | copy-start | bytes 98308
  0.0 27.4 %collective-permute-start.1 = (bf16[2,1024,256]{2,1,0:T(8,128)(2,1)}, bf16[2,1024,256]{2,1,0:T(8,128)(2,1)S(1)}, u32[]{:S(2)}, u32[]{:S(2)}) collective-permute-start(bf16[2,1024,256]{2,1,0:T(8,128)(2,1)} %blk.5), channel_id=1, source_target_pairs={{1,3},{2,0},{3,5},{4,2},{5,7},{6,4},{7,9},{8,6},{9,11},{10,8},{11,... | collective-permute-start | bytes 3145736 | tf_op jit(solution)/shard_map/ppermute | solution.py:315
  11.2 16.2 %copy-start.2 = (bf16[2,1024,256]{2,1,0:T(8,128)(2,1)S(1)}, bf16[2,1024,256]{2,1,0:T(8,128)(2,1)}, u32[]{:S(2)}) copy-start(bf16[2,1024,256]{2,1,0:T(8,128)(2,1)} %blk.5) | copy-start | bytes 3145732
  16.5 12.9 %copy-start.5 = (s32[16,2]{0,1:T(2,128)S(1)}, s32[16,2]{0,1:T(2,128)}, u32[]{:S(2)}) copy-start(s32[16,2]{0,1:T(2,128)} %param.10) | copy-start | bytes 388
  16.5 44.2 %collective-permute-start = (bf16[16,128,256]{2,1,0:T(8,128)(2,1)S(1)}, bf16[16,128,256]{2,1,0:T(8,128)(2,1)S(1)}, u32[]{:S(2)}, u32[]{:S(2)}) collective-permute-start(bf16[16,128,256]{2,1,0:T(8,128)(2,1)S(1)} %get-tuple-element.11), channel_id=1, source_target_pairs={{0,2},{2,4},{3,1},{4,6},{5,3},{6,8},{7,5},{8,10},{9,7},{10,12},{11... | collective-permute-start | bytes 3145736 | tf_op jit(solution)/shard_map/ppermute | solution.py:324
  29.3 32.6 %collective-permute-start.3 = (f32[8,128,256]{2,1,0:T(8,128)S(1)}, f32[8,128,256]{2,1,0:T(8,128)S(1)}, u32[]{:S(2)}, u32[]{:S(2)}) collective-permute-start(f32[8,128,256]{2,1,0:T(8,128)S(1)} %get-tuple-element.13), channel_id=1, source_target_pairs={{0,1},{1,0},{2,3},{3,2},{4,5},{5,4},{6,7},{7,6},{8,9},{9,8},{10,11... | collective-permute-start | bytes 3145736 | tf_op jit(solution)/shard_map/ppermute | solution.py:337
  29.4 9.8 %collective-permute-start.4 = (s32[2,16]{1,0:T(2,128)S(1)}, s32[2,16]{1,0:T(2,128)S(1)}, u32[]{:S(2)}, u32[]{:S(2)}) collective-permute-start(s32[2,16]{1,0:T(2,128)S(1)} %bitcast.7), channel_id=1, source_target_pairs={{1,3},{2,0},{3,5},{4,2},{5,7},{6,4},{7,9},{8,6},{9,11},{10,8},{11,... | collective-permute-start | bytes 392 | tf_op jit(solution)/shard_map/ppermute | solution.py:316
  40.6 14.9 %copy-start.1 = (bf16[16,256,256]{2,1,0:T(8,128)(2,1)S(1)}, bf16[16,256,256]{2,1,0:T(8,128)(2,1)}, u32[]{:S(2)}) copy-start(bf16[16,256,256]{2,1,0:T(8,128)(2,1)} %amp_ref.1) | copy-start | bytes 6291460
  40.6 23.9 %collective-permute-start.6 = (bf16[12,128,256]{2,1,0:T(8,128)(2,1)S(1)}, bf16[12,128,256]{2,1,0:T(8,128)(2,1)S(1)}, u32[]{:S(2)}, u32[]{:S(2)}) collective-permute-start(bf16[12,128,256]{2,1,0:T(8,128)(2,1)S(1)} %get-tuple-element.16), channel_id=1, source_target_pairs={{0,3},{2,5},{3,0},{4,7},{5,2},{6,9},{7,4},{8,11},{9,6},{10,13},{11... | collective-permute-start | bytes 2359304 | tf_op jit(solution)/shard_map/ppermute | solution.py:333
  43.7 18.2 %collective-permute-start.2 = (bf16[4,128,256]{2,1,0:T(8,128)(2,1)S(1)}, bf16[4,128,256]{2,1,0:T(8,128)(2,1)S(1)}, u32[]{:S(2)}, u32[]{:S(2)}) collective-permute-start(bf16[4,128,256]{2,1,0:T(8,128)(2,1)S(1)} %shard_map.93), channel_id=1, source_target_pairs={{0,2},{2,4},{3,1},{4,6},{5,3},{6,8},{7,5},{8,10},{9,7},{10,12},{11... | collective-permute-start | bytes 786440 | tf_op jit(solution)/shard_map/ppermute | solution.py:329
  45.6 16.3 %copy-start.3 = (f32[16,256]{1,0:T(8,128)S(1)}, f32[16,256]{1,0:T(8,128)}, u32[]{:S(2)}) copy-start(f32[16,256]{1,0:T(8,128)} %en_ref.1) | copy-start | bytes 49156
  45.6 16.3 %copy-start.6 = (f32[256]{0:T(256)S(1)}, f32[256]{0:T(256)}, u32[]{:S(2)}) copy-start(f32[256]{0:T(256)} %occ_ref.1) | copy-start | bytes 3076
  45.7 20.7 %collective-permute-start.5 = (bf16[4,128,256]{2,1,0:T(8,128)(2,1)S(1)}, bf16[4,128,256]{2,1,0:T(8,128)(2,1)S(1)}, u32[]{:S(2)}, u32[]{:S(2)}) collective-permute-start(bf16[4,128,256]{2,1,0:T(8,128)(2,1)S(1)} %get-tuple-element.15), channel_id=1, source_target_pairs={{0,3},{2,5},{3,0},{4,7},{5,2},{6,9},{7,4},{8,11},{9,6},{10,13},{11... | collective-permute-start | bytes 786440 | tf_op jit(solution)/shard_map/ppermute | solution.py:334
  61.9 2.6 %copy-start.4 = (s32[16]{0:T(128)S(1)}, s32[16]{0:T(128)}, u32[]{:S(2)}) copy-start(s32[16]{0:T(128)} %refs_1_.3) | copy-start | bytes 196

commit v6 on v5

--- a/solution.py
+++ b/solution.py
@@ -225,7 +225,7 @@
 
 
 def base_kernel(meta_ref, orbs_ref, occ_ref, en_ref, amp_ref, own_ref,
-                early_ref, near_ref, keep_ref, recv_ref, out_ref):
+                early_ref, keep_ref, recv_ref, out_ref):
     slots, rows, width = out_ref.shape
     holder, core = meta_ref[0], meta_ref[1]
     row0 = pl.multiple_of(core * rows, rows)
@@ -246,17 +246,16 @@
         value += own_ref[p]
         value += keep_ref[both] * jnp.where(side == -step, 0.0, 1.0)
         value += recv_ref[both] * jnp.where(side == step, 0.0, 1.0)
-        value += near_ref[index].astype(F32) * jnp.where(side == -step, 1.0, 0.0)
         out_ref[p] = value + early_ref[p].astype(F32)
 
 
-def base(meta, orbs, occ, energy, amplitudes, own, early, near, keep, recv):
+def base(meta, orbs, occ, energy, amplitudes, own, early, keep, recv):
     return whole(
-        base_kernel, jax.ShapeDtypeStruct(own.shape, F32), 3, 7, 4, (16 * 128 * 256 * 8, 8),
-    )(meta, orbs, occ, energy, amplitudes, own, early, near, keep, recv)
-
-
-def final_kernel(start, meta_ref, count_ref, base_ref, far_ref, *rest):
+        base_kernel, jax.ShapeDtypeStruct(own.shape, F32), 3, 6, 4, (16 * 128 * 256 * 8, 8),
+    )(meta, orbs, occ, energy, amplitudes, own, early, keep, recv)
+
+
+def final_kernel(start, meta_ref, count_ref, orbs_ref, base_ref, far_ref, near_ref, *rest):
     out_hbm, buf, sem = rest[-3:]
     slots, rows, width = far_ref.shape
     row = lax.broadcasted_iota(jnp.int32, (rows, width), 0) + meta_ref[1] * rows
@@ -268,7 +267,11 @@
 
     @pl.loop(0, slots)
     def _(s):
+        first, second = orbs_ref[0, start + s], orbs_ref[1, start + s]
+        lacks = second // 2 - meta_ref[0] == 2 * meta_ref[1] - 1
+        product = near_ref[2 * (first % 2) + second % 2].astype(F32)
         value = base_ref[start + s] + far_ref[s].astype(F32)
+        value += product * jnp.where(lacks, 1.0, 0.0)
         buf[s] = jnp.where(most < count_ref[start + s], value, 0.0)
         put(s).start()
 
@@ -277,7 +280,7 @@
         put(s).wait()
 
 
-def final(start, meta, count, base_terms, far, earlier=None):
+def final(start, meta, count, orbs, base_terms, far, near, earlier=None):
     slots, rows, width = far.shape
     smem = pl.BlockSpec(memory_space=SMEM)
     vmem = pl.BlockSpec(memory_space=VMEM)
@@ -290,14 +293,14 @@
     return pl.pallas_call(
         kernel,
         out_shape=jax.ShapeDtypeStruct(base_terms.shape, F32),
-        in_specs=[smem, smem, vmem, vmem] + [hbm] * len(more),
+        in_specs=[smem] * 3 + [vmem] * 3 + [hbm] * len(more),
         out_specs=hbm,
         scratch_shapes=[VMEM((slots, rows, width), F32), pltpu.SemaphoreType.DMA((slots,))],
-        input_output_aliases={4: 0} if more else {},
+        input_output_aliases={6: 0} if more else {},
         compiler_params=pltpu.CompilerParams(vmem_limit_bytes=4 * MIB),
         cost_estimate=pl.CostEstimate(
             flops=slots * 128 * 256 * 2, bytes_accessed=slots * MIB // 4, transcendentals=0),
-    )(meta, count, base_terms, far, *more)
+    )(meta, count, orbs, base_terms, far, near, *more)
 
 
 def local(blocks, pair_orbs, pno_count, amplitudes, margins, couple_target, couple_weight,
@@ -336,10 +339,9 @@
     keep, send = exchange(meta, near_blk, blocks)
     recv = lax.ppermute(send, AXES, swap)
     own, = coupling(meta, rel, weights, amplitudes, margins, rows, 0)
-    base_terms = base(meta, orbs, occ_energy, pno_energy, amplitudes, own, early, near,
-                      keep, recv)
-    out = final(0, meta, pno_count, base_terms, far)
-    return final(chunks[0], meta, pno_count, base_terms, last, out)
+    base_terms = base(meta, orbs, occ_energy, pno_energy, amplitudes, own, early, keep, recv)
+    out = final(0, meta, pno_count, orbs, base_terms, far, near)
+    return final(chunks[0], meta, pno_count, orbs, base_terms, last, near, out)
 
 
 def solution(mesh):

time: 68.2 us -> 66.9 us (0.981)
  waiting for transfers between devices: 11.5 us -> 10.3 us
    ppermute x1, waiting for transfers between devices: 1.24 us -> 0.01 us  [local(): near = lax.ppermute(msg_near, AXES, straight_out)]
  transfers between devices with their start and end apart: 7 -> 7, of which waited for: 3 -> 2; matrix products, arithmetic and copies ran while one was open for 1% -> 1% of each run, Pallas kernels for 28% -> 29%
where the time goes in v6:
time: 66.9 us; the launch traced here: 66.5 us
  starting transfers between devices  34.6 us (52%)
  Pallas kernels  20.5 us (31%)
  waiting for transfers between devices  10.3 us (15%)
  other arithmetic  0.83 us (1%)
    pallas_call x2, Pallas kernels, coupling(): pl.pallas_call(functools.partial(coupling_kernel, early), out_shape=out_s...  10.4 us
    ppermute x1, starting transfers between devices, local(): near_blk = lax.ppermute(blocks, AXES, straight_in)  10.3 us
    ppermute x1, starting transfers between devices, local(): last = lax.ppermute(msg_far[1], AXES, cross_out)  9.85 us
    ppermute x1, waiting for transfers between devices, local(): near_blk = lax.ppermute(blocks, AXES, straight_in)  8.98 us
    ppermute x1, starting transfers between devices, local(): near_orbs = lax.ppermute(orbs, AXES, straight_in)  8.49 us
    pallas_call x2, Pallas kernels, final(): pl.pallas_call(kernel, out_shape=jax.ShapeDtypeStruct(base_terms.shape, F...  3.28 us
    pallas_call x1, Pallas kernels, base(): whole(base_kernel, jax.ShapeDtypeStruct(own.shape, F32), 3, 6, 4, (16 * 1...  2.48 us
    pallas_call x2, Pallas kernels, message(): whole(kernel, [jax.ShapeDtypeStruct((*n, width), BF16) for n in outs], le...  2.43 us
  transfers between devices with their start and end apart: 7, of which 2 were waited for; matrix products, arithmetic and copies ran while one was open for 1% of the time, Pallas kernels for 29%

profile of v6, /device:TPU:24, one launch (start us, length us, event | category | flops | bytes accessed | tf_op | source)
XLA Modules:
  0.0 66.5 jit_solution(12432729097933253858)
XLA Ops:
  0.0 0.0 copy-start
  0.0 10.3 %collective-permute-start.1 = (bf16[2,1024,256]{2,1,0:T(8,128)(2,1)}, bf16[2,1024,256]{2,1,0:T(8,128)(2,1)S(1)}, u32[]{:S(2)}, u32[]{:S(2)}) collective-permute-start(bf16[2,1024,256]{2,1,0:T(8,128)(2,1)} %blk.5), channel_id=1, source_target_pairs={{1,3},{2,0},{3,5},{4,2},{5,7},{6,4},{7,9},{8,6},{9,11},{10,8},{11,... | collective-permute-start | bytes 3145736 | tf_op jit(solution)/shard_map/ppermute | solution.py:318
  10.3 0.1 pad_add_fusion.meta_ref.refs_0_
  10.4 0.8 %subtract_bitcast_fusion.rel_ref = s32[4,16]{1,0:T(4,128)S(1)} fusion(s32[2048,4]{0,1:T(4,128)} %param.14, s32[]{:T(128)S(6)} %select_n.4, s32[]{:T(128)S(6)} %mul.2), kind=kLoop, calls=%fused_computation.1 | loop fusion | flops 64 | bytes 520 | tf_op jit(solution)/shard_map/sub | solution.py:322
  11.1 0.0 copy-done
  11.1 0.1 dynamic-slice_bitcast_fusion.w_ref
  11.2 0.0 copy-start.2
  11.2 5.3 %shard_map.92 = (f32[16,128,256]{2,1,0:T(8,128)S(1)}, bf16[16,128,256]{2,1,0:T(8,128)(2,1)S(1)}) custom-call(s32[2]{0:T(128)S(1)} %pad_add_fusion.meta_ref.refs_0_, s32[4,16]{1,0:T(4,128)S(1)} %subtract_bitcast_fusion.rel_ref, f32[4,16]{1,0:T(4,128)S(1)} %dynamic-slice_bitcast_fusion.w_ref, bf16[16,256,256]{2,1,0:T(8,128)(2,1)} %amp_ref.1, ...), custom_call_target="tpu_custom_call" | custom-call | flops 738197504 | bytes 6291456 | tf_op jit(solution)/shard_map/pallas_call | solution.py:139
  16.5 0.0 copy-start.4
  16.5 1.9 %collective-permute-start = (bf16[16,128,256]{2,1,0:T(8,128)(2,1)S(1)}, bf16[16,128,256]{2,1,0:T(8,128)(2,1)S(1)}, u32[]{:S(2)}, u32[]{:S(2)}) collective-permute-start(bf16[16,128,256]{2,1,0:T(8,128)(2,1)S(1)} %get-tuple-element.11), channel_id=1, source_target_pairs={{0,2},{2,4},{3,1},{4,6},{5,3},{6,8},{7,5},{8,10},{9,7},{10,12},{11... | collective-permute-start | bytes 3145736 | tf_op jit(solution)/shard_map/ppermute | solution.py:327
  18.4 9.0 %collective-permute-done.1.near_blk = bf16[2,1024,256]{2,1,0:T(8,128)(2,1)S(1)} collective-permute-done((bf16[2,1024,256]{2,1,0:T(8,128)(2,1)}, bf16[2,1024,256]{2,1,0:T(8,128)(2,1)S(1)}, u32[]{:S(2)}, u32[]{:S(2)}) %collective-permute-start.1) | collective-permute-done | bytes 1048608 | tf_op jit(solution)/shard_map/ppermute | solution.py:318
  27.4 0.0 copy-done.2
  27.4 1.9 %shard_map.93 = (f32[8,128,256]{2,1,0:T(8,128)S(1)}, f32[8,128,256]{2,1,0:T(8,128)S(1)}) custom-call(s32[2]{0:T(128)S(1)} %pad_add_fusion.meta_ref.refs_0_, bf16[2,1024,256]{2,1,0:T(8,128)(2,1)S(1)} %collective-permute-done.1.near_blk, bf16[2,1024,256]{2,1,0:T(8,128)(2,1)S(1)} %copy-done.2), custom_call_target="tpu_custom_call" | custom-call | flops 1073741824 | bytes 4194304 | tf_op jit(solution)/shard_map/pallas_call | solution.py:222
  29.3 0.1 collective-permute-start.2
  29.4 0.0 copy-done.4
  29.4 8.5 %collective-permute-start.3 = (s32[2,16]{1,0:T(2,128)S(1)}, s32[2,16]{1,0:T(2,128)S(1)}, u32[]{:S(2)}, u32[]{:S(2)}) collective-permute-start(s32[2,16]{1,0:T(2,128)S(1)} %bitcast.7), channel_id=1, source_target_pairs={{1,3},{2,0},{3,5},{4,2},{5,7},{6,4},{7,9},{8,6},{9,11},{10,8},{11,... | collective-permute-start | bytes 392 | tf_op jit(solution)/shard_map/ppermute | solution.py:319
  37.9 1.3 %collective-permute-done.3.orbs_ref = s32[2,16]{1,0:T(2,128)S(1)} collective-permute-done((s32[2,16]{1,0:T(2,128)S(1)}, s32[2,16]{1,0:T(2,128)S(1)}, u32[]{:S(2)}, u32[]{:S(2)}) %collective-permute-start.3) | collective-permute-done | bytes 160 | tf_op jit(solution)/shard_map/ppermute | solution.py:319
  39.2 1.4 %shard_map.95 = (bf16[12,128,256]{2,1,0:T(8,128)(2,1)S(1)}, bf16[4,128,256]{2,1,0:T(8,128)(2,1)S(1)}) custom-call(s32[2]{0:T(128)S(1)} %pad_add_fusion.meta_ref.refs_0_, s32[2,16]{1,0:T(2,128)S(1)} %collective-permute-done.3.orbs_ref, bf16[2,1024,256]{2,1,0:T(8,128)(2,1)S(1)} %collective-permute-done.1.near_blk, bf16[2,1024,256]{2,1,0:T(8,128)(2,1)S(1)} %copy-done.2, ...), custom_call_target="tpu_custom_call" | custom-call | flops 268435456 | bytes 4194304 | tf_op jit(solution)/shard_map/pallas_call | solution.py:200
  40.6 0.0 copy-start.1
  40.6 2.1 %collective-permute-start.6 = (bf16[12,128,256]{2,1,0:T(8,128)(2,1)S(1)}, bf16[12,128,256]{2,1,0:T(8,128)(2,1)S(1)}, u32[]{:S(2)}, u32[]{:S(2)}) collective-permute-start(bf16[12,128,256]{2,1,0:T(8,128)(2,1)S(1)} %get-tuple-element.16), channel_id=1, source_target_pairs={{0,3},{2,5},{3,0},{4,7},{5,2},{6,9},{7,4},{8,11},{9,6},{10,13},{11... | collective-permute-start | bytes 2359304 | tf_op jit(solution)/shard_map/ppermute | solution.py:336
  42.7 1.0 %shard_map.96 = bf16[4,128,256]{2,1,0:T(8,128)(2,1)S(1)} custom-call(s32[2]{0:T(128)S(1)} %pad_add_fusion.meta_ref.refs_0_, bf16[2,1024,256]{2,1,0:T(8,128)(2,1)S(1)} %collective-permute-done.1.near_blk, bf16[2,1024,256]{2,1,0:T(8,128)(2,1)S(1)} %copy-done.2), custom_call_target="tpu_custom_call" | custom-call | flops 268435456 | bytes 4194304 | tf_op jit(solution)/shard_map/pallas_call | solution.py:200
  43.7 1.9 %collective-permute-start.5 = (bf16[4,128,256]{2,1,0:T(8,128)(2,1)S(1)}, bf16[4,128,256]{2,1,0:T(8,128)(2,1)S(1)}, u32[]{:S(2)}, u32[]{:S(2)}) collective-permute-start(bf16[4,128,256]{2,1,0:T(8,128)(2,1)S(1)} %shard_map.96), channel_id=1, source_target_pairs={{0,2},{2,4},{3,1},{4,6},{5,3},{6,8},{7,5},{8,10},{9,7},{10,12},{11... | collective-permute-start | bytes 786440 | tf_op jit(solution)/shard_map/ppermute | solution.py:332
  45.6 0.0 copy-start.3
  45.6 0.0 copy-start.6
  45.7 9.9 %collective-permute-start.4 = (bf16[4,128,256]{2,1,0:T(8,128)(2,1)S(1)}, bf16[4,128,256]{2,1,0:T(8,128)(2,1)S(1)}, u32[]{:S(2)}, u32[]{:S(2)}) collective-permute-start(bf16[4,128,256]{2,1,0:T(8,128)(2,1)S(1)} %get-tuple-element.15), channel_id=1, source_target_pairs={{0,3},{2,5},{3,0},{4,7},{5,2},{6,9},{7,4},{8,11},{9,6},{10,13},{11... | collective-permute-start | bytes 786440 | tf_op jit(solution)/shard_map/ppermute | solution.py:337
  55.5 0.0 copy-done.1
  55.5 5.1 %shard_map.91.own_ref = f32[16,128,256]{2,1,0:T(8,128)S(1)} custom-call(s32[2]{0:T(128)S(1)} %pad_add_fusion.meta_ref.refs_0_, s32[4,16]{1,0:T(4,128)S(1)} %subtract_bitcast_fusion.rel_ref, f32[4,16]{1,0:T(4,128)S(1)} %dynamic-slice_bitcast_fusion.w_ref, bf16[16,256,256]{2,1,0:T(8,128)(2,1)S(1)} %copy-done.1, bf16[16,4,256,256]{3,2,1,0:T(8,128)(2,1)} %mar_hbm.3), custom_call_target="tpu_custom_call" | custom-call | flops 738197504 | bytes 6291456 | tf_op jit(solution)/shard_map/pallas_call | solution.py:139
  60.7 0.0 collective-permute-done.early_ref
  60.7 0.0 collective-permute-done.2.recv_ref
  60.7 0.0 copy-done.3
  60.7 0.0 copy-done.6
  60.7 0.0 copy-start.5
  60.7 2.5 %shard_map.94.refs_3_ = f32[16,128,256]{2,1,0:T(8,128)S(1)} custom-call(s32[2]{0:T(128)S(1)} %pad_add_fusion.meta_ref.refs_0_, s32[2,16]{1,0:T(2,128)S(1)} %bitcast.8, f32[256]{0:T(256)S(1)} %copy-done.6, f32[16,256]{1,0:T(8,128)S(1)} %copy-done.3, bf16[16,256,256]{2,1,0:T(8,128)(2,1)S(1)} %copy-done.1, f32[16,128,256]{2,1,0:T(8,128)S(1)} %shard_map.91.own_ref, ...), custom_call_target="tpu_custom_call" | custom-call | flops 4194304 | bytes 8388608 | tf_op jit(solution)/shard_map/pallas_call | solution.py:253
  63.2 0.0 collective-permute-done.5.refs_5_
  63.2 0.0 collective-permute-done.6.refs_4_
  63.2 0.0 copy-done.5
  63.2 1.8 %shard_map.97.refs_6_ = f32[16,128,256]{2,1,0:T(8,128)} custom-call(s32[2]{0:T(128)S(1)} %pad_add_fusion.meta_ref.refs_0_, s32[16]{0:T(128)S(1)} %copy-done.5, s32[2,16]{1,0:T(2,128)S(1)} %bitcast.9, f32[16,128,256]{2,1,0:T(8,128)S(1)} %shard_map.94.refs_3_, bf16[12,128,256]{2,1,0:T(8,128)(2,1)S(1)} %collective-permute-done.6.refs_4_, ...), custom_call_target="tpu_custom_call" | custom-call | flops 786432 | bytes 3145728 | tf_op jit(solution)/shard_map/pallas_call | solution.py:293
  65.1 0.0 collective-permute-done.4.refs_4_
  65.1 1.4 %shard_map.98 = f32[16,128,256]{2,1,0:T(8,128)} custom-call(s32[2]{0:T(128)S(1)} %pad_add_fusion.meta_ref.refs_0_, s32[16]{0:T(128)S(1)} %copy-done.5, s32[2,16]{1,0:T(2,128)S(1)} %bitcast.10, f32[16,128,256]{2,1,0:T(8,128)S(1)} %shard_map.94.refs_3_, bf16[4,128,256]{2,1,0:T(8,128)(2,1)S(1)} %collective-permute-done.4.refs_4_, ...), custom_call_target="tpu_custom_call", output_to_operand_aliasing={{}: (6, {})} | custom-call | flops 262144 | bytes 1048576 | tf_op jit(solution)/shard_map/pallas_call | solution.py:293
Async XLA Ops:
  0.0 11.1 %copy-start = (f32[2048,4]{0,1:T(4,128)S(1)}, f32[2048,4]{0,1:T(4,128)}, u32[]{:S(2)}) copy-start(f32[2048,4]{0,1:T(4,128)} %param.15) | copy-start | bytes 98308
  0.0 27.4 %collective-permute-start.1 = (bf16[2,1024,256]{2,1,0:T(8,128)(2,1)}, bf16[2,1024,256]{2,1,0:T(8,128)(2,1)S(1)}, u32[]{:S(2)}, u32[]{:S(2)}) collective-permute-start(bf16[2,1024,256]{2,1,0:T(8,128)(2,1)} %blk.5), channel_id=1, source_target_pairs={{1,3},{2,0},{3,5},{4,2},{5,7},{6,4},{7,9},{8,6},{9,11},{10,8},{11,... | collective-permute-start | bytes 3145736 | tf_op jit(solution)/shard_map/ppermute | solution.py:318
  11.2 16.2 %copy-start.2 = (bf16[2,1024,256]{2,1,0:T(8,128)(2,1)S(1)}, bf16[2,1024,256]{2,1,0:T(8,128)(2,1)}, u32[]{:S(2)}) copy-start(bf16[2,1024,256]{2,1,0:T(8,128)(2,1)} %blk.5) | copy-start | bytes 3145732
  16.5 12.9 %copy-start.4 = (s32[16,2]{0,1:T(2,128)S(1)}, s32[16,2]{0,1:T(2,128)}, u32[]{:S(2)}) copy-start(s32[16,2]{0,1:T(2,128)} %param.10) | copy-start | bytes 388
  16.5 44.2 %collective-permute-start = (bf16[16,128,256]{2,1,0:T(8,128)(2,1)S(1)}, bf16[16,128,256]{2,1,0:T(8,128)(2,1)S(1)}, u32[]{:S(2)}, u32[]{:S(2)}) collective-permute-start(bf16[16,128,256]{2,1,0:T(8,128)(2,1)S(1)} %get-tuple-element.11), channel_id=1, source_target_pairs={{0,2},{2,4},{3,1},{4,6},{5,3},{6,8},{7,5},{8,10},{9,7},{10,12},{11... | collective-permute-start | bytes 3145736 | tf_op jit(solution)/shard_map/ppermute | solution.py:327
  29.3 31.4 %collective-permute-start.2 = (f32[8,128,256]{2,1,0:T(8,128)S(1)}, f32[8,128,256]{2,1,0:T(8,128)S(1)}, u32[]{:S(2)}, u32[]{:S(2)}) collective-permute-start(f32[8,128,256]{2,1,0:T(8,128)S(1)} %get-tuple-element.13), channel_id=1, source_target_pairs={{0,1},{1,0},{2,3},{3,2},{4,5},{5,4},{6,7},{7,6},{8,9},{9,8},{10,11... | collective-permute-start | bytes 3145736 | tf_op jit(solution)/shard_map/ppermute | solution.py:340
  29.4 9.8 %collective-permute-start.3 = (s32[2,16]{1,0:T(2,128)S(1)}, s32[2,16]{1,0:T(2,128)S(1)}, u32[]{:S(2)}, u32[]{:S(2)}) collective-permute-start(s32[2,16]{1,0:T(2,128)S(1)} %bitcast.7), channel_id=1, source_target_pairs={{1,3},{2,0},{3,5},{4,2},{5,7},{6,4},{7,9},{8,6},{9,11},{10,8},{11,... | collective-permute-start | bytes 392 | tf_op jit(solution)/shard_map/ppermute | solution.py:319
  40.6 14.9 %copy-start.1 = (bf16[16,256,256]{2,1,0:T(8,128)(2,1)S(1)}, bf16[16,256,256]{2,1,0:T(8,128)(2,1)}, u32[]{:S(2)}) copy-start(bf16[16,256,256]{2,1,0:T(8,128)(2,1)} %amp_ref.1) | copy-start | bytes 6291460
  40.6 22.6 %collective-permute-start.6 = (bf16[12,128,256]{2,1,0:T(8,128)(2,1)S(1)}, bf16[12,128,256]{2,1,0:T(8,128)(2,1)S(1)}, u32[]{:S(2)}, u32[]{:S(2)}) collective-permute-start(bf16[12,128,256]{2,1,0:T(8,128)(2,1)S(1)} %get-tuple-element.16), channel_id=1, source_target_pairs={{0,3},{2,5},{3,0},{4,7},{5,2},{6,9},{7,4},{8,11},{9,6},{10,13},{11... | collective-permute-start | bytes 2359304 | tf_op jit(solution)/shard_map/ppermute | solution.py:336
  43.7 19.5 %collective-permute-start.5 = (bf16[4,128,256]{2,1,0:T(8,128)(2,1)S(1)}, bf16[4,128,256]{2,1,0:T(8,128)(2,1)S(1)}, u32[]{:S(2)}, u32[]{:S(2)}) collective-permute-start(bf16[4,128,256]{2,1,0:T(8,128)(2,1)S(1)} %shard_map.96), channel_id=1, source_target_pairs={{0,2},{2,4},{3,1},{4,6},{5,3},{6,8},{7,5},{8,10},{9,7},{10,12},{11... | collective-permute-start | bytes 786440 | tf_op jit(solution)/shard_map/ppermute | solution.py:332
  45.6 15.0 %copy-start.3 = (f32[16,256]{1,0:T(8,128)S(1)}, f32[16,256]{1,0:T(8,128)}, u32[]{:S(2)}) copy-start(f32[16,256]{1,0:T(8,128)} %en_ref.1) | copy-start | bytes 49156
  45.6 15.0 %copy-start.6 = (f32[256]{0:T(256)S(1)}, f32[256]{0:T(256)}, u32[]{:S(2)}) copy-start(f32[256]{0:T(256)} %occ_ref.1) | copy-start | bytes 3076
  45.7 19.4 %collective-permute-start.4 = (bf16[4,128,256]{2,1,0:T(8,128)(2,1)S(1)}, bf16[4,128,256]{2,1,0:T(8,128)(2,1)S(1)}, u32[]{:S(2)}, u32[]{:S(2)}) collective-permute-start(bf16[4,128,256]{2,1,0:T(8,128)(2,1)S(1)} %get-tuple-element.15), channel_id=1, source_target_pairs={{0,3},{2,5},{3,0},{4,7},{5,2},{6,9},{7,4},{8,11},{9,6},{10,13},{11... | collective-permute-start | bytes 786440 | tf_op jit(solution)/shard_map/ppermute | solution.py:337
  60.7 2.5 %copy-start.5 = (s32[16]{0:T(128)S(1)}, s32[16]{0:T(128)}, u32[]{:S(2)}) copy-start(s32[16]{0:T(128)} %refs_1_.3) | copy-start | bytes 196

commit v7 on v6

--- a/solution.py
+++ b/solution.py
@@ -161,13 +161,17 @@
     )
 
 
-def products(far, near_blk, blk, meta_ref, prod):
+def products(far, near_blks, blk, meta_ref, prod):
     rows = prod.shape[1]
-    core = meta_ref[1]
-    row0 = pl.multiple_of((1 - core if far else core) * rows, rows)
-    for j in range(2):
-        for i in range(2):
-            prod[2 * j + i] = tn_dot(near_blk[j, :, pl.ds(row0, rows)], blk[i])
+    for core in range(2):
+        row0 = (1 - core if far else core) * rows
+
+        @pl.when(meta_ref[1] == core)
+        def _(near_blk=near_blks[core], row0=row0):
+            for j in range(2):
+                for i in range(2):
+                    prod[2 * j + i] = tn_dot(near_blk[j, :, row0:row0 + rows], blk[i])
+
     prod[4] = jnp.zeros(prod.shape[1:], F32)
 
 
@@ -177,15 +181,15 @@
     return jnp.where(mine, 2 * (orbs_ref[0, s] % 2) + second, 4)
 
 
-def near_kernel(meta_ref, near_blk, blk, out, prod):
-    products(False, near_blk, blk, meta_ref, prod)
+def near_kernel(meta_ref, next_blk, prev_blk, blk, out, prod):
+    products(False, (next_blk, prev_blk), blk, meta_ref, prod)
     for k in range(4):
         out[k] = prod[k].astype(BF16)
 
 
-def far_kernel(meta_ref, orbs_ref, near_blk, blk, acc_ref, *rest):
+def far_kernel(meta_ref, orbs_ref, next_blk, prev_blk, blk, acc_ref, *rest):
     out_refs, prod = rest[:-1], rest[-1]
-    products(True, near_blk, blk, meta_ref, prod)
+    products(True, (next_blk, prev_blk), blk, meta_ref, prod)
     start = 0
     for out in out_refs:
         @pl.loop(0, out.shape[0])
@@ -205,23 +209,25 @@
     )(*smem, *vmem)
 
 
-def exchange_kernel(meta_ref, near_blk, blk, keep_ref, send_ref):
+def exchange_kernel(meta_ref, next_blk, prev_blk, blk, keep_ref, send_ref):
     rows = keep_ref.shape[1]
-    for out, side in ((keep_ref, meta_ref[1]), (send_ref, 1 - meta_ref[1])):
-        row0 = pl.multiple_of(side * rows, rows)
-        for i in range(2):
-            left = blk[i, :, pl.ds(row0, rows)]
-            for j in range(2):
-                out[2 * i + j] = tn_dot(left, near_blk[j])
-                out[4 + 2 * i + j] = tn_dot(left, blk[j])
-
-
-def exchange(meta, near_blk, blk):
+    for core, near_blk in enumerate((next_blk, prev_blk)):
+        @pl.when(meta_ref[1] == core)
+        def _(core=core, near_blk=near_blk):
+            for out, side in ((keep_ref, core), (send_ref, 1 - core)):
+                for i in range(2):
+                    left = blk[i, :, side * rows:(side + 1) * rows]
+                    for j in range(2):
+                        out[2 * i + j] = tn_dot(left, near_blk[j])
+                        out[4 + 2 * i + j] = tn_dot(left, blk[j])
+
+
+def exchange(meta, next_blk, prev_blk, blk):
     width = blk.shape[2]
     half = jax.ShapeDtypeStruct((8, width // 2, width), F32)
     return whole(
-        exchange_kernel, [half, half], 1, 2, 4, (16 * 2 * 128 * 256 * 1024, 4),
-    )(meta, near_blk, blk)
+        exchange_kernel, [half, half], 1, 3, 4, (16 * 2 * 128 * 256 * 1024, 4),
+    )(meta, next_blk, prev_blk, blk)
 
 
 def base_kernel(meta_ref, orbs_ref, occ_ref, en_ref, amp_ref, own_ref,
@@ -315,7 +321,8 @@
     swap = [(2 * h + c, 2 * h + 1 - c) for h in range(holders) for c in range(2)]
 
     orbs = pair_orbs.T
-    near_blk = lax.ppermute(blocks, AXES, straight_in)
+    prev_blk = lax.ppermute(blocks, AXES, [(s, t) for s, t in straight_in if s % 2 == 1])
+    next_blk = lax.ppermute(blocks, AXES, [(s, t) for s, t in straight_in if s % 2 == 0])
     near_orbs = lax.ppermute(orbs, AXES, straight_in)
 
     meta = jnp.stack([holder, core])
@@ -328,15 +335,15 @@
 
     chunks = [pairs * 3 // 4, pairs - pairs * 3 // 4]
     msg_near, = message(
-        near_kernel, [meta], [near_blk, blocks], [(4, rows)], width)
+        near_kernel, [meta], [next_blk, prev_blk, blocks], [(4, rows)], width)
     near = lax.ppermute(msg_near, AXES, straight_out)
     msg_far = message(
-        far_kernel, [meta, near_orbs], [near_blk, blocks, acc_far],
+        far_kernel, [meta, near_orbs], [next_blk, prev_blk, blocks, acc_far],
         [(n, rows) for n in chunks], width)
     far = lax.ppermute(msg_far[0], AXES, cross_out)
     last = lax.ppermute(msg_far[1], AXES, cross_out)
 
-    keep, send = exchange(meta, near_blk, blocks)
+    keep, send = exchange(meta, next_blk, prev_blk, blocks)
     recv = lax.ppermute(send, AXES, swap)
     own, = coupling(meta, rel, weights, amplitudes, margins, rows, 0)
     base_terms = base(meta, orbs, occ_energy, pno_energy, amplitudes, own, early, keep, recv)

time: 66.9 us -> 67.7 us (1.012)
  starting transfers between devices: 34.6 us -> 35.3 us
    ppermute x1 -> x2, starting transfers between devices: 10.3 us -> 11 us  [the longest x1 10.1 us: local(): lax.ppermute(blocks, AXES, [(s, t) for s, t in straight_in if s % 2 == 0])]
    ppermute x1 -> x2, waiting for transfers between devices: 8.98 us -> 8.97 us  [the longest x1 8.96 us: local(): lax.ppermute(blocks, AXES, [(s, t) for s, t in straight_in if s % 2 == 0])]
  transfers between devices with their start and end apart: 7 -> 8, of which waited for: 2 -> 2; matrix products, arithmetic and copies ran while one was open for 1% -> 1% of each run, Pallas kernels for 29% -> 28%
where the time goes in v7:
time: 67.7 us; the launch traced here: 67.3 us
  starting transfers between devices  35.3 us (52%)
  Pallas kernels  20.5 us (30%)
  waiting for transfers between devices  10.3 us (15%)
  other arithmetic  0.83 us (1%)
    pallas_call x2, Pallas kernels, coupling(): pl.pallas_call(functools.partial(coupling_kernel, early), out_shape=out_s...  10.4 us
    ppermute x1, starting transfers between devices, local(): lax.ppermute(blocks, AXES, [(s, t) for s, t in straight_in if s % 2 == 0])  10.1 us
    ppermute x1, starting transfers between devices, local(): last = lax.ppermute(msg_far[1], AXES, cross_out)  9.85 us
    ppermute x1, waiting for transfers between devices, local(): lax.ppermute(blocks, AXES, [(s, t) for s, t in straight_in if s % 2 == 0])  8.96 us
    ppermute x1, starting transfers between devices, local(): near_orbs = lax.ppermute(orbs, AXES, straight_in)  8.5 us
    pallas_call x2, Pallas kernels, final(): pl.pallas_call(kernel, out_shape=jax.ShapeDtypeStruct(base_terms.shape, F...  3.28 us
    pallas_call x2, Pallas kernels, message(): whole(kernel, [jax.ShapeDtypeStruct((*n, width), BF16) for n in outs], le...  2.48 us
    pallas_call x1, Pallas kernels, base(): whole(base_kernel, jax.ShapeDtypeStruct(own.shape, F32), 3, 6, 4, (16 * 1...  2.48 us
  transfers between devices with their start and end apart: 8, of which 2 were waited for; matrix products, arithmetic and copies ran while one was open for 1% of the time, Pallas kernels for 28%

profile of v7, /device:TPU:24, one launch (start us, length us, event | category | flops | bytes accessed | tf_op | source)
XLA Modules:
  0.0 67.3 jit_solution(326764224526472111)
XLA Ops:
  0.0 0.0 copy-start
  0.0 0.8 %collective-permute-start.2 = (bf16[2,1024,256]{2,1,0:T(8,128)(2,1)}, bf16[2,1024,256]{2,1,0:T(8,128)(2,1)S(1)}, u32[]{:S(2)}, u32[]{:S(2)}) collective-permute-start(bf16[2,1024,256]{2,1,0:T(8,128)(2,1)} %blk.5), channel_id=1, source_target_pairs={{1,3},{3,5},{5,7},{7,9},{9,11},{11,13},{13,15},{15,17},{17,19},{19... | collective-permute-start | bytes 3145736 | tf_op jit(solution)/shard_map/ppermute | solution.py:324
  0.9 10.1 %collective-permute-start.1 = (bf16[2,1024,256]{2,1,0:T(8,128)(2,1)}, bf16[2,1024,256]{2,1,0:T(8,128)(2,1)S(1)}, u32[]{:S(2)}, u32[]{:S(2)}) collective-permute-start(bf16[2,1024,256]{2,1,0:T(8,128)(2,1)} %blk.5), channel_id=1, source_target_pairs={{2,0},{4,2},{6,4},{8,6},{10,8},{12,10},{14,12},{16,14},{18,16},{20... | collective-permute-start | bytes 3145736 | tf_op jit(solution)/shard_map/ppermute | solution.py:325
  11.0 0.1 pad_add_fusion.meta_ref.refs_0_
  11.1 0.8 %subtract_bitcast_fusion.rel_ref = s32[4,16]{1,0:T(4,128)S(1)} fusion(s32[2048,4]{0,1:T(4,128)} %param.14, s32[]{:T(128)S(6)} %select_n.4, s32[]{:T(128)S(6)} %mul.2), kind=kLoop, calls=%fused_computation.1 | loop fusion | flops 64 | bytes 520 | tf_op jit(solution)/shard_map/sub | solution.py:329
  11.8 0.0 copy-done
  11.8 0.1 dynamic-slice_bitcast_fusion.w_ref
  11.9 0.0 copy-start.2
  11.9 5.3 %shard_map.92 = (f32[16,128,256]{2,1,0:T(8,128)S(1)}, bf16[16,128,256]{2,1,0:T(8,128)(2,1)S(1)}) custom-call(s32[2]{0:T(128)S(1)} %pad_add_fusion.meta_ref.refs_0_, s32[4,16]{1,0:T(4,128)S(1)} %subtract_bitcast_fusion.rel_ref, f32[4,16]{1,0:T(4,128)S(1)} %dynamic-slice_bitcast_fusion.w_ref, bf16[16,256,256]{2,1,0:T(8,128)(2,1)} %amp_ref.1, ...), custom_call_target="tpu_custom_call" | custom-call | flops 738197504 | bytes 6291456 | tf_op jit(solution)/shard_map/pallas_call | solution.py:139
  17.2 0.0 copy-start.4
  17.2 1.9 %collective-permute-start = (bf16[16,128,256]{2,1,0:T(8,128)(2,1)S(1)}, bf16[16,128,256]{2,1,0:T(8,128)(2,1)S(1)}, u32[]{:S(2)}, u32[]{:S(2)}) collective-permute-start(bf16[16,128,256]{2,1,0:T(8,128)(2,1)S(1)} %get-tuple-element.11), channel_id=1, source_target_pairs={{0,2},{2,4},{3,1},{4,6},{5,3},{6,8},{7,5},{8,10},{9,7},{10,12},{11... | collective-permute-start | bytes 3145736 | tf_op jit(solution)/shard_map/ppermute | solution.py:334
  19.2 0.0 collective-permute-done.2.prev_blk
  19.2 9.0 %collective-permute-done.1.next_blk = bf16[2,1024,256]{2,1,0:T(8,128)(2,1)S(1)} collective-permute-done((bf16[2,1024,256]{2,1,0:T(8,128)(2,1)}, bf16[2,1024,256]{2,1,0:T(8,128)(2,1)S(1)}, u32[]{:S(2)}, u32[]{:S(2)}) %collective-permute-start.1) | collective-permute-done | bytes 1048608 | tf_op jit(solution)/shard_map/ppermute | solution.py:325
  28.1 0.0 copy-done.2
  28.1 1.9 %shard_map.93 = (f32[8,128,256]{2,1,0:T(8,128)S(1)}, f32[8,128,256]{2,1,0:T(8,128)S(1)}) custom-call(s32[2]{0:T(128)S(1)} %pad_add_fusion.meta_ref.refs_0_, bf16[2,1024,256]{2,1,0:T(8,128)(2,1)S(1)} %collective-permute-done.1.next_blk, bf16[2,1024,256]{2,1,0:T(8,128)(2,1)S(1)} %collective-permute-done.2.prev_blk, bf16[2,1024,256]{2,1,0:T(8,128)(2,1)S(1)} %copy-done.2), custom_call_target="tpu_custom_call" | custom-call | flops 1073741824 | bytes 4194304 | tf_op jit(solution)/shard_map/pallas_call | solution.py:228
  30.0 0.1 collective-permute-start.3
  30.1 0.0 copy-done.4
  30.1 8.5 %collective-permute-start.4 = (s32[2,16]{1,0:T(2,128)S(1)}, s32[2,16]{1,0:T(2,128)S(1)}, u32[]{:S(2)}, u32[]{:S(2)}) collective-permute-start(s32[2,16]{1,0:T(2,128)S(1)} %bitcast.7), channel_id=1, source_target_pairs={{1,3},{2,0},{3,5},{4,2},{5,7},{6,4},{7,9},{8,6},{9,11},{10,8},{11,... | collective-permute-start | bytes 392 | tf_op jit(solution)/shard_map/ppermute | solution.py:326
  38.6 1.3 %collective-permute-done.4.orbs_ref = s32[2,16]{1,0:T(2,128)S(1)} collective-permute-done((s32[2,16]{1,0:T(2,128)S(1)}, s32[2,16]{1,0:T(2,128)S(1)}, u32[]{:S(2)}, u32[]{:S(2)}) %collective-permute-start.4) | collective-permute-done | bytes 160 | tf_op jit(solution)/shard_map/ppermute | solution.py:326
  39.9 1.4 %shard_map.95 = (bf16[12,128,256]{2,1,0:T(8,128)(2,1)S(1)}, bf16[4,128,256]{2,1,0:T(8,128)(2,1)S(1)}) custom-call(s32[2]{0:T(128)S(1)} %pad_add_fusion.meta_ref.refs_0_, s32[2,16]{1,0:T(2,128)S(1)} %collective-permute-done.4.orbs_ref, bf16[2,1024,256]{2,1,0:T(8,128)(2,1)S(1)} %collective-permute-done.1.next_blk, ...), custom_call_target="tpu_custom_call" | custom-call | flops 268435456 | bytes 4194304 | tf_op jit(solution)/shard_map/pallas_call | solution.py:204
  41.3 0.0 copy-start.1
  41.3 2.1 %collective-permute-start.7 = (bf16[12,128,256]{2,1,0:T(8,128)(2,1)S(1)}, bf16[12,128,256]{2,1,0:T(8,128)(2,1)S(1)}, u32[]{:S(2)}, u32[]{:S(2)}) collective-permute-start(bf16[12,128,256]{2,1,0:T(8,128)(2,1)S(1)} %get-tuple-element.16), channel_id=1, source_target_pairs={{0,3},{2,5},{3,0},{4,7},{5,2},{6,9},{7,4},{8,11},{9,6},{10,13},{11... | collective-permute-start | bytes 2359304 | tf_op jit(solution)/shard_map/ppermute | solution.py:343
  43.4 1.1 %shard_map.96 = bf16[4,128,256]{2,1,0:T(8,128)(2,1)S(1)} custom-call(s32[2]{0:T(128)S(1)} %pad_add_fusion.meta_ref.refs_0_, bf16[2,1024,256]{2,1,0:T(8,128)(2,1)S(1)} %collective-permute-done.1.next_blk, bf16[2,1024,256]{2,1,0:T(8,128)(2,1)S(1)} %collective-permute-done.2.prev_blk, bf16[2,1024,256]{2,1,0:T(8,128)(2,1)S(1)} %copy-done.2), custom_call_target="tpu_custom_call" | custom-call | flops 268435456 | bytes 4194304 | tf_op jit(solution)/shard_map/pallas_call | solution.py:204
  44.5 1.9 %collective-permute-start.6 = (bf16[4,128,256]{2,1,0:T(8,128)(2,1)S(1)}, bf16[4,128,256]{2,1,0:T(8,128)(2,1)S(1)}, u32[]{:S(2)}, u32[]{:S(2)}) collective-permute-start(bf16[4,128,256]{2,1,0:T(8,128)(2,1)S(1)} %shard_map.96), channel_id=1, source_target_pairs={{0,2},{2,4},{3,1},{4,6},{5,3},{6,8},{7,5},{8,10},{9,7},{10,12},{11... | collective-permute-start | bytes 786440 | tf_op jit(solution)/shard_map/ppermute | solution.py:339
  46.4 0.0 copy-start.3
  46.4 0.0 copy-start.6
  46.4 9.9 %collective-permute-start.5 = (bf16[4,128,256]{2,1,0:T(8,128)(2,1)S(1)}, bf16[4,128,256]{2,1,0:T(8,128)(2,1)S(1)}, u32[]{:S(2)}, u32[]{:S(2)}) collective-permute-start(bf16[4,128,256]{2,1,0:T(8,128)(2,1)S(1)} %get-tuple-element.15), channel_id=1, source_target_pairs={{0,3},{2,5},{3,0},{4,7},{5,2},{6,9},{7,4},{8,11},{9,6},{10,13},{11... | collective-permute-start | bytes 786440 | tf_op jit(solution)/shard_map/ppermute | solution.py:344
  56.3 0.0 copy-done.1
  56.3 5.1 %shard_map.91.own_ref = f32[16,128,256]{2,1,0:T(8,128)S(1)} custom-call(s32[2]{0:T(128)S(1)} %pad_add_fusion.meta_ref.refs_0_, s32[4,16]{1,0:T(4,128)S(1)} %subtract_bitcast_fusion.rel_ref, f32[4,16]{1,0:T(4,128)S(1)} %dynamic-slice_bitcast_fusion.w_ref, bf16[16,256,256]{2,1,0:T(8,128)(2,1)S(1)} %copy-done.1, bf16[16,4,256,256]{3,2,1,0:T(8,128)(2,1)} %mar_hbm.3), custom_call_target="tpu_custom_call" | custom-call | flops 738197504 | bytes 6291456 | tf_op jit(solution)/shard_map/pallas_call | solution.py:139
  61.4 0.0 collective-permute-done.early_ref
  61.4 0.0 collective-permute-done.3.recv_ref
  61.4 0.0 copy-done.3
  61.5 0.0 copy-done.6
  61.5 0.0 copy-start.5
  61.5 2.5 %shard_map.94.refs_3_ = f32[16,128,256]{2,1,0:T(8,128)S(1)} custom-call(s32[2]{0:T(128)S(1)} %pad_add_fusion.meta_ref.refs_0_, s32[2,16]{1,0:T(2,128)S(1)} %bitcast.8, f32[256]{0:T(256)S(1)} %copy-done.6, f32[16,256]{1,0:T(8,128)S(1)} %copy-done.3, bf16[16,256,256]{2,1,0:T(8,128)(2,1)S(1)} %copy-done.1, f32[16,128,256]{2,1,0:T(8,128)S(1)} %shard_map.91.own_ref, ...), custom_call_target="tpu_custom_call" | custom-call | flops 4194304 | bytes 8388608 | tf_op jit(solution)/shard_map/pallas_call | solution.py:259
  64.0 0.0 collective-permute-done.6.refs_5_
  64.0 0.0 collective-permute-done.7.refs_4_
  64.0 0.0 copy-done.5
  64.0 1.8 %shard_map.97.refs_6_ = f32[16,128,256]{2,1,0:T(8,128)} custom-call(s32[2]{0:T(128)S(1)} %pad_add_fusion.meta_ref.refs_0_, s32[16]{0:T(128)S(1)} %copy-done.5, s32[2,16]{1,0:T(2,128)S(1)} %bitcast.9, f32[16,128,256]{2,1,0:T(8,128)S(1)} %shard_map.94.refs_3_, bf16[12,128,256]{2,1,0:T(8,128)(2,1)S(1)} %collective-permute-done.7.refs_4_, ...), custom_call_target="tpu_custom_call" | custom-call | flops 786432 | bytes 3145728 | tf_op jit(solution)/shard_map/pallas_call | solution.py:299
  65.8 0.0 collective-permute-done.5.refs_4_
  65.9 1.4 %shard_map.98 = f32[16,128,256]{2,1,0:T(8,128)} custom-call(s32[2]{0:T(128)S(1)} %pad_add_fusion.meta_ref.refs_0_, s32[16]{0:T(128)S(1)} %copy-done.5, s32[2,16]{1,0:T(2,128)S(1)} %bitcast.10, f32[16,128,256]{2,1,0:T(8,128)S(1)} %shard_map.94.refs_3_, bf16[4,128,256]{2,1,0:T(8,128)(2,1)S(1)} %collective-permute-done.5.refs_4_, ...), custom_call_target="tpu_custom_call", output_to_operand_aliasing={{}: (6, {})} | custom-call | flops 262144 | bytes 1048576 | tf_op jit(solution)/shard_map/pallas_call | solution.py:299
Async XLA Ops:
  0.0 11.8 %copy-start = (f32[2048,4]{0,1:T(4,128)S(1)}, f32[2048,4]{0,1:T(4,128)}, u32[]{:S(2)}) copy-start(f32[2048,4]{0,1:T(4,128)} %param.15) | copy-start | bytes 98308
  0.0 19.2 %collective-permute-start.2 = (bf16[2,1024,256]{2,1,0:T(8,128)(2,1)}, bf16[2,1024,256]{2,1,0:T(8,128)(2,1)S(1)}, u32[]{:S(2)}, u32[]{:S(2)}) collective-permute-start(bf16[2,1024,256]{2,1,0:T(8,128)(2,1)} %blk.5), channel_id=1, source_target_pairs={{1,3},{3,5},{5,7},{7,9},{9,11},{11,13},{13,15},{15,17},{17,19},{19... | collective-permute-start | bytes 3145736 | tf_op jit(solution)/shard_map/ppermute | solution.py:324
  0.9 27.3 %collective-permute-start.1 = (bf16[2,1024,256]{2,1,0:T(8,128)(2,1)}, bf16[2,1024,256]{2,1,0:T(8,128)(2,1)S(1)}, u32[]{:S(2)}, u32[]{:S(2)}) collective-permute-start(bf16[2,1024,256]{2,1,0:T(8,128)(2,1)} %blk.5), channel_id=1, source_target_pairs={{2,0},{4,2},{6,4},{8,6},{10,8},{12,10},{14,12},{16,14},{18,16},{20... | collective-permute-start | bytes 3145736 | tf_op jit(solution)/shard_map/ppermute | solution.py:325
  11.9 16.2 %copy-start.2 = (bf16[2,1024,256]{2,1,0:T(8,128)(2,1)S(1)}, bf16[2,1024,256]{2,1,0:T(8,128)(2,1)}, u32[]{:S(2)}) copy-start(bf16[2,1024,256]{2,1,0:T(8,128)(2,1)} %blk.5) | copy-start | bytes 3145732
  17.2 12.9 %copy-start.4 = (s32[16,2]{0,1:T(2,128)S(1)}, s32[16,2]{0,1:T(2,128)}, u32[]{:S(2)}) copy-start(s32[16,2]{0,1:T(2,128)} %param.10) | copy-start | bytes 388
  17.2 44.2 %collective-permute-start = (bf16[16,128,256]{2,1,0:T(8,128)(2,1)S(1)}, bf16[16,128,256]{2,1,0:T(8,128)(2,1)S(1)}, u32[]{:S(2)}, u32[]{:S(2)}) collective-permute-start(bf16[16,128,256]{2,1,0:T(8,128)(2,1)S(1)} %get-tuple-element.11), channel_id=1, source_target_pairs={{0,2},{2,4},{3,1},{4,6},{5,3},{6,8},{7,5},{8,10},{9,7},{10,12},{11... | collective-permute-start | bytes 3145736 | tf_op jit(solution)/shard_map/ppermute | solution.py:334
  30.0 31.4 %collective-permute-start.3 = (f32[8,128,256]{2,1,0:T(8,128)S(1)}, f32[8,128,256]{2,1,0:T(8,128)S(1)}, u32[]{:S(2)}, u32[]{:S(2)}) collective-permute-start(f32[8,128,256]{2,1,0:T(8,128)S(1)} %get-tuple-element.13), channel_id=1, source_target_pairs={{0,1},{1,0},{2,3},{3,2},{4,5},{5,4},{6,7},{7,6},{8,9},{9,8},{10,11... | collective-permute-start | bytes 3145736 | tf_op jit(solution)/shard_map/ppermute | solution.py:347
  30.1 9.8 %collective-permute-start.4 = (s32[2,16]{1,0:T(2,128)S(1)}, s32[2,16]{1,0:T(2,128)S(1)}, u32[]{:S(2)}, u32[]{:S(2)}) collective-permute-start(s32[2,16]{1,0:T(2,128)S(1)} %bitcast.7), channel_id=1, source_target_pairs={{1,3},{2,0},{3,5},{4,2},{5,7},{6,4},{7,9},{8,6},{9,11},{10,8},{11,... | collective-permute-start | bytes 392 | tf_op jit(solution)/shard_map/ppermute | solution.py:326
  41.3 15.0 %copy-start.1 = (bf16[16,256,256]{2,1,0:T(8,128)(2,1)S(1)}, bf16[16,256,256]{2,1,0:T(8,128)(2,1)}, u32[]{:S(2)}) copy-start(bf16[16,256,256]{2,1,0:T(8,128)(2,1)} %amp_ref.1) | copy-start | bytes 6291460
  41.3 22.6 %collective-permute-start.7 = (bf16[12,128,256]{2,1,0:T(8,128)(2,1)S(1)}, bf16[12,128,256]{2,1,0:T(8,128)(2,1)S(1)}, u32[]{:S(2)}, u32[]{:S(2)}) collective-permute-start(bf16[12,128,256]{2,1,0:T(8,128)(2,1)S(1)} %get-tuple-element.16), channel_id=1, source_target_pairs={{0,3},{2,5},{3,0},{4,7},{5,2},{6,9},{7,4},{8,11},{9,6},{10,13},{11... | collective-permute-start | bytes 2359304 | tf_op jit(solution)/shard_map/ppermute | solution.py:343
  44.5 19.5 %collective-permute-start.6 = (bf16[4,128,256]{2,1,0:T(8,128)(2,1)S(1)}, bf16[4,128,256]{2,1,0:T(8,128)(2,1)S(1)}, u32[]{:S(2)}, u32[]{:S(2)}) collective-permute-start(bf16[4,128,256]{2,1,0:T(8,128)(2,1)S(1)} %shard_map.96), channel_id=1, source_target_pairs={{0,2},{2,4},{3,1},{4,6},{5,3},{6,8},{7,5},{8,10},{9,7},{10,12},{11... | collective-permute-start | bytes 786440 | tf_op jit(solution)/shard_map/ppermute | solution.py:339
  46.4 15.0 %copy-start.3 = (f32[16,256]{1,0:T(8,128)S(1)}, f32[16,256]{1,0:T(8,128)}, u32[]{:S(2)}) copy-start(f32[16,256]{1,0:T(8,128)} %en_ref.1) | copy-start | bytes 49156
  46.4 15.0 %copy-start.6 = (f32[256]{0:T(256)S(1)}, f32[256]{0:T(256)}, u32[]{:S(2)}) copy-start(f32[256]{0:T(256)} %occ_ref.1) | copy-start | bytes 3076
  46.4 19.4 %collective-permute-start.5 = (bf16[4,128,256]{2,1,0:T(8,128)(2,1)S(1)}, bf16[4,128,256]{2,1,0:T(8,128)(2,1)S(1)}, u32[]{:S(2)}, u32[]{:S(2)}) collective-permute-start(bf16[4,128,256]{2,1,0:T(8,128)(2,1)S(1)} %get-tuple-element.15), channel_id=1, source_target_pairs={{0,3},{2,5},{3,0},{4,7},{5,2},{6,9},{7,4},{8,11},{9,6},{10,13},{11... | collective-permute-start | bytes 786440 | tf_op jit(solution)/shard_map/ppermute | solution.py:344
  61.5 2.5 %copy-start.5 = (s32[16]{0:T(128)S(1)}, s32[16]{0:T(128)}, u32[]{:S(2)}) copy-start(s32[16]{0:T(128)} %refs_1_.3) | copy-start | bytes 196

commit v8 on v5

--- a/solution.py
+++ b/solution.py
@@ -41,7 +41,7 @@
     sources, couplings = mar_hbm.shape[0], mar_hbm.shape[1]
     slots, rows = acc_ref.shape[0], acc_ref.shape[1]
     core = meta_ref[1]
-    shift = (1 - 2 * core) * slots if early else 0
+    shift = (2 * core - 1) * slots if early else 0
     row0 = pl.multiple_of(core * rows, rows)
     far0 = pl.multiple_of(rows - core * rows, rows)
 
@@ -205,23 +205,24 @@
     )(*smem, *vmem)
 
 
-def exchange_kernel(meta_ref, near_blk, blk, keep_ref, send_ref):
+def exchange_kernel(meta_ref, near_blk, swapped, blk, keep_ref, send_ref):
     rows = keep_ref.shape[1]
     for out, side in ((keep_ref, meta_ref[1]), (send_ref, 1 - meta_ref[1])):
         row0 = pl.multiple_of(side * rows, rows)
         for i in range(2):
+            other = swapped[i, :, pl.ds(row0, rows)]
             left = blk[i, :, pl.ds(row0, rows)]
             for j in range(2):
-                out[2 * i + j] = tn_dot(left, near_blk[j])
+                out[2 * i + j] = tn_dot(other, near_blk[j])
                 out[4 + 2 * i + j] = tn_dot(left, blk[j])
 
 
-def exchange(meta, near_blk, blk):
+def exchange(meta, near_blk, swapped, blk):
     width = blk.shape[2]
     half = jax.ShapeDtypeStruct((8, width // 2, width), F32)
     return whole(
-        exchange_kernel, [half, half], 1, 2, 4, (16 * 2 * 128 * 256 * 1024, 4),
-    )(meta, near_blk, blk)
+        exchange_kernel, [half, half], 1, 3, 4, (16 * 2 * 128 * 256 * 1024, 4),
+    )(meta, near_blk, swapped, blk)
 
 
 def base_kernel(meta_ref, orbs_ref, occ_ref, en_ref, amp_ref, own_ref,
@@ -234,7 +235,7 @@
     def _(p):
         first, second = orbs_ref[0, p], orbs_ref[1, p]
         side = second // 2 - holder
-        step = 1 - 2 * core
+        step = 2 * core - 1
         index = 2 * (first % 2) + second % 2
         both = index + jnp.where(side == 0, 4, 0)
         cols = en_ref[pl.ds(p, 1), :]
@@ -306,14 +307,13 @@
     core = lax.axis_index("aux").astype(jnp.int32)
     holders = lax.axis_size("pairs")
     pairs, width = amplitudes.shape[0], amplitudes.shape[1]
-    straight_in = toward(holders, False, True)
-    straight_out = toward(holders, False, False)
-    cross_out = toward(holders, True, False)
+    straight_out = toward(holders, False, True)
+    cross_out = toward(holders, True, True)
     swap = [(2 * h + c, 2 * h + 1 - c) for h in range(holders) for c in range(2)]
 
     orbs = pair_orbs.T
-    near_blk = lax.ppermute(blocks, AXES, straight_in)
-    near_orbs = lax.ppermute(orbs, AXES, straight_in)
+    near_blk = lax.ppermute(blocks, AXES, cross_out)
+    near_orbs = lax.ppermute(orbs, AXES, cross_out)
 
     meta = jnp.stack([holder, core])
     rel = lax.dynamic_slice_in_dim(couple_target, holder * pairs, pairs, 0).T - holder * pairs
@@ -322,18 +322,19 @@
     acc_far, msg_early = coupling(
         meta, rel, weights, amplitudes, margins, rows, rows)
     early = lax.ppermute(msg_early, AXES, straight_out)
+    swapped = lax.ppermute(blocks, AXES, swap)
 
     chunks = [pairs * 3 // 4, pairs - pairs * 3 // 4]
     msg_near, = message(
-        near_kernel, [meta], [near_blk, blocks], [(4, rows)], width)
+        near_kernel, [meta], [near_blk, swapped], [(4, rows)], width)
     near = lax.ppermute(msg_near, AXES, straight_out)
     msg_far = message(
-        far_kernel, [meta, near_orbs], [near_blk, blocks, acc_far],
+        far_kernel, [meta, near_orbs], [near_blk, swapped, acc_far],
         [(n, rows) for n in chunks], width)
     far = lax.ppermute(msg_far[0], AXES, cross_out)
     last = lax.ppermute(msg_far[1], AXES, cross_out)
 
-    keep, send = exchange(meta, near_blk, blocks)
+    keep, send = exchange(meta, near_blk, swapped, blocks)
     recv = lax.ppermute(send, AXES, swap)
     own, = coupling(meta, rel, weights, amplitudes, margins, rows, 0)
     base_terms = base(meta, orbs, occ_energy, pno_energy, amplitudes, own, early, near,

time: 68.2 us -> 65.2 us (0.956)
  the two profiles are of different devices: /device:TPU:24 before, /device:TPU:17 now
where the time goes in v8:
time: 65.2 us; the launch traced here: 64.8 us
  starting transfers between devices  32.6 us (50%)
  Pallas kernels  20.9 us (32%)
  waiting for transfers between devices  10.1 us (15%)
  other arithmetic  0.83 us (1%)
    pallas_call x2, Pallas kernels, coupling(): pl.pallas_call(functools.partial(coupling_kernel, early), out_shape=out_s...  10.7 us
    ppermute x1, starting transfers between devices, local(): last = lax.ppermute(msg_far[1], AXES, cross_out)  10.3 us
    ppermute x1, waiting for transfers between devices, local(): near_orbs = lax.ppermute(orbs, AXES, cross_out)  5.97 us
    ppermute x1, starting transfers between devices, local(): swapped = lax.ppermute(blocks, AXES, swap)  5.94 us
    ppermute x1, starting transfers between devices, local(): near_blk = lax.ppermute(blocks, AXES, cross_out)  4.23 us
    ppermute x1, waiting for transfers between devices, local(): near = lax.ppermute(msg_near, AXES, straight_out)  4.13 us
    ppermute x1, starting transfers between devices, local(): recv = lax.ppermute(send, AXES, swap)  3.62 us
    pallas_call x2, Pallas kernels, final(): pl.pallas_call(kernel, out_shape=jax.ShapeDtypeStruct(base_terms.shape, F...  3.21 us
  transfers between devices with their start and end apart: 8, of which 2 were waited for; matrix products, arithmetic and copies ran while one was open for 1% of the time, Pallas kernels for 30%

profile of v8, /device:TPU:17, one launch (start us, length us, event | category | flops | bytes accessed | tf_op | source)
XLA Modules:
  0.0 64.8 jit_solution(1528092332058142940)
XLA Ops:
  0.0 0.0 copy-start
  0.0 4.2 %collective-permute-start.1 = (bf16[2,1024,256]{2,1,0:T(8,128)(2,1)}, bf16[2,1024,256]{2,1,0:T(8,128)(2,1)S(1)}, u32[]{:S(2)}, u32[]{:S(2)}) collective-permute-start(bf16[2,1024,256]{2,1,0:T(8,128)(2,1)} %blk.1), channel_id=1, source_target_pairs={{1,2},{2,1},{3,4},{4,3},{5,6},{6,5},{7,8},{8,7},{9,10},{10,9},{11,... | collective-permute-start | bytes 3145736 | tf_op jit(solution)/shard_map/ppermute | solution.py:315
  4.2 5.9 %collective-permute-start.2 = (bf16[2,1024,256]{2,1,0:T(8,128)(2,1)}, bf16[2,1024,256]{2,1,0:T(8,128)(2,1)S(1)}, u32[]{:S(2)}, u32[]{:S(2)}) collective-permute-start(bf16[2,1024,256]{2,1,0:T(8,128)(2,1)} %blk.1), channel_id=1, source_target_pairs={{0,1},{1,0},{2,3},{3,2},{4,5},{5,4},{6,7},{7,6},{8,9},{9,8},{10,11... | collective-permute-start | bytes 3145736 | tf_op jit(solution)/shard_map/ppermute | solution.py:325
  10.2 0.1 pad_add_fusion.meta_ref.refs_0_
  10.3 0.8 %subtract_bitcast_fusion.rel_ref = s32[4,16]{1,0:T(4,128)S(1)} fusion(s32[2048,4]{0,1:T(4,128)} %param.14, s32[]{:T(128)S(6)} %select_n.4, s32[]{:T(128)S(6)} %mul.2), kind=kLoop, calls=%fused_computation.1 | loop fusion | flops 64 | bytes 520 | tf_op jit(solution)/shard_map/sub | solution.py:319
  11.0 0.0 copy-done
  11.0 0.1 dynamic-slice_bitcast_fusion.w_ref
  11.1 0.0 copy-start.6
  11.1 6.2 %shard_map.92 = (f32[16,128,256]{2,1,0:T(8,128)S(1)}, bf16[16,128,256]{2,1,0:T(8,128)(2,1)S(1)}) custom-call(s32[2]{0:T(128)S(1)} %pad_add_fusion.meta_ref.refs_0_, s32[4,16]{1,0:T(4,128)S(1)} %subtract_bitcast_fusion.rel_ref, f32[4,16]{1,0:T(4,128)S(1)} %dynamic-slice_bitcast_fusion.w_ref, bf16[16,256,256]{2,1,0:T(8,128)(2,1)} %amp_ref.1, ...), custom_call_target="tpu_custom_call" | custom-call | flops 738197504 | bytes 6291456 | tf_op jit(solution)/shard_map/pallas_call | solution.py:139
  17.3 0.0 copy-start.4
  17.3 1.9 %collective-permute-start = (bf16[16,128,256]{2,1,0:T(8,128)(2,1)S(1)}, bf16[16,128,256]{2,1,0:T(8,128)(2,1)S(1)}, u32[]{:S(2)}, u32[]{:S(2)}) collective-permute-start(bf16[16,128,256]{2,1,0:T(8,128)(2,1)S(1)} %get-tuple-element.11), channel_id=1, source_target_pairs={{1,3},{2,0},{3,5},{4,2},{5,7},{6,4},{7,9},{8,6},{9,11},{10,8},{11,... | collective-permute-start | bytes 3145736 | tf_op jit(solution)/shard_map/ppermute | solution.py:324
  19.2 0.0 collective-permute-done.1.near_blk
  19.2 0.0 collective-permute-done.2.blk.swapped
  19.2 0.0 copy-done.6
  19.3 1.9 %shard_map.94 = (f32[8,128,256]{2,1,0:T(8,128)S(1)}, f32[8,128,256]{2,1,0:T(8,128)S(1)}) custom-call(s32[2]{0:T(128)S(1)} %pad_add_fusion.meta_ref.refs_0_, bf16[2,1024,256]{2,1,0:T(8,128)(2,1)S(1)} %collective-permute-done.1.near_blk, bf16[2,1024,256]{2,1,0:T(8,128)(2,1)S(1)} %collective-permute-done.2.blk.swapped, bf16[2,1024,256]{2,1,0:T(8,128)(2,1)S(1)} %copy-done.6), custom_call_target="tpu_custom_call" | custom-call | flops 1073741824 | bytes 4194304 | tf_op jit(solution)/shard_map/pallas_call | solution.py:223
  21.2 3.6 %collective-permute-start.4 = (f32[8,128,256]{2,1,0:T(8,128)S(1)}, f32[8,128,256]{2,1,0:T(8,128)S(1)}, u32[]{:S(2)}, u32[]{:S(2)}) collective-permute-start(f32[8,128,256]{2,1,0:T(8,128)S(1)} %get-tuple-element.13), channel_id=1, source_target_pairs={{0,1},{1,0},{2,3},{3,2},{4,5},{5,4},{6,7},{7,6},{8,9},{9,8},{10,11... | collective-permute-start | bytes 3145736 | tf_op jit(solution)/shard_map/ppermute | solution.py:338
  24.8 0.0 copy-done.4
  24.8 1.9 %collective-permute-start.5 = (s32[2,16]{1,0:T(2,128)S(1)}, s32[2,16]{1,0:T(2,128)S(1)}, u32[]{:S(2)}, u32[]{:S(2)}) collective-permute-start(s32[2,16]{1,0:T(2,128)S(1)} %bitcast.7), channel_id=1, source_target_pairs={{1,2},{2,1},{3,4},{4,3},{5,6},{6,5},{7,8},{8,7},{9,10},{10,9},{11,... | collective-permute-start | bytes 392 | tf_op jit(solution)/shard_map/ppermute | solution.py:316
  26.7 6.0 %collective-permute-done.5.orbs_ref = s32[2,16]{1,0:T(2,128)S(1)} collective-permute-done((s32[2,16]{1,0:T(2,128)S(1)}, s32[2,16]{1,0:T(2,128)S(1)}, u32[]{:S(2)}, u32[]{:S(2)}) %collective-permute-start.5) | collective-permute-done | bytes 160 | tf_op jit(solution)/shard_map/ppermute | solution.py:316
  32.7 1.4 %shard_map.96 = (bf16[12,128,256]{2,1,0:T(8,128)(2,1)S(1)}, bf16[4,128,256]{2,1,0:T(8,128)(2,1)S(1)}) custom-call(s32[2]{0:T(128)S(1)} %pad_add_fusion.meta_ref.refs_0_, s32[2,16]{1,0:T(2,128)S(1)} %collective-permute-done.5.orbs_ref, bf16[2,1024,256]{2,1,0:T(8,128)(2,1)S(1)} %collective-permute-done.1.near_blk, ...), custom_call_target="tpu_custom_call" | custom-call | flops 268435456 | bytes 4194304 | tf_op jit(solution)/shard_map/pallas_call | solution.py:200
  34.1 0.0 copy-start.1
  34.1 2.8 %collective-permute-start.7 = (bf16[12,128,256]{2,1,0:T(8,128)(2,1)S(1)}, bf16[12,128,256]{2,1,0:T(8,128)(2,1)S(1)}, u32[]{:S(2)}, u32[]{:S(2)}) collective-permute-start(bf16[12,128,256]{2,1,0:T(8,128)(2,1)S(1)} %get-tuple-element.16), channel_id=1, source_target_pairs={{1,2},{2,1},{3,4},{4,3},{5,6},{6,5},{7,8},{8,7},{9,10},{10,9},{11,... | collective-permute-start | bytes 2359304 | tf_op jit(solution)/shard_map/ppermute | solution.py:334
  36.9 1.0 %shard_map.93 = bf16[4,128,256]{2,1,0:T(8,128)(2,1)S(1)} custom-call(s32[2]{0:T(128)S(1)} %pad_add_fusion.meta_ref.refs_0_, bf16[2,1024,256]{2,1,0:T(8,128)(2,1)S(1)} %collective-permute-done.1.near_blk, bf16[2,1024,256]{2,1,0:T(8,128)(2,1)S(1)} %collective-permute-done.2.blk.swapped), custom_call_target="tpu_custom_call" | custom-call | flops 268435456 | bytes 4194304 | tf_op jit(solution)/shard_map/pallas_call | solution.py:200
  37.9 1.9 %collective-permute-start.3 = (bf16[4,128,256]{2,1,0:T(8,128)(2,1)S(1)}, bf16[4,128,256]{2,1,0:T(8,128)(2,1)S(1)}, u32[]{:S(2)}, u32[]{:S(2)}) collective-permute-start(bf16[4,128,256]{2,1,0:T(8,128)(2,1)S(1)} %shard_map.93), channel_id=1, source_target_pairs={{1,3},{2,0},{3,5},{4,2},{5,7},{6,4},{7,9},{8,6},{9,11},{10,8},{11,... | collective-permute-start | bytes 786440 | tf_op jit(solution)/shard_map/ppermute | solution.py:330
  39.9 0.0 copy-start.2
  39.9 0.0 copy-start.5
  39.9 10.3 %collective-permute-start.6 = (bf16[4,128,256]{2,1,0:T(8,128)(2,1)S(1)}, bf16[4,128,256]{2,1,0:T(8,128)(2,1)S(1)}, u32[]{:S(2)}, u32[]{:S(2)}) collective-permute-start(bf16[4,128,256]{2,1,0:T(8,128)(2,1)S(1)} %get-tuple-element.15), channel_id=1, source_target_pairs={{1,2},{2,1},{3,4},{4,3},{5,6},{6,5},{7,8},{8,7},{9,10},{10,9},{11,... | collective-permute-start | bytes 786440 | tf_op jit(solution)/shard_map/ppermute | solution.py:335
  50.2 0.0 copy-done.1
  50.2 4.6 %shard_map.91.own_ref = f32[16,128,256]{2,1,0:T(8,128)S(1)} custom-call(s32[2]{0:T(128)S(1)} %pad_add_fusion.meta_ref.refs_0_, s32[4,16]{1,0:T(4,128)S(1)} %subtract_bitcast_fusion.rel_ref, f32[4,16]{1,0:T(4,128)S(1)} %dynamic-slice_bitcast_fusion.w_ref, bf16[16,256,256]{2,1,0:T(8,128)(2,1)S(1)} %copy-done.1, bf16[16,4,256,256]{3,2,1,0:T(8,128)(2,1)} %mar_hbm.3), custom_call_target="tpu_custom_call" | custom-call | flops 738197504 | bytes 6291456 | tf_op jit(solution)/shard_map/pallas_call | solution.py:139
  54.8 0.0 collective-permute-done.early_ref
  54.8 4.1 %collective-permute-done.3.near_ref = bf16[4,128,256]{2,1,0:T(8,128)(2,1)S(1)} collective-permute-done((bf16[4,128,256]{2,1,0:T(8,128)(2,1)S(1)}, bf16[4,128,256]{2,1,0:T(8,128)(2,1)S(1)}, u32[]{:S(2)}, u32[]{:S(2)}) %collective-permute-start.3) | collective-permute-done | bytes 262176 | tf_op jit(solution)/shard_map/ppermute | solution.py:330
  58.9 0.0 collective-permute-done.4.recv_ref
  58.9 0.0 copy-done.2
  58.9 0.0 copy-done.5
  59.0 0.0 copy-start.3
  59.0 2.6 %shard_map.95.refs_2_ = f32[16,128,256]{2,1,0:T(8,128)S(1)} custom-call(s32[2]{0:T(128)S(1)} %pad_add_fusion.meta_ref.refs_0_, s32[2,16]{1,0:T(2,128)S(1)} %bitcast.8, f32[256]{0:T(256)S(1)} %copy-done.5, f32[16,256]{1,0:T(8,128)S(1)} %copy-done.2, bf16[16,256,256]{2,1,0:T(8,128)(2,1)S(1)} %copy-done.1, f32[16,128,256]{2,1,0:T(8,128)S(1)} %shard_map.91.own_ref, ...), custom_call_target="tpu_custom_call" | custom-call | flops 4194304 | bytes 8388608 | tf_op jit(solution)/shard_map/pallas_call | solution.py:255
  61.5 0.0 collective-permute-done.7.refs_3_
  61.6 0.0 copy-done.3
  61.6 1.8 %shard_map.97.refs_4_ = f32[16,128,256]{2,1,0:T(8,128)} custom-call(s32[2]{0:T(128)S(1)} %pad_add_fusion.meta_ref.refs_0_, s32[16]{0:T(128)S(1)} %copy-done.3, f32[16,128,256]{2,1,0:T(8,128)S(1)} %shard_map.95.refs_2_, bf16[12,128,256]{2,1,0:T(8,128)(2,1)S(1)} %collective-permute-done.7.refs_3_), custom_call_target="tpu_custom_call" | custom-call | flops 786432 | bytes 3145728 | tf_op jit(solution)/shard_map/pallas_call | solution.py:291
  63.4 0.0 collective-permute-done.6.refs_3_
  63.4 1.4 %shard_map.98 = f32[16,128,256]{2,1,0:T(8,128)} custom-call(s32[2]{0:T(128)S(1)} %pad_add_fusion.meta_ref.refs_0_, s32[16]{0:T(128)S(1)} %copy-done.3, f32[16,128,256]{2,1,0:T(8,128)S(1)} %shard_map.95.refs_2_, bf16[4,128,256]{2,1,0:T(8,128)(2,1)S(1)} %collective-permute-done.6.refs_3_, ...), custom_call_target="tpu_custom_call", output_to_operand_aliasing={{}: (4, {})} | custom-call | flops 262144 | bytes 1048576 | tf_op jit(solution)/shard_map/pallas_call | solution.py:291
Async XLA Ops:
  0.0 11.0 %copy-start = (f32[2048,4]{0,1:T(4,128)S(1)}, f32[2048,4]{0,1:T(4,128)}, u32[]{:S(2)}) copy-start(f32[2048,4]{0,1:T(4,128)} %param.15) | copy-start | bytes 98308
  0.0 19.2 %collective-permute-start.1 = (bf16[2,1024,256]{2,1,0:T(8,128)(2,1)}, bf16[2,1024,256]{2,1,0:T(8,128)(2,1)S(1)}, u32[]{:S(2)}, u32[]{:S(2)}) collective-permute-start(bf16[2,1024,256]{2,1,0:T(8,128)(2,1)} %blk.1), channel_id=1, source_target_pairs={{1,2},{2,1},{3,4},{4,3},{5,6},{6,5},{7,8},{8,7},{9,10},{10,9},{11,... | collective-permute-start | bytes 3145736 | tf_op jit(solution)/shard_map/ppermute | solution.py:315
  4.2 15.0 %collective-permute-start.2 = (bf16[2,1024,256]{2,1,0:T(8,128)(2,1)}, bf16[2,1024,256]{2,1,0:T(8,128)(2,1)S(1)}, u32[]{:S(2)}, u32[]{:S(2)}) collective-permute-start(bf16[2,1024,256]{2,1,0:T(8,128)(2,1)} %blk.1), channel_id=1, source_target_pairs={{0,1},{1,0},{2,3},{3,2},{4,5},{5,4},{6,7},{7,6},{8,9},{9,8},{10,11... | collective-permute-start | bytes 3145736 | tf_op jit(solution)/shard_map/ppermute | solution.py:325
  11.1 8.2 %copy-start.6 = (bf16[2,1024,256]{2,1,0:T(8,128)(2,1)S(1)}, bf16[2,1024,256]{2,1,0:T(8,128)(2,1)}, u32[]{:S(2)}) copy-start(bf16[2,1024,256]{2,1,0:T(8,128)(2,1)} %blk.1) | copy-start | bytes 3145732
  17.3 7.5 %copy-start.4 = (s32[16,2]{0,1:T(2,128)S(1)}, s32[16,2]{0,1:T(2,128)}, u32[]{:S(2)}) copy-start(s32[16,2]{0,1:T(2,128)} %param.10) | copy-start | bytes 388
  17.3 37.5 %collective-permute-start = (bf16[16,128,256]{2,1,0:T(8,128)(2,1)S(1)}, bf16[16,128,256]{2,1,0:T(8,128)(2,1)S(1)}, u32[]{:S(2)}, u32[]{:S(2)}) collective-permute-start(bf16[16,128,256]{2,1,0:T(8,128)(2,1)S(1)} %get-tuple-element.11), channel_id=1, source_target_pairs={{1,3},{2,0},{3,5},{4,2},{5,7},{6,4},{7,9},{8,6},{9,11},{10,8},{11,... | collective-permute-start | bytes 3145736 | tf_op jit(solution)/shard_map/ppermute | solution.py:324
  21.2 37.7 %collective-permute-start.4 = (f32[8,128,256]{2,1,0:T(8,128)S(1)}, f32[8,128,256]{2,1,0:T(8,128)S(1)}, u32[]{:S(2)}, u32[]{:S(2)}) collective-permute-start(f32[8,128,256]{2,1,0:T(8,128)S(1)} %get-tuple-element.13), channel_id=1, source_target_pairs={{0,1},{1,0},{2,3},{3,2},{4,5},{5,4},{6,7},{7,6},{8,9},{9,8},{10,11... | collective-permute-start | bytes 3145736 | tf_op jit(solution)/shard_map/ppermute | solution.py:338
  24.8 7.9 %collective-permute-start.5 = (s32[2,16]{1,0:T(2,128)S(1)}, s32[2,16]{1,0:T(2,128)S(1)}, u32[]{:S(2)}, u32[]{:S(2)}) collective-permute-start(s32[2,16]{1,0:T(2,128)S(1)} %bitcast.7), channel_id=1, source_target_pairs={{1,2},{2,1},{3,4},{4,3},{5,6},{6,5},{7,8},{8,7},{9,10},{10,9},{11,... | collective-permute-start | bytes 392 | tf_op jit(solution)/shard_map/ppermute | solution.py:316
  34.1 16.1 %copy-start.1 = (bf16[16,256,256]{2,1,0:T(8,128)(2,1)S(1)}, bf16[16,256,256]{2,1,0:T(8,128)(2,1)}, u32[]{:S(2)}) copy-start(bf16[16,256,256]{2,1,0:T(8,128)(2,1)} %amp_ref.1) | copy-start | bytes 6291460
  34.1 27.4 %collective-permute-start.7 = (bf16[12,128,256]{2,1,0:T(8,128)(2,1)S(1)}, bf16[12,128,256]{2,1,0:T(8,128)(2,1)S(1)}, u32[]{:S(2)}, u32[]{:S(2)}) collective-permute-start(bf16[12,128,256]{2,1,0:T(8,128)(2,1)S(1)} %get-tuple-element.16), channel_id=1, source_target_pairs={{1,2},{2,1},{3,4},{4,3},{5,6},{6,5},{7,8},{8,7},{9,10},{10,9},{11,... | collective-permute-start | bytes 2359304 | tf_op jit(solution)/shard_map/ppermute | solution.py:334
  37.9 21.0 %collective-permute-start.3 = (bf16[4,128,256]{2,1,0:T(8,128)(2,1)S(1)}, bf16[4,128,256]{2,1,0:T(8,128)(2,1)S(1)}, u32[]{:S(2)}, u32[]{:S(2)}) collective-permute-start(bf16[4,128,256]{2,1,0:T(8,128)(2,1)S(1)} %shard_map.93), channel_id=1, source_target_pairs={{1,3},{2,0},{3,5},{4,2},{5,7},{6,4},{7,9},{8,6},{9,11},{10,8},{11,... | collective-permute-start | bytes 786440 | tf_op jit(solution)/shard_map/ppermute | solution.py:330
  39.9 19.1 %copy-start.2 = (f32[16,256]{1,0:T(8,128)S(1)}, f32[16,256]{1,0:T(8,128)}, u32[]{:S(2)}) copy-start(f32[16,256]{1,0:T(8,128)} %en_ref.1) | copy-start | bytes 49156
  39.9 19.1 %copy-start.5 = (f32[256]{0:T(256)S(1)}, f32[256]{0:T(256)}, u32[]{:S(2)}) copy-start(f32[256]{0:T(256)} %occ_ref.1) | copy-start | bytes 3076
  39.9 23.5 %collective-permute-start.6 = (bf16[4,128,256]{2,1,0:T(8,128)(2,1)S(1)}, bf16[4,128,256]{2,1,0:T(8,128)(2,1)S(1)}, u32[]{:S(2)}, u32[]{:S(2)}) collective-permute-start(bf16[4,128,256]{2,1,0:T(8,128)(2,1)S(1)} %get-tuple-element.15), channel_id=1, source_target_pairs={{1,2},{2,1},{3,4},{4,3},{5,6},{6,5},{7,8},{8,7},{9,10},{10,9},{11,... | collective-permute-start | bytes 786440 | tf_op jit(solution)/shard_map/ppermute | solution.py:335
  59.0 2.6 %copy-start.3 = (s32[16]{0:T(128)S(1)}, s32[16]{0:T(128)}, u32[]{:S(2)}) copy-start(s32[16]{0:T(128)} %refs_1_.3) | copy-start | bytes 196
